TPU v7x, 32 devices: a whole 2x2x4 slice. The times are simulated.
32 devices in a mesh: grp: 4 (over z), ctx: 8 (over y, x, core).
Axes of the slice: x: 2, y: 2, z: 4, core: 2. Of those that a mesh axis runs over, the one named last changes fastest.
Arguments:
- queries: bfloat16 [12288, 1024], P(('grp', 'ctx')), may hold values from -10 to 10
- keys_cache: bfloat16 [4096, 128, 128], P(('grp', 'ctx')), may hold values from -8 to 8
- values_cache: bfloat16 [4096, 128, 128], P(('grp', 'ctx')), may hold values from -6 to 6
- block_list: int32 [96, 36], P(('grp', 'ctx')), may hold values from 0 to 4095, as said below
- page_table: int32 [4096], replicated, may hold values from 0 to 4095, as said below
Outputs:
- attended: bfloat16 [12288, 1024], P(('grp', 'ctx'))
Inputs may be any that keep to these rules, and one draw needn't show every extreme that they name: `block_list`: each tile's 36 listed blocks are distinct. Page p is row p of keys_cache and values_cache. Through page_table, each tile lists exactly 9 blocks stored on the devices of each index of grp. Over the 3 tiles of one device and one index of grp, at most 7 listed blocks are stored on any one device, and in every draw, for every device and every group, some device of that group stores exactly 7 of them. `page_table`: each page once.
All inputs are finite; a program needn't handle non-finite values.
Results may differ from a plain program's by a relative error of at most 0.0045.
Values may be sent and summed in bfloat16 or wider, within the bound.
No kernel may reach another device: no remote copies, remote signals or barrier semaphores. Data moves between devices by JAX's collectives and lax.ppermute only.
A program may use at most 192 MiB of HBM per device.

v0:
```python
import functools
import math

import jax
import jax.numpy as jnp
from jax import lax
from jax.experimental import pallas as pl
from jax.experimental.pallas import tpu as pltpu
from jax.sharding import PartitionSpec as P

LANES = 128
LOG2E = math.log2(math.e)


def shifted(block, axis, distance):
    devices = range(lax.axis_size(axis))
    route = [((i - distance) % len(devices), i) for i in devices]
    return lax.ppermute(block, axis, route)


def before(first, second):
    return lax.optimization_barrier((first, second))


def plan_body(groups, ctx_count, cap, shift, place, lists, sends, picks):
    group, here = place[0], place[1]
    rows = groups * ctx_count
    lane = lax.broadcasted_iota(jnp.int32, (rows, LANES), 1)
    earlier = (
        lax.broadcasted_iota(jnp.int32, (LANES, LANES), 0)
        < lax.broadcasted_iota(jnp.int32, (LANES, LANES), 1)
    ).astype(jnp.float32).astype(jnp.bfloat16)

    def rank_of(mask):
        ones = jnp.where(mask, 1.0, 0.0).astype(jnp.bfloat16)
        return jnp.dot(ones, earlier, preferred_element_type=jnp.float32).astype(jnp.int32)

    pages = lists[...]
    mine = (pages >> shift) == group * ctx_count + here
    rank = rank_of(mine)
    within = pages & ((1 << shift) - 1)
    found = jnp.full((rows, LANES), -1, jnp.int32)
    for k in range(cap):
        chosen = jnp.max(jnp.where(mine & (rank == k), within, -1), axis=1, keepdims=True)
        found = jnp.where(lane == k, chosen, found)
    sends[...] = found

    owner = lax.broadcasted_iota(jnp.int32, (ctx_count, LANES), 0)
    order = lax.broadcasted_iota(jnp.int32, (LANES, LANES), 0)
    for home in range(groups):
        listed = lists[pl.ds(home * ctx_count + here, 1), :]
        member = (jnp.broadcast_to(listed, (ctx_count, LANES)) >> shift) == group * ctx_count + owner
        slot = jnp.where(member, owner * cap + rank_of(member), 0)
        slot = jnp.sum(slot, axis=0, keepdims=True)
        inside = jnp.broadcast_to((listed >> shift) // ctx_count == group, (8, LANES))
        ordinal = rank_of(inside)[0:1]
        here_row = jnp.broadcast_to(ordinal, (LANES, LANES)) == order
        here_row = here_row & (jnp.broadcast_to(inside[0:1].astype(jnp.int32), (LANES, LANES)) > 0)
        onehot = jnp.where(here_row, 1.0, 0.0).astype(jnp.bfloat16)
        picked = lax.dot_general(
            jnp.broadcast_to(slot, (8, LANES)).astype(jnp.float32).astype(jnp.bfloat16),
            onehot,
            (((1,), (1,)), ((), ())),
            preferred_element_type=jnp.float32,
        )
        picks[home : home + 1, :] = picked[0:1].astype(jnp.int32)


def make_plan(place, lists, groups, ctx_count, cap, pages_here):
    rows = groups * ctx_count
    shift = pages_here.bit_length() - 1
    return pl.pallas_call(
        functools.partial(plan_body, groups, ctx_count, cap, shift),
        out_shape=(
            jax.ShapeDtypeStruct((rows, LANES), jnp.int32),
            jax.ShapeDtypeStruct((groups, LANES), jnp.int32),
        ),
        in_specs=[
            pl.BlockSpec(memory_space=pltpu.SMEM),
            pl.BlockSpec(memory_space=pltpu.VMEM),
        ],
        name="plan",
    )(place, lists)


def collect_body(ctx_count, cap, home, sends, keys, values, out, sem):
    first = home[0] * ctx_count

    def copies(i):
        page = sends[first + i // cap, i % cap]
        return page, (
            pltpu.make_async_copy(keys.at[page], out.at[i, 0], sem),
            pltpu.make_async_copy(values.at[page], out.at[i, 1], sem),
        )

    def begin(i, carry):
        page, pair = copies(i)

        @pl.when(page >= 0)
        def _():
            pair[0].start()
            pair[1].start()

        return carry

    def finish(i, carry):
        page = sends[first + i // cap, i % cap]

        @pl.when(page >= 0)
        def _():
            pltpu.make_async_copy(keys.at[0], out.at[0, 0], sem).wait()
            pltpu.make_async_copy(values.at[0], out.at[0, 1], sem).wait()

        return carry

    lax.fori_loop(0, ctx_count * cap, begin, 0)
    lax.fori_loop(0, ctx_count * cap, finish, 0)


def collect(home, sends, keys, values, ctx_count, cap):
    _, block, hd = keys.shape
    slots = ctx_count * cap
    return pl.pallas_call(
        functools.partial(collect_body, ctx_count, cap),
        out_shape=jax.ShapeDtypeStruct((slots, 2, block, hd), keys.dtype),
        grid_spec=pltpu.PrefetchScalarGridSpec(
            num_scalar_prefetch=2,
            grid=(),
            in_specs=[pl.BlockSpec(memory_space=pl.ANY)] * 2,
            out_specs=pl.BlockSpec(memory_space=pl.ANY),
            scratch_shapes=[pltpu.SemaphoreType.DMA(())],
        ),
        name="collect",
    )(home, sends, keys, values)


def attend_body(per_grp, heads, others, home, picks, q, fetched, *rest):
    if others:
        parts, sizes, out, kbuf, vbuf, sem = rest
    else:
        out, size_out, kbuf, vbuf, sem = rest
    tile = pl.program_id(0)
    tiles = pl.num_programs(0)
    block = q.shape[0]
    hd = q.shape[1] // heads

    def copies(which, slot):
        pairs = []
        for j in range(per_grp):
            page = picks[home[0], which * per_grp + j]
            span = pl.ds(j * block, block)
            pairs.append(pltpu.make_async_copy(fetched.at[page, 0], kbuf.at[slot, span], sem.at[slot]))
            pairs.append(
                pltpu.make_async_copy(fetched.at[page, 1], vbuf.at[slot, span, pl.ds(0, hd)], sem.at[slot])
            )
        return pairs

    slot = lax.rem(tile, 2)

    @pl.when(tile == 0)
    def _():
        vbuf[:, :, hd:] = jnp.ones((2, per_grp * block, hd), vbuf.dtype)
        for copy in copies(0, 0):
            copy.start()

    @pl.when(tile + 1 < tiles)
    def _():
        for copy in copies(tile + 1, 1 - slot):
            copy.start()

    for copy in copies(tile, slot):
        copy.wait()

    factor = hd ** (-0.5) * LOG2E
    diagonal = lax.broadcasted_iota(jnp.int32, (block, block), 0) == lax.broadcasted_iota(
        jnp.int32, (block, block), 1
    )
    pair = 2
    if others:
        size_rows = [sizes[g] for g in range(others)]
        size_cols = [jnp.transpose(rows) for rows in size_rows]
    for first in range(0, heads, pair):
        rows = jnp.concatenate([q[:, (first + i) * hd : (first + i + 1) * hd] for i in range(pair)], axis=0)
        scores = lax.dot_general(
            rows, kbuf[slot], (((1,), (1,)), ((), ())), preferred_element_type=jnp.float32
        )
        top = jnp.max(scores, axis=1, keepdims=True)
        weights = jnp.exp2((scores - top) * factor).astype(jnp.bfloat16)
        summed = jnp.dot(weights, vbuf[slot], preferred_element_type=jnp.float32)
        for i in range(pair):
            span = slice(i * block, (i + 1) * block)
            col = slice((first + i) * hd, (first + i + 1) * hd)
            total = summed[span, hd:]
            mine = summed[span, :hd] / total
            size = top[span] * factor + jnp.log2(total)
            if others:
                theirs = [
                    jnp.broadcast_to(size_cols[g][:, first + i : first + i + 1], (block, hd))
                    for g in range(others)
                ]
                peak = size
                for one in theirs:
                    peak = jnp.maximum(peak, one)
                share = jnp.exp2(size - peak)
                whole = share
                merged = mine * share
                for g in range(others):
                    share = jnp.exp2(theirs[g] - peak)
                    whole = whole + share
                    merged = merged + parts[g, :, col].astype(jnp.float32) * share
                out[:, col] = (merged / whole).astype(out.dtype)
            else:
                out[:, col] = mine.astype(out.dtype)
                size_out[0, first + i : first + i + 1, :] = jnp.sum(
                    jnp.where(diagonal, size, 0.0), axis=0, keepdims=True
                )


def attend(home, picks, q, fetched, per_grp, heads, parts=None, sizes=None):
    tokens, width = q.shape
    block, hd = fetched.shape[2:]
    tiles = tokens // block
    others = 0 if parts is None else parts.shape[0]
    q_spec = pl.BlockSpec((block, width), lambda t, *_: (t, 0))
    size_shape = (heads, block)
    in_specs = [q_spec, pl.BlockSpec(memory_space=pl.ANY)]
    operands = [q, fetched]
    out_shape = [jax.ShapeDtypeStruct((tokens, width), q.dtype)]
    out_specs = [q_spec]
    if others:
        in_specs += [
            pl.BlockSpec((others, block, width), lambda t, *_: (0, t, 0)),
            pl.BlockSpec((others, None) + size_shape, lambda t, *_: (0, t, 0, 0)),
        ]
        operands += [parts, sizes]
    else:
        out_shape.append(jax.ShapeDtypeStruct((tiles,) + size_shape, jnp.float32))
        out_specs.append(pl.BlockSpec((1,) + size_shape, lambda t, *_: (t, 0, 0)))
    return pl.pallas_call(
        functools.partial(attend_body, per_grp, heads, others),
        out_shape=tuple(out_shape),
        grid_spec=pltpu.PrefetchScalarGridSpec(
            num_scalar_prefetch=2,
            grid=(tiles,),
            in_specs=in_specs,
            out_specs=tuple(out_specs),
            scratch_shapes=[
                pltpu.VMEM((2, per_grp * block, hd), q.dtype),
                pltpu.VMEM((2, per_grp * block, 2 * hd), q.dtype),
                pltpu.SemaphoreType.DMA((2,)),
            ],
        ),
        compiler_params=pltpu.CompilerParams(vmem_limit_bytes=48 * 1024 * 1024),
        name="attend_last" if others else "attend",
    )(home, picks, *operands)


def on_device(queries, keys_cache, values_cache, block_list, page_table):
    groups = lax.axis_size("grp")
    ctx_count = lax.axis_size("ctx")
    tile_count, listed = block_list.shape
    pages_here, block, hd = keys_cache.shape
    heads = queries.shape[1] // hd
    per_grp = listed // groups
    cap = max(3, (2 * tile_count * per_grp + ctx_count - 1) // ctx_count)
    group_here = lax.axis_index("grp")
    ctx_here = lax.axis_index("ctx")
    place = jnp.stack([group_here, ctx_here]).astype(jnp.int32)

    page_ids = page_table[block_list].reshape(1, tile_count * listed)
    page_ids = jnp.pad(page_ids, ((0, 0), (0, LANES - tile_count * listed)), constant_values=-1)
    everywhere = jnp.broadcast_to(page_ids, (groups * ctx_count, LANES))
    lists = lax.all_to_all(everywhere, ("grp", "ctx"), split_axis=0, concat_axis=0, tiled=True)
    sends, picks = make_plan(place, lists, groups, ctx_count, cap, pages_here)

    shifts = [s for s in (2, 1, 3) if s < groups] + [s for s in range(4, groups)]
    sends, queries_out = before(sends, queries)
    homes = {s: ((group_here - s) % groups).astype(jnp.int32).reshape(1) for s in shifts + [0]}
    visiting = {s: shifted(queries_out, "grp", s) for s in shifts}
    visiting[0] = queries

    def fetch(s):
        gathered = collect(homes[s], sends, keys_cache, values_cache, ctx_count, cap)
        return lax.all_to_all(gathered, "ctx", split_axis=0, concat_axis=0, tiled=True)

    parts, sizes = [], []
    for s in shifts:
        part, size = attend(homes[s], picks, visiting[s], fetch(s), per_grp, heads)
        parts.append(shifted(part, "grp", -s))
        sizes.append(shifted(size, "grp", -s))
    return attend(
        homes[0], picks, queries, fetch(0), per_grp, heads, jnp.stack(parts), jnp.stack(sizes)
    )[0]


def solution(mesh):
    in_specs = (
        P(("grp", "ctx"), None),
        P(("grp", "ctx"), None, None),
        P(("grp", "ctx"), None, None),
        P(("grp", "ctx"), None),
        P(),
    )
    out_specs = P(("grp", "ctx"), None)
    return jax.shard_map(
        on_device, mesh=mesh, in_specs=in_specs, out_specs=out_specs, check_vma=False
    )
```

profile of v0, /device:TPU:0, one launch (start us, length us, event | category | flops | bytes accessed | tf_op | source)
XLA Modules:
  0.0 652.9 jit_solution(13850775874379728364)
XLA Ops:
  0.0 0.0 copy-start
  0.0 0.7 compare_select_fusion
  0.7 0.1 reshape.28
  0.8 0.0 copy-done
  0.8 1.1 gather_fusion
  2.0 0.6 broadcast_in_dim.9
  2.6 7.3 %all-to-all-start = ((s32[32,1,128]{2,1,0:T(1,128)}), s32[32,1,128]{2,1,0:T(1,128)S(1)}, u32[]{:S(2)}, u32[]{:S(2)}) async-start(s32[32,1,128]{2,1,0:T(1,128)} %broadcast_in_dim.9), calls=%async_computation | async-start | bytes 32768 | tf_op jit(solution)/shard_map/all_to_all | solution.py:273
  9.9 0.7 pad_add_fusion.place
  10.6 6.4 all-to-all-done
  17.0 0.6 copy-done.3
  17.6 1.7 plan.1
  19.3 47.7 %collect.7 = bf16[56,2,128,128]{3,2,1,0:T(8,128)(2,1)} custom-call(s32[1]{0:T(128)} %bitcast.10.home, s32[32,128]{1,0:T(8,128)} %get-tuple-element.17.sends, bf16[128,128,128]{2,1,0:T(8,128)(2,1)} %keys.7, bf16[128,128,128]{2,1,0:T(8,128)(2,1)} %values.7), custom_call_target="tpu_custom_call" | custom-call | tf_op jit(solution)/shard_map/collect/pallas_call | solution.py:123
  67.1 66.8 %all-to-all-start.4 = ((bf16[56,2,128,128]{3,2,1,0:T(8,128)(2,1)}), bf16[56,2,128,128]{3,2,1,0:T(8,128)(2,1)}, u32[]{:S(2)}, u32[]{:S(2)}) async-start(bf16[56,2,128,128]{3,2,1,0:T(8,128)(2,1)} %collect.7), calls=%async_computation.4 | async-start | bytes 7340032 | tf_op jit(solution)/shard_map/all_to_all | solution.py:284
  133.8 39.9 %collect.5 = bf16[56,2,128,128]{3,2,1,0:T(8,128)(2,1)} custom-call(s32[1]{0:T(128)} %bitcast.6.home, s32[32,128]{1,0:T(8,128)} %get-tuple-element.17.sends, bf16[128,128,128]{2,1,0:T(8,128)(2,1)} %keys.7, bf16[128,128,128]{2,1,0:T(8,128)(2,1)} %values.7), custom_call_target="tpu_custom_call" | custom-call | tf_op jit(solution)/shard_map/collect/pallas_call | solution.py:123
  173.7 3.7 all-to-all-done.4.fetched
  177.4 74.2 %all-to-all-start.2 = ((bf16[56,2,128,128]{3,2,1,0:T(8,128)(2,1)}), bf16[56,2,128,128]{3,2,1,0:T(8,128)(2,1)}, u32[]{:S(2)}, u32[]{:S(2)}) async-start(bf16[56,2,128,128]{3,2,1,0:T(8,128)(2,1)} %collect.5), calls=%async_computation.2 | async-start | bytes 7340032 | tf_op jit(solution)/shard_map/all_to_all | solution.py:284
  251.6 41.8 %collect.6 = bf16[56,2,128,128]{3,2,1,0:T(8,128)(2,1)} custom-call(s32[1]{0:T(128)} %bitcast.8.home, s32[32,128]{1,0:T(8,128)} %get-tuple-element.17.sends, bf16[128,128,128]{2,1,0:T(8,128)(2,1)} %keys.7, bf16[128,128,128]{2,1,0:T(8,128)(2,1)} %values.7), custom_call_target="tpu_custom_call" | custom-call | tf_op jit(solution)/shard_map/collect/pallas_call | solution.py:123
  293.3 1.8 all-to-all-done.2.fetched
  295.1 74.2 %all-to-all-start.3 = ((bf16[56,2,128,128]{3,2,1,0:T(8,128)(2,1)}), bf16[56,2,128,128]{3,2,1,0:T(8,128)(2,1)}, u32[]{:S(2)}, u32[]{:S(2)}) async-start(bf16[56,2,128,128]{3,2,1,0:T(8,128)(2,1)} %collect.6), calls=%async_computation.3 | async-start | bytes 7340032 | tf_op jit(solution)/shard_map/all_to_all | solution.py:284
  369.3 35.8 %collect.4 = bf16[56,2,128,128]{3,2,1,0:T(8,128)(2,1)} custom-call(s32[1]{0:T(128)} %bitcast.home, s32[32,128]{1,0:T(8,128)} %get-tuple-element.17.sends, bf16[128,128,128]{2,1,0:T(8,128)(2,1)} %keys.7, bf16[128,128,128]{2,1,0:T(8,128)(2,1)} %values.7), custom_call_target="tpu_custom_call" | custom-call | tf_op jit(solution)/shard_map/collect/pallas_call | solution.py:123
  405.1 0.0 copy-start.1
  405.1 7.7 %all-to-all-done.3.fetched = bf16[56,2,128,128]{3,2,1,0:T(8,128)(2,1)} async-done(((bf16[56,2,128,128]{3,2,1,0:T(8,128)(2,1)}), bf16[56,2,128,128]{3,2,1,0:T(8,128)(2,1)}, u32[]{:S(2)}, u32[]{:S(2)}) %all-to-all-start.3) | async-done | bytes 3670048 | tf_op jit(solution)/shard_map/all_to_all | solution.py:284
  412.9 74.3 %all-to-all-start.1 = ((bf16[56,2,128,128]{3,2,1,0:T(8,128)(2,1)}), bf16[56,2,128,128]{3,2,1,0:T(8,128)(2,1)}, u32[]{:S(2)}, u32[]{:S(2)}) async-start(bf16[56,2,128,128]{3,2,1,0:T(8,128)(2,1)} %collect.4), calls=%async_computation.1 | async-start | bytes 7340032 | tf_op jit(solution)/shard_map/all_to_all | solution.py:284
  487.2 0.0 copy-done.1
  487.2 0.7 collective-permute-start.4
  487.9 1.5 collective-permute-start
  489.3 1.2 collective-permute-start.2
  490.5 17.0 %collective-permute-done.4.q = bf16[384,1024]{1,0:T(8,128)(2,1)S(1)} collective-permute-done((bf16[384,1024]{1,0:T(8,128)(2,1)S(1)}, bf16[384,1024]{1,0:T(8,128)(2,1)S(1)}, u32[]{:S(2)}, u32[]{:S(2)}) %collective-permute-start.4) | collective-permute-done | bytes 786464 | tf_op jit(solution)/shard_map/ppermute | solution.py:18
  507.5 8.2 %attend.5 = (bf16[384,1024]{1,0:T(8,128)(2,1)S(1)}, f32[3,8,128]{2,1,0:T(8,128)S(1)}) custom-call(s32[1]{0:T(128)} %bitcast.10.home, s32[4,128]{1,0:T(4,128)S(1)} %copy-done.2, bf16[384,1024]{1,0:T(8,128)(2,1)S(1)} %collective-permute-done.4.q, bf16[56,2,128,128]{3,2,1,0:T(8,128)(2,1)} %all-to-all-done.4.fetched), custom_call_target="tpu_custom_call" | custom-call | tf_op jit(solution)/shard_map/attend/pallas_call | solution.py:239
  515.7 1.3 collective-permute-start.5
  516.9 74.5 %collective-permute-done.q = bf16[384,1024]{1,0:T(8,128)(2,1)S(1)} collective-permute-done((bf16[384,1024]{1,0:T(8,128)(2,1)S(1)}, bf16[384,1024]{1,0:T(8,128)(2,1)S(1)}, u32[]{:S(2)}, u32[]{:S(2)}) %collective-permute-start) | collective-permute-done | bytes 786464 | tf_op jit(solution)/shard_map/ppermute | solution.py:18
  591.5 8.2 %attend.3 = (bf16[384,1024]{1,0:T(8,128)(2,1)S(1)}, f32[3,8,128]{2,1,0:T(8,128)S(1)}) custom-call(s32[1]{0:T(128)} %bitcast.6.home, s32[4,128]{1,0:T(4,128)S(1)} %copy-done.2, bf16[384,1024]{1,0:T(8,128)(2,1)S(1)} %collective-permute-done.q, bf16[56,2,128,128]{3,2,1,0:T(8,128)(2,1)} %all-to-all-done.2.fetched), custom_call_target="tpu_custom_call" | custom-call | tf_op jit(solution)/shard_map/attend/pallas_call | solution.py:239
  599.6 0.1 collective-permute-start.1
  599.7 0.0 collective-permute-done.2.q
  599.7 8.2 %attend.4 = (bf16[384,1024]{1,0:T(8,128)(2,1)S(1)}, f32[3,8,128]{2,1,0:T(8,128)S(1)}) custom-call(s32[1]{0:T(128)} %bitcast.8.home, s32[4,128]{1,0:T(4,128)S(1)} %copy-done.2, bf16[384,1024]{1,0:T(8,128)(2,1)S(1)} %collective-permute-done.2.q, bf16[56,2,128,128]{3,2,1,0:T(8,128)(2,1)} %all-to-all-done.3.fetched), custom_call_target="tpu_custom_call" | custom-call | tf_op jit(solution)/shard_map/attend/pallas_call | solution.py:239
  607.9 0.1 collective-permute-start.3
  608.0 3.0 collective-permute-start.6
  611.0 1.4 collective-permute-start.7
  612.4 24.8 %collective-permute-done.6 = f32[3,8,128]{2,1,0:T(8,128)S(1)} collective-permute-done((f32[3,8,128]{2,1,0:T(8,128)S(1)}, f32[3,8,128]{2,1,0:T(8,128)S(1)}, u32[]{:S(2)}, u32[]{:S(2)}) %collective-permute-start.6) | collective-permute-done | bytes 12320 | tf_op jit(solution)/shard_map/ppermute | solution.py:18
  637.2 0.0 collective-permute-start.8
  637.2 0.0 collective-permute-done.7
  637.2 5.5 collective-permute-done.8
  642.7 0.0 collective-permute-done.5
  642.7 0.0 collective-permute-done.1
  642.7 0.0 collective-permute-done.3
  642.7 0.3 pad_maximum_fusion.rest_0_
  643.0 0.0 all-to-all-done.1.fetched
  643.0 9.9 %attend_last.1 = bf16[384,1024]{1,0:T(8,128)(2,1)} custom-call(s32[1]{0:T(128)} %bitcast.home, s32[4,128]{1,0:T(4,128)S(1)} %copy-done.2, bf16[384,1024]{1,0:T(8,128)(2,1)S(1)} %copy-done.1, bf16[56,2,128,128]{3,2,1,0:T(8,128)(2,1)} %all-to-all-done.1.fetched, bf16[3,384,1024]{2,1,0:T(8,128)(2,1)S(1)} %pad_maximum_fusion.rest_0_, ...), custom_call_target="tpu_custom_call" | custom-call | tf_op jit(solution)/shard_map/attend_last/pallas_call | solution.py:239
  (6 shorter events, 0.0 us)
Async XLA Ops:
  0.0 0.8 copy-start
  2.6 14.4 %all-to-all-start = ((s32[32,1,128]{2,1,0:T(1,128)}), s32[32,1,128]{2,1,0:T(1,128)S(1)}, u32[]{:S(2)}, u32[]{:S(2)}) async-start(s32[32,1,128]{2,1,0:T(1,128)} %broadcast_in_dim.9), calls=%async_computation | async-start | bytes 32768 | tf_op jit(solution)/shard_map/all_to_all | solution.py:273
  17.0 0.6 copy-start.3
  67.1 110.4 %all-to-all-start.4 = ((bf16[56,2,128,128]{3,2,1,0:T(8,128)(2,1)}), bf16[56,2,128,128]{3,2,1,0:T(8,128)(2,1)}, u32[]{:S(2)}, u32[]{:S(2)}) async-start(bf16[56,2,128,128]{3,2,1,0:T(8,128)(2,1)} %collect.7), calls=%async_computation.4 | async-start | bytes 7340032 | tf_op jit(solution)/shard_map/all_to_all | solution.py:284
  177.4 117.7 %all-to-all-start.2 = ((bf16[56,2,128,128]{3,2,1,0:T(8,128)(2,1)}), bf16[56,2,128,128]{3,2,1,0:T(8,128)(2,1)}, u32[]{:S(2)}, u32[]{:S(2)}) async-start(bf16[56,2,128,128]{3,2,1,0:T(8,128)(2,1)} %collect.5), calls=%async_computation.2 | async-start | bytes 7340032 | tf_op jit(solution)/shard_map/all_to_all | solution.py:284
  295.1 117.7 %all-to-all-start.3 = ((bf16[56,2,128,128]{3,2,1,0:T(8,128)(2,1)}), bf16[56,2,128,128]{3,2,1,0:T(8,128)(2,1)}, u32[]{:S(2)}, u32[]{:S(2)}) async-start(bf16[56,2,128,128]{3,2,1,0:T(8,128)(2,1)} %collect.6), calls=%async_computation.3 | async-start | bytes 7340032 | tf_op jit(solution)/shard_map/all_to_all | solution.py:284
  405.1 82.1 %copy-start.1 = (bf16[384,1024]{1,0:T(8,128)(2,1)S(1)}, bf16[384,1024]{1,0:T(8,128)(2,1)}, u32[]{:S(2)}) copy-start(bf16[384,1024]{1,0:T(8,128)(2,1)} %q.1) | copy-start | bytes 2359300
  405.1 102.4 %copy-start.2 = (s32[4,128]{1,0:T(4,128)S(1)}, s32[4,128]{1,0:T(4,128)}, u32[]{:S(2)}) copy-start(s32[4,128]{1,0:T(4,128)} %get-tuple-element.15.picks) | copy-start | bytes 6148
  412.9 230.1 %all-to-all-start.1 = ((bf16[56,2,128,128]{3,2,1,0:T(8,128)(2,1)}), bf16[56,2,128,128]{3,2,1,0:T(8,128)(2,1)}, u32[]{:S(2)}, u32[]{:S(2)}) async-start(bf16[56,2,128,128]{3,2,1,0:T(8,128)(2,1)} %collect.4), calls=%async_computation.1 | async-start | bytes 7340032 | tf_op jit(solution)/shard_map/all_to_all | solution.py:284
  487.2 20.3 %collective-permute-start.4 = (bf16[384,1024]{1,0:T(8,128)(2,1)S(1)}, bf16[384,1024]{1,0:T(8,128)(2,1)S(1)}, u32[]{:S(2)}, u32[]{:S(2)}) collective-permute-start(bf16[384,1024]{1,0:T(8,128)(2,1)S(1)} %copy-done.1), channel_id=1, source_target_pairs={{8,0},{16,8},{24,16},{0,24},{9,1},{17,9},{25,17},{1,25},{10,2},{18... | collective-permute-start | bytes 2359304 | tf_op jit(solution)/shard_map/ppermute | solution.py:18
  487.9 103.6 %collective-permute-start = (bf16[384,1024]{1,0:T(8,128)(2,1)S(1)}, bf16[384,1024]{1,0:T(8,128)(2,1)S(1)}, u32[]{:S(2)}, u32[]{:S(2)}) collective-permute-start(bf16[384,1024]{1,0:T(8,128)(2,1)S(1)} %copy-done.1), channel_id=1, source_target_pairs={{16,0},{24,8},{0,16},{8,24},{17,1},{25,9},{1,17},{9,25},{18,2},{26... | collective-permute-start | bytes 2359304 | tf_op jit(solution)/shard_map/ppermute | solution.py:18
  489.3 110.4 %collective-permute-start.2 = (bf16[384,1024]{1,0:T(8,128)(2,1)S(1)}, bf16[384,1024]{1,0:T(8,128)(2,1)S(1)}, u32[]{:S(2)}, u32[]{:S(2)}) collective-permute-start(bf16[384,1024]{1,0:T(8,128)(2,1)S(1)} %copy-done.1), channel_id=1, source_target_pairs={{24,0},{0,8},{8,16},{16,24},{25,1},{1,9},{9,17},{17,25},{26,2},{2,... | collective-permute-start | bytes 2359304 | tf_op jit(solution)/shard_map/ppermute | solution.py:18
  515.7 127.0 %collective-permute-start.5 = (bf16[384,1024]{1,0:T(8,128)(2,1)S(1)}, bf16[384,1024]{1,0:T(8,128)(2,1)S(1)}, u32[]{:S(2)}, u32[]{:S(2)}) collective-permute-start(bf16[384,1024]{1,0:T(8,128)(2,1)S(1)} %get-tuple-element.21), channel_id=1, source_target_pairs={{24,0},{0,8},{8,16},{16,24},{25,1},{1,9},{9,17},{17,25},{26,2},{2,... | collective-permute-start | bytes 2359304 | tf_op jit(solution)/shard_map/ppermute | solution.py:18
  599.6 43.1 %collective-permute-start.1 = (bf16[384,1024]{1,0:T(8,128)(2,1)S(1)}, bf16[384,1024]{1,0:T(8,128)(2,1)S(1)}, u32[]{:S(2)}, u32[]{:S(2)}) collective-permute-start(bf16[384,1024]{1,0:T(8,128)(2,1)S(1)} %get-tuple-element.19), channel_id=1, source_target_pairs={{16,0},{24,8},{0,16},{8,24},{17,1},{25,9},{1,17},{9,25},{18,2},{26... | collective-permute-start | bytes 2359304 | tf_op jit(solution)/shard_map/ppermute | solution.py:18
  607.9 34.8 %collective-permute-start.3 = (bf16[384,1024]{1,0:T(8,128)(2,1)S(1)}, bf16[384,1024]{1,0:T(8,128)(2,1)S(1)}, u32[]{:S(2)}, u32[]{:S(2)}) collective-permute-start(bf16[384,1024]{1,0:T(8,128)(2,1)S(1)} %get-tuple-element.20), channel_id=1, source_target_pairs={{8,0},{16,8},{24,16},{0,24},{9,1},{17,9},{25,17},{1,25},{10,2},{18... | collective-permute-start | bytes 2359304 | tf_op jit(solution)/shard_map/ppermute | solution.py:18
  608.0 29.2 %collective-permute-start.6 = (f32[3,8,128]{2,1,0:T(8,128)S(1)}, f32[3,8,128]{2,1,0:T(8,128)S(1)}, u32[]{:S(2)}, u32[]{:S(2)}) collective-permute-start(f32[3,8,128]{2,1,0:T(8,128)S(1)} %get-tuple-element.22), channel_id=1, source_target_pairs={{16,0},{24,8},{0,16},{8,24},{17,1},{25,9},{1,17},{9,25},{18,2},{26... | collective-permute-start | bytes 36872 | tf_op jit(solution)/shard_map/ppermute | solution.py:18
  611.0 26.3 %collective-permute-start.7 = (f32[3,8,128]{2,1,0:T(8,128)S(1)}, f32[3,8,128]{2,1,0:T(8,128)S(1)}, u32[]{:S(2)}, u32[]{:S(2)}) collective-permute-start(f32[3,8,128]{2,1,0:T(8,128)S(1)} %get-tuple-element.23), channel_id=1, source_target_pairs={{8,0},{16,8},{24,16},{0,24},{9,1},{17,9},{25,17},{1,25},{10,2},{18... | collective-permute-start | bytes 36872 | tf_op jit(solution)/shard_map/ppermute | solution.py:18
  637.2 5.5 collective-permute-start.8
where the time goes:
time: 651 us; the launch traced here: 653 us
  starting transfers between devices  306 us (47%)
  Pallas kernels  201 us (31%)
  waiting for transfers between devices  142 us (22%)
    all_to_all x4, starting transfers between devices, fetch(): lax.all_to_all(gathered, 'ctx', split_axis=0, concat_axis=0, tiled=True)  289 us
    pallas_call x4, Pallas kernels, collect(): pl.pallas_call(functools.partial(collect_body, ctx_count, cap), out_shape...  165 us
    ppermute x9, waiting for transfers between devices, shifted(): return lax.ppermute(block, axis, route)  122 us
    pallas_call x4, Pallas kernels, attend(): pl.pallas_call(functools.partial(attend_body, per_grp, heads, others), ou...  34.4 us
    all_to_all x4, waiting for transfers between devices, fetch(): lax.all_to_all(gathered, 'ctx', split_axis=0, concat_axis=0, tiled=True)  13.2 us
  transfers between devices with their start and end apart: 14, of which 8 were waited for; matrix products, arithmetic and copies ran while one was open for 0% of the time, Pallas kernels for 22%

commit v1 on v0

v1 whole, which is shorter than its diff:
```python
import functools
import math

import jax
import jax.numpy as jnp
from jax import lax
from jax.experimental import pallas as pl
from jax.experimental.pallas import tpu as pltpu
from jax.sharding import PartitionSpec as P


LANES = 128
LOG2E = math.log2(math.e)


def shifted(block, axis, distance):
    devices = range(lax.axis_size(axis))
    route = [((i - distance) % len(devices), i) for i in devices]
    return lax.ppermute(block, axis, route)


def plan_body(groups, ctx_count, cap, shift, place, lists, sends, places):
    group, here = place[0], place[1]
    rows = groups * ctx_count
    lane = lax.broadcasted_iota(jnp.int32, (rows, LANES), 1)
    earlier = (
        lax.broadcasted_iota(jnp.int32, (LANES, LANES), 0)
        < lax.broadcasted_iota(jnp.int32, (LANES, LANES), 1)
    ).astype(jnp.float32).astype(jnp.bfloat16)

    def rank_of(mask):
        ones = jnp.where(mask, 1.0, 0.0).astype(jnp.bfloat16)
        return jnp.dot(ones, earlier, preferred_element_type=jnp.float32).astype(jnp.int32)

    pages = lists[...]
    mine = (pages >> shift) == group * ctx_count + here
    rank = rank_of(mine)
    within = pages & ((1 << shift) - 1)
    found = jnp.full((rows, LANES), -1, jnp.int32)
    for k in range(cap):
        chosen = jnp.max(jnp.where(mine & (rank == k), within, -1), axis=1, keepdims=True)
        found = jnp.where(lane == k, chosen, found)
    sends[...] = found

    offset = lax.broadcasted_iota(jnp.int32, (ctx_count, LANES), 0)
    owner = here - offset
    owner = jnp.where(owner < 0, owner + ctx_count, owner)
    order = lax.broadcasted_iota(jnp.int32, (LANES, LANES), 0)
    for home in range(groups):
        listed = jnp.broadcast_to(lists[pl.ds(home * ctx_count + here, 1), :], (ctx_count, LANES))
        member = (listed >> shift) == group * ctx_count + owner
        slot = jnp.where(member, offset * cap + rank_of(member) + 1, 0)
        slot = jnp.broadcast_to(jnp.sum(slot, axis=0, keepdims=True) - 1, (LANES, LANES))
        inside = jnp.broadcast_to(slot[0:1] >= 0, (8, LANES))
        ordinal = (rank_of(inside) + 1).astype(jnp.float32).astype(jnp.bfloat16)
        onehot = jnp.where(slot == order, 1.0, 0.0).astype(jnp.bfloat16)
        position = lax.dot_general(
            ordinal, onehot, (((1,), (1,)), ((), ())), preferred_element_type=jnp.float32
        )
        places[home : home + 1, :] = position[0:1].astype(jnp.int32) - 1


def make_plan(place, lists, groups, ctx_count, cap, pages_here):
    rows = groups * ctx_count
    shift = pages_here.bit_length() - 1
    return pl.pallas_call(
        functools.partial(plan_body, groups, ctx_count, cap, shift),
        out_shape=(
            jax.ShapeDtypeStruct((rows, LANES), jnp.int32),
            jax.ShapeDtypeStruct((groups, LANES), jnp.int32),
        ),
        in_specs=[
            pl.BlockSpec(memory_space=pltpu.SMEM),
            pl.BlockSpec(memory_space=pltpu.VMEM),
        ],
        name="plan",
    )(place, lists)


def collect_body(ctx_count, cap, home, sends, keys, values, *rest):
    outs, sem = rest[:-1], rest[-1]
    here = home[1]

    def each(k, act):
        row = home[0] * ctx_count + lax.rem(here + k, ctx_count)

        def step(j, carry):
            page = sends[row, j]

            @pl.when(page >= 0)
            def _():
                act(pltpu.make_async_copy(keys.at[page], outs[k - 1].at[j, 0], sem))
                act(pltpu.make_async_copy(values.at[page], outs[k - 1].at[j, 1], sem))

            return carry

        lax.fori_loop(0, cap, step, 0)

    for k in range(1, ctx_count):
        each(k, lambda copy: copy.start())
    for k in range(1, ctx_count):
        each(k, lambda copy: copy.wait())


def collect(home, sends, keys, values, ctx_count, cap):
    _, block, hd = keys.shape
    peers = ctx_count - 1
    return pl.pallas_call(
        functools.partial(collect_body, ctx_count, cap),
        out_shape=(jax.ShapeDtypeStruct((cap, 2, block, hd), keys.dtype),) * peers,
        grid_spec=pltpu.PrefetchScalarGridSpec(
            num_scalar_prefetch=2,
            grid=(),
            in_specs=[pl.BlockSpec(memory_space=pl.ANY)] * 2,
            out_specs=(pl.BlockSpec(memory_space=pltpu.VMEM),) * peers,
            scratch_shapes=[pltpu.SemaphoreType.DMA(())],
        ),
        name="collect",
    )(home, sends, keys, values)


def attend_body(per_grp, heads, others, ctx_count, cap, home, places, sends, q, keys, values, *rest):
    arrived, rest = rest[: ctx_count - 1], rest[ctx_count - 1 :]
    if others:
        parts, sizes, out, kbuf, vbuf, sem = rest
    else:
        out, size_out, kbuf, vbuf, sem = rest
    tile = pl.program_id(0)
    block = q.shape[0]
    hd = q.shape[1] // heads
    span_keys = per_grp * block

    @pl.when(tile == 0)
    def _():
        own_row = home[0] * ctx_count + home[1]

        def load(k, j):
            position = places[home[0], k * cap + j]

            @pl.when(position >= 0)
            def _():
                which = position // per_grp
                span = pl.ds(pl.multiple_of(position * block, block), block)
                if k == 0:
                    page = sends[own_row, j]
                    key, value = keys.at[page], values.at[page]
                else:
                    key, value = arrived[k - 1].at[j, 0], arrived[k - 1].at[j, 1]
                pltpu.make_async_copy(key, kbuf.at[span], sem.at[which]).start()
                pltpu.make_async_copy(value, vbuf.at[span, pl.ds(0, hd)], sem.at[which]).start()

        for k in range(ctx_count):
            lax.fori_loop(0, cap, lambda j, carry, k=k: (load(k, j), carry)[1], 0)
        vbuf[:, hd:] = jnp.ones((vbuf.shape[0], hd), vbuf.dtype)

    here = pl.ds(pl.multiple_of(tile * span_keys, block), span_keys)
    for _ in range(per_grp):
        pltpu.make_async_copy(keys.at[0], kbuf.at[pl.ds(0, block)], sem.at[tile]).wait()
        pltpu.make_async_copy(values.at[0], vbuf.at[pl.ds(0, block), pl.ds(0, hd)], sem.at[tile]).wait()

    factor = hd ** (-0.5) * LOG2E
    diagonal = lax.broadcasted_iota(jnp.int32, (block, block), 0) == lax.broadcasted_iota(
        jnp.int32, (block, block), 1
    )
    pair = 2
    if others:
        size_rows = [sizes[g] for g in range(others)]
        size_cols = [jnp.transpose(rows) for rows in size_rows]
    for first in range(0, heads, pair):
        rows = jnp.concatenate([q[:, (first + i) * hd : (first + i + 1) * hd] for i in range(pair)], axis=0)
        scores = lax.dot_general(
            rows, kbuf[here, :], (((1,), (1,)), ((), ())), preferred_element_type=jnp.float32
        )
        top = jnp.max(scores, axis=1, keepdims=True)
        weights = jnp.exp2((scores - top) * factor).astype(jnp.bfloat16)
        summed = jnp.dot(weights, vbuf[here, :], preferred_element_type=jnp.float32)
        for i in range(pair):
            span = slice(i * block, (i + 1) * block)
            col = slice((first + i) * hd, (first + i + 1) * hd)
            total = summed[span, hd:]
            mine = summed[span, :hd] / total
            size = top[span] * factor + jnp.log2(total)
            if others:
                theirs = [
                    jnp.broadcast_to(size_cols[g][:, first + i : first + i + 1], (block, hd))
                    for g in range(others)
                ]
                peak = size
                for one in theirs:
                    peak = jnp.maximum(peak, one)
                share = jnp.exp2(size - peak)
                whole = share
                merged = mine * share
                for g in range(others):
                    share = jnp.exp2(theirs[g] - peak)
                    whole = whole + share
                    merged = merged + parts[g, :, col].astype(jnp.float32) * share
                out[:, col] = (merged / whole).astype(out.dtype)
            else:
                out[:, col] = mine.astype(out.dtype)
                size_out[0, first + i : first + i + 1, :] = jnp.sum(
                    jnp.where(diagonal, size, 0.0), axis=0, keepdims=True
                )


def attend(home, places, sends, q, keys, values, arrived, per_grp, cap, heads, parts=None, sizes=None):
    tokens, width = q.shape
    block, hd = keys.shape[1:]
    tiles = tokens // block
    ctx_count = len(arrived) + 1
    others = 0 if parts is None else parts.shape[0]
    q_spec = pl.BlockSpec((block, width), lambda t, *_: (t, 0))
    size_shape = (heads, block)
    in_specs = [q_spec] + [pl.BlockSpec(memory_space=pl.ANY)] * (ctx_count + 1)
    operands = [q, keys, values, *arrived]
    out_shape = [jax.ShapeDtypeStruct((tokens, width), q.dtype)]
    out_specs = [q_spec]
    if others:
        in_specs += [
            pl.BlockSpec((others, block, width), lambda t, *_: (0, t, 0)),
            pl.BlockSpec((others, None) + size_shape, lambda t, *_: (0, t, 0, 0)),
        ]
        operands += [parts, sizes]
    else:
        out_shape.append(jax.ShapeDtypeStruct((tiles,) + size_shape, jnp.float32))
        out_specs.append(pl.BlockSpec((1,) + size_shape, lambda t, *_: (t, 0, 0)))
    return pl.pallas_call(
        functools.partial(attend_body, per_grp, heads, others, ctx_count, cap),
        out_shape=tuple(out_shape),
        grid_spec=pltpu.PrefetchScalarGridSpec(
            num_scalar_prefetch=3,
            grid=(tiles,),
            in_specs=in_specs,
            out_specs=tuple(out_specs),
            scratch_shapes=[
                pltpu.VMEM((tiles * per_grp * block, hd), q.dtype),
                pltpu.VMEM((tiles * per_grp * block, 2 * hd), q.dtype),
                pltpu.SemaphoreType.DMA((tiles,)),
            ],
        ),
        compiler_params=pltpu.CompilerParams(vmem_limit_bytes=48 * 1024 * 1024),
        name="attend_last" if others else "attend",
    )(home, places, sends, *operands)


def on_device(queries, keys_cache, values_cache, block_list, page_table):
    groups = lax.axis_size("grp")
    ctx_count = lax.axis_size("ctx")
    tile_count, listed = block_list.shape
    pages_here, _, hd = keys_cache.shape
    heads = queries.shape[1] // hd
    per_grp = listed // groups
    cap = max(3, (2 * tile_count * per_grp + ctx_count - 1) // ctx_count)
    group_here = lax.axis_index("grp")
    ctx_here = lax.axis_index("ctx")
    place = jnp.stack([group_here, ctx_here]).astype(jnp.int32)

    page_ids = page_table[block_list].reshape(1, tile_count * listed)
    page_ids = jnp.pad(page_ids, ((0, 0), (0, LANES - tile_count * listed)), constant_values=-1)
    everywhere = jnp.broadcast_to(page_ids, (groups * ctx_count, LANES))
    lists = lax.all_to_all(everywhere, ("grp", "ctx"), split_axis=0, concat_axis=0, tiled=True)
    sends, places = make_plan(place, lists, groups, ctx_count, cap, pages_here)

    shifts = visit_order(groups)
    homes = [jnp.stack([(group_here - s) % groups, ctx_here]).astype(jnp.int32) for s in shifts]
    visiting = []
    for s in shifts[:-1]:
        visiting.append(shifted(queries, "grp", s))
    visiting.append(queries)

    parts, sizes = [], []
    for r, s in enumerate(shifts):
        gathered = collect(homes[r], sends, keys_cache, values_cache, ctx_count, cap)
        arrived = []
        for k in range(1, ctx_count):
            arrived.append(shifted(gathered[k - 1], "ctx", k))
        local = (homes[r], places, sends, visiting[r], keys_cache, values_cache, arrived)
        if s:
            part, size = attend(*local, per_grp, cap, heads)
            parts.append(shifted(part, "grp", -s))
            sizes.append(shifted(size, "grp", -s))
    return attend(*local, per_grp, cap, heads, jnp.stack(parts), jnp.stack(sizes))[0]


def visit_order(groups):
    middle = groups // 2
    return [middle] + [s for s in range(1, groups) if s != middle] + [0]


def solution(mesh):
    in_specs = (
        P(("grp", "ctx"), None),
        P(("grp", "ctx"), None, None),
        P(("grp", "ctx"), None, None),
        P(("grp", "ctx"), None),
        P(),
    )
    out_specs = P(("grp", "ctx"), None)

    return jax.shard_map(on_device, mesh=mesh, in_specs=in_specs, out_specs=out_specs, check_vma=False)
```

time: 651 us -> 291 us (0.45)
  the two profiles are of different devices: /device:TPU:0 before, /device:TPU:3 now
where the time goes in v1:
time: 291 us; the launch traced here: 289 us
  waiting for transfers between devices  134 us (46%)
  starting transfers between devices  80.2 us (28%)
  Pallas kernels  62 us (21%)
  other arithmetic  7.12 us (2%)
  local copies, waits for them, and re-layouts  5.83 us (2%)
    ppermute x37, waiting for transfers between devices, shifted(): return lax.ppermute(block, axis, route)  130 us
    ppermute x37, starting transfers between devices, shifted(): return lax.ppermute(block, axis, route)  73.8 us
    pallas_call x4, Pallas kernels, attend(): pl.pallas_call(functools.partial(attend_body, per_grp, heads, others, ctx...  41.7 us
    pallas_call x4, Pallas kernels, collect(): pl.pallas_call(functools.partial(collect_body, ctx_count, cap), out_shape...  18.2 us
    all_to_all x1, starting transfers between devices, on_device(): lax.all_to_all(everywhere, ('grp', 'ctx'), split_axis=0, concat_axis=0, t...  6.41 us
  transfers between devices with their start and end apart: 38, of which 16 were waited for; matrix products, arithmetic and copies ran while one was open for 2% of the time, Pallas kernels for 15%

profile of v1, /device:TPU:3, one launch (start us, length us, event | category | flops | bytes accessed | tf_op | source)
XLA Modules:
  0.0 289.4 jit_solution(18274852873038500130)
XLA Ops:
  0.8 1.1 gather_fusion
  2.6 6.4 %all-to-all-start = ((s32[32,1,128]{2,1,0:T(1,128)}), s32[32,1,128]{2,1,0:T(1,128)S(1)}, u32[]{:S(2)}, u32[]{:S(2)}) async-start(s32[32,1,128]{2,1,0:T(1,128)} %broadcast_in_dim.9), calls=%async_computation | async-start | bytes 32768 | tf_op jit(solution)/shard_map/all_to_all | solution.py:261
  10.3 4.3 %all-to-all-done = s32[32,1,128]{2,1,0:T(1,128)S(1)} async-done(((s32[32,1,128]{2,1,0:T(1,128)}), s32[32,1,128]{2,1,0:T(1,128)S(1)}, u32[]{:S(2)}, u32[]{:S(2)}) %all-to-all-start) | async-done | bytes 16416 | tf_op jit(solution)/shard_map/all_to_all | solution.py:261
  15.2 2.1 plan.1
  17.3 4.5 %collect.7 = (bf16[7,2,128,128]{3,2,1,0:T(8,128)(2,1)}, bf16[7,2,128,128]{3,2,1,0:T(8,128)(2,1)}, bf16[7,2,128,128]{3,2,1,0:T(8,128)(2,1)}, bf16[7,2,128,128]{3,...) custom-call(s32[2]{0:T(128)} %pad_add_fusion.4.home, ...), custom_call_target="tpu_custom_call" | custom-call | tf_op jit(solution)/shard_map/collect/pallas_call | solution.py:108
  21.8 1.3 collective-permute-start.26
  23.4 1.2 collective-permute-start.28
  24.9 1.6 collective-permute-start.30
  26.5 6.6 %collective-permute-done.26.rest_0_ = bf16[7,2,128,128]{3,2,1,0:T(8,128)(2,1)S(1)} collective-permute-done((bf16[7,2,128,128]{3,2,1,0:T(8,128)(2,1)}, bf16[7,2,128,128]{3,2,1,0:T(8,128)(2,1)S(1)}, u32[]{:S(2)}, u32[]{:S(2)}) %collective-permute-start.26) | collective-permute-done | bytes 458784 | tf_op jit(solution)/shard_map/ppermute | solution.py:19
  33.2 10.0 %collective-permute-done.27.rest_1_ = bf16[7,2,128,128]{3,2,1,0:T(8,128)(2,1)S(1)} collective-permute-done((bf16[7,2,128,128]{3,2,1,0:T(8,128)(2,1)}, bf16[7,2,128,128]{3,2,1,0:T(8,128)(2,1)S(1)}, u32[]{:S(2)}, u32[]{:S(2)}) %collective-permute-start.27) | collective-permute-done | bytes 458784 | tf_op jit(solution)/shard_map/ppermute | solution.py:19
  43.7 4.5 %collect.6 = (bf16[7,2,128,128]{3,2,1,0:T(8,128)(2,1)}, bf16[7,2,128,128]{3,2,1,0:T(8,128)(2,1)}, bf16[7,2,128,128]{3,2,1,0:T(8,128)(2,1)}, bf16[7,2,128,128]{3,...) custom-call(s32[2]{0:T(128)} %pad_add_fusion.3.home, ...), custom_call_target="tpu_custom_call" | custom-call | tf_op jit(solution)/shard_map/collect/pallas_call | solution.py:108
  48.3 8.3 %collective-permute-start.17 = (bf16[7,2,128,128]{3,2,1,0:T(8,128)(2,1)}, bf16[7,2,128,128]{3,2,1,0:T(8,128)(2,1)S(1)}, u32[]{:S(2)}, u32[]{:S(2)}) collective-permute-start(bf16[7,2,128,128]{3,2,1,0:T(8,128)(2,1)} %get-tuple-element.58), channel_id=1, source_target_pairs={{7,0},{0,1},{1,2},{2,3},{3,4},{4,5},{5,6},{6,7},{15,8},{8,9},{9,10... | collective-permute-start | bytes 1376264 | tf_op jit(solution)/shard_map/ppermute | solution.py:19
  56.6 10.0 %collective-permute-start.18 = (bf16[7,2,128,128]{3,2,1,0:T(8,128)(2,1)}, bf16[7,2,128,128]{3,2,1,0:T(8,128)(2,1)S(1)}, u32[]{:S(2)}, u32[]{:S(2)}) collective-permute-start(bf16[7,2,128,128]{3,2,1,0:T(8,128)(2,1)} %get-tuple-element.59), channel_id=1, source_target_pairs={{6,0},{7,1},{0,2},{1,3},{2,4},{3,5},{4,6},{5,7},{14,8},{15,9},{8,1... | collective-permute-start | bytes 1376264 | tf_op jit(solution)/shard_map/ppermute | solution.py:19
  66.7 0.8 copy-done.4
  67.4 1.2 collective-permute-start.20
  68.6 2.0 collective-permute-start.21
  70.6 1.9 collective-permute-done.17.rest_0_
  72.5 0.8 copy-done.6
  73.3 9.2 %collective-permute-done.18.rest_1_ = bf16[7,2,128,128]{3,2,1,0:T(8,128)(2,1)S(1)} collective-permute-done((bf16[7,2,128,128]{3,2,1,0:T(8,128)(2,1)}, bf16[7,2,128,128]{3,2,1,0:T(8,128)(2,1)S(1)}, u32[]{:S(2)}, u32[]{:S(2)}) %collective-permute-start.18) | collective-permute-done | bytes 458784 | tf_op jit(solution)/shard_map/ppermute | solution.py:19
  82.5 0.8 copy-done.8
  83.9 4.7 %collect.5 = (bf16[7,2,128,128]{3,2,1,0:T(8,128)(2,1)}, bf16[7,2,128,128]{3,2,1,0:T(8,128)(2,1)}, bf16[7,2,128,128]{3,2,1,0:T(8,128)(2,1)}, bf16[7,2,128,128]{3,...) custom-call(s32[2]{0:T(128)} %pad_add_fusion.2.home, ...), custom_call_target="tpu_custom_call" | custom-call | tf_op jit(solution)/shard_map/collect/pallas_call | solution.py:108
  89.2 17.2 %collective-permute-done.20.rest_3_ = bf16[7,2,128,128]{3,2,1,0:T(8,128)(2,1)} collective-permute-done((bf16[7,2,128,128]{3,2,1,0:T(8,128)(2,1)}, bf16[7,2,128,128]{3,2,1,0:T(8,128)(2,1)}, u32[]{:S(2)}, u32[]{:S(2)}) %collective-permute-start.20) | collective-permute-done | bytes 458784 | tf_op jit(solution)/shard_map/ppermute | solution.py:19
  106.4 2.1 collective-permute-done.21.rest_4_
  108.6 0.8 collective-permute-start.9
  109.4 9.2 %collective-permute-done.8.rest_0_ = bf16[7,2,128,128]{3,2,1,0:T(8,128)(2,1)S(1)} collective-permute-done((bf16[7,2,128,128]{3,2,1,0:T(8,128)(2,1)}, bf16[7,2,128,128]{3,2,1,0:T(8,128)(2,1)S(1)}, u32[]{:S(2)}, u32[]{:S(2)}) %collective-permute-start.8) | collective-permute-done | bytes 458784 | tf_op jit(solution)/shard_map/ppermute | solution.py:19
  118.9 9.5 %collective-permute-done.9.rest_1_ = bf16[7,2,128,128]{3,2,1,0:T(8,128)(2,1)S(1)} collective-permute-done((bf16[7,2,128,128]{3,2,1,0:T(8,128)(2,1)}, bf16[7,2,128,128]{3,2,1,0:T(8,128)(2,1)S(1)}, u32[]{:S(2)}, u32[]{:S(2)}) %collective-permute-start.9) | collective-permute-done | bytes 458784 | tf_op jit(solution)/shard_map/ppermute | solution.py:19
  128.4 0.8 collective-permute-start.11
  129.7 11.5 %collective-permute-start.12 = (bf16[7,2,128,128]{3,2,1,0:T(8,128)(2,1)}, bf16[7,2,128,128]{3,2,1,0:T(8,128)(2,1)S(1)}, u32[]{:S(2)}, u32[]{:S(2)}) collective-permute-start(bf16[7,2,128,128]{3,2,1,0:T(8,128)(2,1)} %get-tuple-element.54), channel_id=1, source_target_pairs={{3,0},{4,1},{5,2},{6,3},{7,4},{0,5},{1,6},{2,7},{11,8},{12,9},{13,... | collective-permute-start | bytes 1376264 | tf_op jit(solution)/shard_map/ppermute | solution.py:19
  141.6 1.0 copy-done.5
  142.6 10.7 %attend.5 = (bf16[384,1024]{1,0:T(8,128)(2,1)}, f32[3,8,128]{2,1,0:T(8,128)S(1)}) custom-call(s32[2]{0:T(128)S(1)} %copy-done.12, s32[4,128]{1,0:T(4,128)S(1)} %copy-done.10, s32[32,128]{1,0:T(8,128)S(1)} %copy-done.1, bf16[384,1024]{1,0:T(8,128)(2,1)S(1)} %collective-permute-done.25.q, bf16[128,128,128]{2,1,0:T(8,128)(2,1)} %keys.15, ...), custom_call_target="tpu_custom_call" | custom-call | tf_op jit(solution)/shard_map/attend/pallas_call | solution.py:227
  153.4 9.4 %attend.4 = (bf16[384,1024]{1,0:T(8,128)(2,1)S(1)}, f32[3,8,128]{2,1,0:T(8,128)S(1)}) custom-call(s32[2]{0:T(128)S(1)} %copy-done.13, s32[4,128]{1,0:T(4,128)S(1)} %copy-done.10, s32[32,128]{1,0:T(8,128)S(1)} %copy-done.1, bf16[384,1024]{1,0:T(8,128)(2,1)S(1)} %collective-permute-done.16.q, bf16[128,128,128]{2,1,0:T(8,128)(2,1)} %keys.15, ...), custom_call_target="tpu_custom_call" | custom-call | tf_op jit(solution)/shard_map/attend/pallas_call | solution.py:227
  163.2 2.9 %collective-permute-start.24 = (bf16[384,1024]{1,0:T(8,128)(2,1)S(1)}, bf16[384,1024]{1,0:T(8,128)(2,1)}, u32[]{:S(2)}, u32[]{:S(2)}) collective-permute-start(bf16[384,1024]{1,0:T(8,128)(2,1)S(1)} %get-tuple-element.65), channel_id=1, source_target_pairs={{8,0},{16,8},{24,16},{0,24},{9,1},{17,9},{25,17},{1,25},{10,2},{18... | collective-permute-start | bytes 2359304 | tf_op jit(solution)/shard_map/ppermute | solution.py:19
  166.1 9.6 %attend.3 = (bf16[384,1024]{1,0:T(8,128)(2,1)S(1)}, f32[3,8,128]{2,1,0:T(8,128)S(1)}) custom-call(s32[2]{0:T(128)S(1)} %copy-done.14, s32[4,128]{1,0:T(4,128)S(1)} %copy-done.10, s32[32,128]{1,0:T(8,128)S(1)} %copy-done.1, bf16[384,1024]{1,0:T(8,128)(2,1)S(1)} %collective-permute-done.7.q, bf16[128,128,128]{2,1,0:T(8,128)(2,1)} %keys.15, ...), custom_call_target="tpu_custom_call" | custom-call | tf_op jit(solution)/shard_map/attend/pallas_call | solution.py:227
  176.4 4.5 %collect.4 = (bf16[7,2,128,128]{3,2,1,0:T(8,128)(2,1)}, bf16[7,2,128,128]{3,2,1,0:T(8,128)(2,1)}, bf16[7,2,128,128]{3,2,1,0:T(8,128)(2,1)}, bf16[7,2,128,128]{3,...) custom-call(s32[2]{0:T(128)} %pad_add_fusion.home, ...), custom_call_target="tpu_custom_call" | custom-call | tf_op jit(solution)/shard_map/collect/pallas_call | solution.py:108
  180.9 2.8 collective-permute-start
  183.7 1.2 collective-permute-start.1
  184.9 8.9 %collective-permute-done.rest_0_ = bf16[7,2,128,128]{3,2,1,0:T(8,128)(2,1)S(1)} collective-permute-done((bf16[7,2,128,128]{3,2,1,0:T(8,128)(2,1)}, bf16[7,2,128,128]{3,2,1,0:T(8,128)(2,1)S(1)}, u32[]{:S(2)}, u32[]{:S(2)}) %collective-permute-start) | collective-permute-done | bytes 458784 | tf_op jit(solution)/shard_map/ppermute | solution.py:19
  194.0 7.1 %collective-permute-done.1.rest_1_ = bf16[7,2,128,128]{3,2,1,0:T(8,128)(2,1)S(1)} collective-permute-done((bf16[7,2,128,128]{3,2,1,0:T(8,128)(2,1)}, bf16[7,2,128,128]{3,2,1,0:T(8,128)(2,1)S(1)}, u32[]{:S(2)}, u32[]{:S(2)}) %collective-permute-start.1) | collective-permute-done | bytes 458784 | tf_op jit(solution)/shard_map/ppermute | solution.py:19
  201.1 0.8 collective-permute-start.35
  201.9 13.3 %collective-permute-done.36 = f32[3,8,128]{2,1,0:T(8,128)S(1)} collective-permute-done((f32[3,8,128]{2,1,0:T(8,128)S(1)}, f32[3,8,128]{2,1,0:T(8,128)S(1)}, u32[]{:S(2)}, u32[]{:S(2)}) %collective-permute-start.36) | collective-permute-done | bytes 12320 | tf_op jit(solution)/shard_map/ppermute | solution.py:19
  215.2 17.1 %collective-permute-start.34 = (f32[3,8,128]{2,1,0:T(8,128)S(1)}, f32[3,8,128]{2,1,0:T(8,128)S(1)}, u32[]{:S(2)}, u32[]{:S(2)}) collective-permute-start(f32[3,8,128]{2,1,0:T(8,128)S(1)} %get-tuple-element.74), channel_id=1, source_target_pairs={{16,0},{24,8},{0,16},{8,24},{17,1},{25,9},{1,17},{9,25},{18,2},{26... | collective-permute-start | bytes 36872 | tf_op jit(solution)/shard_map/ppermute | solution.py:19
  232.3 3.9 %collective-permute-start.2 = (bf16[7,2,128,128]{3,2,1,0:T(8,128)(2,1)}, bf16[7,2,128,128]{3,2,1,0:T(8,128)(2,1)S(1)}, u32[]{:S(2)}, u32[]{:S(2)}) collective-permute-start(bf16[7,2,128,128]{3,2,1,0:T(8,128)(2,1)} %get-tuple-element.45), channel_id=1, source_target_pairs={{5,0},{6,1},{7,2},{0,3},{1,4},{2,5},{3,6},{4,7},{13,8},{14,9},{15,... | collective-permute-start | bytes 1376264 | tf_op jit(solution)/shard_map/ppermute | solution.py:19
  236.7 2.6 collective-permute-start.4
  239.9 3.3 %pad_maximum_fusion.rest_7_ = bf16[3,384,1024]{2,1,0:T(8,128)(2,1)} fusion(bf16[1,384,1024]{2,1,0:T(8,128)(2,1)} %bitcast.11, bf16[1,384,1024]{2,1,0:T(8,128)(2,1)} %bitcast.9, bf16[1,384,1024]{2,1,0:T(8,128)(2,1)} %bitcast.7), kind=kLoop, calls=%fused_computation.1 | loop fusion | flops 2359296 | bytes 4718592 | tf_op jit(solution)/shard_map/stack | solution.py:282
  243.2 21.2 %collective-permute-done.2.rest_2_ = bf16[7,2,128,128]{3,2,1,0:T(8,128)(2,1)S(1)} collective-permute-done((bf16[7,2,128,128]{3,2,1,0:T(8,128)(2,1)}, bf16[7,2,128,128]{3,2,1,0:T(8,128)(2,1)S(1)}, u32[]{:S(2)}, u32[]{:S(2)}) %collective-permute-start.2) | collective-permute-done | bytes 458784 | tf_op jit(solution)/shard_map/ppermute | solution.py:19
  264.3 10.6 %collective-permute-done.3.rest_3_ = bf16[7,2,128,128]{3,2,1,0:T(8,128)(2,1)S(1)} collective-permute-done((bf16[7,2,128,128]{3,2,1,0:T(8,128)(2,1)}, bf16[7,2,128,128]{3,2,1,0:T(8,128)(2,1)S(1)}, u32[]{:S(2)}, u32[]{:S(2)}) %collective-permute-start.3) | collective-permute-done | bytes 458784 | tf_op jit(solution)/shard_map/ppermute | solution.py:19
  275.0 2.2 collective-permute-done.4.rest_4_
  277.2 12.0 %attend_last.1 = bf16[384,1024]{1,0:T(8,128)(2,1)} custom-call(s32[2]{0:T(128)S(1)} %copy-done.11, s32[4,128]{1,0:T(4,128)S(1)} %copy-done.10, s32[32,128]{1,0:T(8,128)S(1)} %copy-done.2, bf16[384,1024]{1,0:T(8,128)(2,1)S(1)} %copy-done.3, bf16[128,128,128]{2,1,0:T(8,128)(2,1)} %keys.15, bf16[128,128,128]{2,1,0:T(8,128)(2,1)} %values.15, ...), custom_call_target="tpu_custom_call" | custom-call | tf_op jit(solution)/shard_map/attend_last/pallas_call | solution.py:227
  (82 shorter events, 9.5 us)
Async XLA Ops:
  2.6 12.0 %all-to-all-start = ((s32[32,1,128]{2,1,0:T(1,128)}), s32[32,1,128]{2,1,0:T(1,128)S(1)}, u32[]{:S(2)}, u32[]{:S(2)}) async-start(s32[32,1,128]{2,1,0:T(1,128)} %broadcast_in_dim.9), calls=%async_computation | async-start | bytes 32768 | tf_op jit(solution)/shard_map/all_to_all | solution.py:261
  21.8 11.3 %collective-permute-start.26 = (bf16[7,2,128,128]{3,2,1,0:T(8,128)(2,1)}, bf16[7,2,128,128]{3,2,1,0:T(8,128)(2,1)S(1)}, u32[]{:S(2)}, u32[]{:S(2)}) collective-permute-start(bf16[7,2,128,128]{3,2,1,0:T(8,128)(2,1)} %get-tuple-element.66), channel_id=1, source_target_pairs={{7,0},{0,1},{1,2},{2,3},{3,4},{4,5},{5,6},{6,7},{15,8},{8,9},{9,10... | collective-permute-start | bytes 1376264 | tf_op jit(solution)/shard_map/ppermute | solution.py:19
  23.1 20.0 %collective-permute-start.27 = (bf16[7,2,128,128]{3,2,1,0:T(8,128)(2,1)}, bf16[7,2,128,128]{3,2,1,0:T(8,128)(2,1)S(1)}, u32[]{:S(2)}, u32[]{:S(2)}) collective-permute-start(bf16[7,2,128,128]{3,2,1,0:T(8,128)(2,1)} %get-tuple-element.67), channel_id=1, source_target_pairs={{6,0},{7,1},{0,2},{1,3},{2,4},{3,5},{4,6},{5,7},{14,8},{15,9},{8,1... | collective-permute-start | bytes 1376264 | tf_op jit(solution)/shard_map/ppermute | solution.py:19
  23.4 24.9 %collective-permute-start.28 = (bf16[7,2,128,128]{3,2,1,0:T(8,128)(2,1)}, bf16[7,2,128,128]{3,2,1,0:T(8,128)(2,1)S(1)}, u32[]{:S(2)}, u32[]{:S(2)}) collective-permute-start(bf16[7,2,128,128]{3,2,1,0:T(8,128)(2,1)} %get-tuple-element.68), channel_id=1, source_target_pairs={{5,0},{6,1},{7,2},{0,3},{1,4},{2,5},{3,6},{4,7},{13,8},{14,9},{15,... | collective-permute-start | bytes 1376264 | tf_op jit(solution)/shard_map/ppermute | solution.py:19
  24.6 32.0 %collective-permute-start.29 = (bf16[7,2,128,128]{3,2,1,0:T(8,128)(2,1)}, bf16[7,2,128,128]{3,2,1,0:T(8,128)(2,1)S(1)}, u32[]{:S(2)}, u32[]{:S(2)}) collective-permute-start(bf16[7,2,128,128]{3,2,1,0:T(8,128)(2,1)} %get-tuple-element.69), channel_id=1, source_target_pairs={{4,0},{5,1},{6,2},{7,3},{0,4},{1,5},{2,6},{3,7},{12,8},{13,9},{14,... | collective-permute-start | bytes 1376264 | tf_op jit(solution)/shard_map/ppermute | solution.py:19
  24.9 41.7 %collective-permute-start.30 = (bf16[7,2,128,128]{3,2,1,0:T(8,128)(2,1)}, bf16[7,2,128,128]{3,2,1,0:T(8,128)(2,1)S(1)}, u32[]{:S(2)}, u32[]{:S(2)}) collective-permute-start(bf16[7,2,128,128]{3,2,1,0:T(8,128)(2,1)} %get-tuple-element.70), channel_id=1, source_target_pairs={{3,0},{4,1},{5,2},{6,3},{7,4},{0,5},{1,6},{2,7},{11,8},{12,9},{13,... | collective-permute-start | bytes 1376264 | tf_op jit(solution)/shard_map/ppermute | solution.py:19
  33.2 33.5 %collective-permute-start.31 = (bf16[7,2,128,128]{3,2,1,0:T(8,128)(2,1)}, bf16[7,2,128,128]{3,2,1,0:T(8,128)(2,1)S(1)}, u32[]{:S(2)}, u32[]{:S(2)}) collective-permute-start(bf16[7,2,128,128]{3,2,1,0:T(8,128)(2,1)} %get-tuple-element.71), channel_id=1, source_target_pairs={{2,0},{3,1},{4,2},{5,3},{6,4},{7,5},{0,6},{1,7},{10,8},{11,9},{12,... | collective-permute-start | bytes 1376264 | tf_op jit(solution)/shard_map/ppermute | solution.py:19
  43.1 25.5 %collective-permute-start.32 = (bf16[7,2,128,128]{3,2,1,0:T(8,128)(2,1)}, bf16[7,2,128,128]{3,2,1,0:T(8,128)(2,1)}, u32[]{:S(2)}, u32[]{:S(2)}) collective-permute-start(bf16[7,2,128,128]{3,2,1,0:T(8,128)(2,1)} %get-tuple-element.72), channel_id=1, source_target_pairs={{1,0},{2,1},{3,2},{4,3},{5,4},{6,5},{7,6},{0,7},{9,8},{10,9},{11,1... | collective-permute-start | bytes 1376264 | tf_op jit(solution)/shard_map/ppermute | solution.py:19
  48.3 24.3 %collective-permute-start.17 = (bf16[7,2,128,128]{3,2,1,0:T(8,128)(2,1)}, bf16[7,2,128,128]{3,2,1,0:T(8,128)(2,1)S(1)}, u32[]{:S(2)}, u32[]{:S(2)}) collective-permute-start(bf16[7,2,128,128]{3,2,1,0:T(8,128)(2,1)} %get-tuple-element.58), channel_id=1, source_target_pairs={{7,0},{0,1},{1,2},{2,3},{3,4},{4,5},{5,6},{6,7},{15,8},{8,9},{9,10... | collective-permute-start | bytes 1376264 | tf_op jit(solution)/shard_map/ppermute | solution.py:19
  56.6 25.9 %collective-permute-start.18 = (bf16[7,2,128,128]{3,2,1,0:T(8,128)(2,1)}, bf16[7,2,128,128]{3,2,1,0:T(8,128)(2,1)S(1)}, u32[]{:S(2)}, u32[]{:S(2)}) collective-permute-start(bf16[7,2,128,128]{3,2,1,0:T(8,128)(2,1)} %get-tuple-element.59), channel_id=1, source_target_pairs={{6,0},{7,1},{0,2},{1,3},{2,4},{3,5},{4,6},{5,7},{14,8},{15,9},{8,1... | collective-permute-start | bytes 1376264 | tf_op jit(solution)/shard_map/ppermute | solution.py:19
  66.6 21.9 %collective-permute-start.19 = (bf16[7,2,128,128]{3,2,1,0:T(8,128)(2,1)}, bf16[7,2,128,128]{3,2,1,0:T(8,128)(2,1)}, u32[]{:S(2)}, u32[]{:S(2)}) collective-permute-start(bf16[7,2,128,128]{3,2,1,0:T(8,128)(2,1)} %get-tuple-element.60), channel_id=1, source_target_pairs={{5,0},{6,1},{7,2},{0,3},{1,4},{2,5},{3,6},{4,7},{13,8},{14,9},{15,... | collective-permute-start | bytes 1376264 | tf_op jit(solution)/shard_map/ppermute | solution.py:19
  67.4 39.0 %collective-permute-start.20 = (bf16[7,2,128,128]{3,2,1,0:T(8,128)(2,1)}, bf16[7,2,128,128]{3,2,1,0:T(8,128)(2,1)}, u32[]{:S(2)}, u32[]{:S(2)}) collective-permute-start(bf16[7,2,128,128]{3,2,1,0:T(8,128)(2,1)} %get-tuple-element.61), channel_id=1, source_target_pairs={{4,0},{5,1},{6,2},{7,3},{0,4},{1,5},{2,6},{3,7},{12,8},{13,9},{14,... | collective-permute-start | bytes 1376264 | tf_op jit(solution)/shard_map/ppermute | solution.py:19
  68.6 40.0 %collective-permute-start.21 = (bf16[7,2,128,128]{3,2,1,0:T(8,128)(2,1)}, bf16[7,2,128,128]{3,2,1,0:T(8,128)(2,1)}, u32[]{:S(2)}, u32[]{:S(2)}) collective-permute-start(bf16[7,2,128,128]{3,2,1,0:T(8,128)(2,1)} %get-tuple-element.62), channel_id=1, source_target_pairs={{3,0},{4,1},{5,2},{6,3},{7,4},{0,5},{1,6},{2,7},{11,8},{12,9},{13,... | collective-permute-start | bytes 1376264 | tf_op jit(solution)/shard_map/ppermute | solution.py:19
  73.3 35.3 %collective-permute-start.22 = (bf16[7,2,128,128]{3,2,1,0:T(8,128)(2,1)}, bf16[7,2,128,128]{3,2,1,0:T(8,128)(2,1)}, u32[]{:S(2)}, u32[]{:S(2)}) collective-permute-start(bf16[7,2,128,128]{3,2,1,0:T(8,128)(2,1)} %get-tuple-element.63), channel_id=1, source_target_pairs={{2,0},{3,1},{4,2},{5,3},{6,4},{7,5},{0,6},{1,7},{10,8},{11,9},{12,... | collective-permute-start | bytes 1376264 | tf_op jit(solution)/shard_map/ppermute | solution.py:19
  83.3 26.2 %collective-permute-start.23 = (bf16[7,2,128,128]{3,2,1,0:T(8,128)(2,1)}, bf16[7,2,128,128]{3,2,1,0:T(8,128)(2,1)}, u32[]{:S(2)}, u32[]{:S(2)}) collective-permute-start(bf16[7,2,128,128]{3,2,1,0:T(8,128)(2,1)} %get-tuple-element.64), channel_id=1, source_target_pairs={{1,0},{2,1},{3,2},{4,3},{5,4},{6,5},{7,6},{0,7},{9,8},{10,9},{11,1... | collective-permute-start | bytes 1376264 | tf_op jit(solution)/shard_map/ppermute | solution.py:19
  83.8 4.7 %copy-start.3 = (bf16[384,1024]{1,0:T(8,128)(2,1)S(1)}, bf16[384,1024]{1,0:T(8,128)(2,1)}, u32[]{:S(2)}) copy-start(bf16[384,1024]{1,0:T(8,128)(2,1)} %q.1) | copy-start | bytes 2359300
  83.9 57.8 %copy-start.1 = (s32[32,128]{1,0:T(8,128)S(1)}, s32[32,128]{1,0:T(8,128)}, u32[]{:S(2)}) copy-start(s32[32,128]{1,0:T(8,128)} %get-tuple-element.42.sends) | copy-start | bytes 49156
  83.9 57.8 %copy-start.10 = (s32[4,128]{1,0:T(4,128)S(1)}, s32[4,128]{1,0:T(4,128)}, u32[]{:S(2)}) copy-start(s32[4,128]{1,0:T(4,128)} %get-tuple-element.41.places) | copy-start | bytes 6148
  83.9 57.8 %copy-start.12 = (s32[2]{0:T(128)S(1)}, s32[2]{0:T(128)}, u32[]{:S(2)}) copy-start(s32[2]{0:T(128)} %pad_add_fusion.4.home) | copy-start | bytes 28
  88.6 52.6 %collective-permute-start.16 = (bf16[384,1024]{1,0:T(8,128)(2,1)S(1)}, bf16[384,1024]{1,0:T(8,128)(2,1)S(1)}, u32[]{:S(2)}, u32[]{:S(2)}) collective-permute-start(bf16[384,1024]{1,0:T(8,128)(2,1)S(1)} %copy-done.3), channel_id=1, source_target_pairs={{24,0},{0,8},{8,16},{16,24},{25,1},{1,9},{9,17},{17,25},{26,2},{2,... | collective-permute-start | bytes 2359304 | tf_op jit(solution)/shard_map/ppermute | solution.py:19
  106.4 34.8 %collective-permute-start.25 = (bf16[384,1024]{1,0:T(8,128)(2,1)S(1)}, bf16[384,1024]{1,0:T(8,128)(2,1)S(1)}, u32[]{:S(2)}, u32[]{:S(2)}) collective-permute-start(bf16[384,1024]{1,0:T(8,128)(2,1)S(1)} %copy-done.3), channel_id=1, source_target_pairs={{8,0},{16,8},{24,16},{0,24},{9,1},{17,9},{25,17},{1,25},{10,2},{18... | collective-permute-start | bytes 2359304 | tf_op jit(solution)/shard_map/ppermute | solution.py:19
  108.6 10.0 %collective-permute-start.8 = (bf16[7,2,128,128]{3,2,1,0:T(8,128)(2,1)}, bf16[7,2,128,128]{3,2,1,0:T(8,128)(2,1)S(1)}, u32[]{:S(2)}, u32[]{:S(2)}) collective-permute-start(bf16[7,2,128,128]{3,2,1,0:T(8,128)(2,1)} %get-tuple-element.50), channel_id=1, source_target_pairs={{7,0},{0,1},{1,2},{2,3},{3,4},{4,5},{5,6},{6,7},{15,8},{8,9},{9,10... | collective-permute-start | bytes 1376264 | tf_op jit(solution)/shard_map/ppermute | solution.py:19
  108.6 19.8 %collective-permute-start.9 = (bf16[7,2,128,128]{3,2,1,0:T(8,128)(2,1)}, bf16[7,2,128,128]{3,2,1,0:T(8,128)(2,1)S(1)}, u32[]{:S(2)}, u32[]{:S(2)}) collective-permute-start(bf16[7,2,128,128]{3,2,1,0:T(8,128)(2,1)} %get-tuple-element.51), channel_id=1, source_target_pairs={{6,0},{7,1},{0,2},{1,3},{2,4},{3,5},{4,6},{5,7},{14,8},{15,9},{8,1... | collective-permute-start | bytes 1376264 | tf_op jit(solution)/shard_map/ppermute | solution.py:19
  109.4 20.2 %collective-permute-start.10 = (bf16[7,2,128,128]{3,2,1,0:T(8,128)(2,1)}, bf16[7,2,128,128]{3,2,1,0:T(8,128)(2,1)S(1)}, u32[]{:S(2)}, u32[]{:S(2)}) collective-permute-start(bf16[7,2,128,128]{3,2,1,0:T(8,128)(2,1)} %get-tuple-element.52), channel_id=1, source_target_pairs={{5,0},{6,1},{7,2},{0,3},{1,4},{2,5},{3,6},{4,7},{13,8},{14,9},{15,... | collective-permute-start | bytes 1376264 | tf_op jit(solution)/shard_map/ppermute | solution.py:19
  118.6 47.5 %collective-permute-start.7 = (bf16[384,1024]{1,0:T(8,128)(2,1)S(1)}, bf16[384,1024]{1,0:T(8,128)(2,1)S(1)}, u32[]{:S(2)}, u32[]{:S(2)}) collective-permute-start(bf16[384,1024]{1,0:T(8,128)(2,1)S(1)} %copy-done.3), channel_id=1, source_target_pairs={{16,0},{24,8},{0,16},{8,24},{17,1},{25,9},{1,17},{9,25},{18,2},{26... | collective-permute-start | bytes 2359304 | tf_op jit(solution)/shard_map/ppermute | solution.py:19
  128.4 34.4 %collective-permute-start.11 = (bf16[7,2,128,128]{3,2,1,0:T(8,128)(2,1)}, bf16[7,2,128,128]{3,2,1,0:T(8,128)(2,1)S(1)}, u32[]{:S(2)}, u32[]{:S(2)}) collective-permute-start(bf16[7,2,128,128]{3,2,1,0:T(8,128)(2,1)} %get-tuple-element.53), channel_id=1, source_target_pairs={{4,0},{5,1},{6,2},{7,3},{0,4},{1,5},{2,6},{3,7},{12,8},{13,9},{14,... | collective-permute-start | bytes 1376264 | tf_op jit(solution)/shard_map/ppermute | solution.py:19
  129.7 33.5 %collective-permute-start.12 = (bf16[7,2,128,128]{3,2,1,0:T(8,128)(2,1)}, bf16[7,2,128,128]{3,2,1,0:T(8,128)(2,1)S(1)}, u32[]{:S(2)}, u32[]{:S(2)}) collective-permute-start(bf16[7,2,128,128]{3,2,1,0:T(8,128)(2,1)} %get-tuple-element.54), channel_id=1, source_target_pairs={{3,0},{4,1},{5,2},{6,3},{7,4},{0,5},{1,6},{2,7},{11,8},{12,9},{13,... | collective-permute-start | bytes 1376264 | tf_op jit(solution)/shard_map/ppermute | solution.py:19
  141.2 24.9 %collective-permute-start.13 = (bf16[7,2,128,128]{3,2,1,0:T(8,128)(2,1)}, bf16[7,2,128,128]{3,2,1,0:T(8,128)(2,1)S(1)}, u32[]{:S(2)}, u32[]{:S(2)}) collective-permute-start(bf16[7,2,128,128]{3,2,1,0:T(8,128)(2,1)} %get-tuple-element.55), channel_id=1, source_target_pairs={{2,0},{3,1},{4,2},{5,3},{6,4},{7,5},{0,6},{1,7},{10,8},{11,9},{12,... | collective-permute-start | bytes 1376264 | tf_op jit(solution)/shard_map/ppermute | solution.py:19
  141.2 24.9 %collective-permute-start.14 = (bf16[7,2,128,128]{3,2,1,0:T(8,128)(2,1)}, bf16[7,2,128,128]{3,2,1,0:T(8,128)(2,1)S(1)}, u32[]{:S(2)}, u32[]{:S(2)}) collective-permute-start(bf16[7,2,128,128]{3,2,1,0:T(8,128)(2,1)} %get-tuple-element.56), channel_id=1, source_target_pairs={{1,0},{2,1},{3,2},{4,3},{5,4},{6,5},{7,6},{0,7},{9,8},{10,9},{11,1... | collective-permute-start | bytes 1376264 | tf_op jit(solution)/shard_map/ppermute | solution.py:19
  142.6 10.7 %copy-start.7 = (bf16[7,2,128,128]{3,2,1,0:T(8,128)(2,1)S(1)}, bf16[7,2,128,128]{3,2,1,0:T(8,128)(2,1)}, u32[]{:S(2)}) copy-start(bf16[7,2,128,128]{3,2,1,0:T(8,128)(2,1)} %copy-done.6) | copy-start | bytes 1376260
  142.6 10.7 %copy-start.9 = (bf16[7,2,128,128]{3,2,1,0:T(8,128)(2,1)S(1)}, bf16[7,2,128,128]{3,2,1,0:T(8,128)(2,1)}, u32[]{:S(2)}) copy-start(bf16[7,2,128,128]{3,2,1,0:T(8,128)(2,1)} %copy-done.8) | copy-start | bytes 1376260
  142.6 10.7 %copy-start.13 = (s32[2]{0:T(128)S(1)}, s32[2]{0:T(128)}, u32[]{:S(2)}) copy-start(s32[2]{0:T(128)} %pad_add_fusion.3.home) | copy-start | bytes 28
  153.4 12.7 %copy-start.14 = (s32[2]{0:T(128)S(1)}, s32[2]{0:T(128)}, u32[]{:S(2)}) copy-start(s32[2]{0:T(128)} %pad_add_fusion.2.home) | copy-start | bytes 28
  162.8 74.0 %collective-permute-start.33 = (bf16[384,1024]{1,0:T(8,128)(2,1)}, bf16[384,1024]{1,0:T(8,128)(2,1)}, u32[]{:S(2)}, u32[]{:S(2)}) collective-permute-start(bf16[384,1024]{1,0:T(8,128)(2,1)} %get-tuple-element.73), channel_id=1, source_target_pairs={{24,0},{0,8},{8,16},{16,24},{25,1},{1,9},{9,17},{17,25},{26,2},{2,... | collective-permute-start | bytes 2359304 | tf_op jit(solution)/shard_map/ppermute | solution.py:19
  163.2 76.2 %collective-permute-start.24 = (bf16[384,1024]{1,0:T(8,128)(2,1)S(1)}, bf16[384,1024]{1,0:T(8,128)(2,1)}, u32[]{:S(2)}, u32[]{:S(2)}) collective-permute-start(bf16[384,1024]{1,0:T(8,128)(2,1)S(1)} %get-tuple-element.65), channel_id=1, source_target_pairs={{8,0},{16,8},{24,16},{0,24},{9,1},{17,9},{25,17},{1,25},{10,2},{18... | collective-permute-start | bytes 2359304 | tf_op jit(solution)/shard_map/ppermute | solution.py:19
  175.7 64.2 %collective-permute-start.15 = (bf16[384,1024]{1,0:T(8,128)(2,1)S(1)}, bf16[384,1024]{1,0:T(8,128)(2,1)}, u32[]{:S(2)}, u32[]{:S(2)}) collective-permute-start(bf16[384,1024]{1,0:T(8,128)(2,1)S(1)} %get-tuple-element.57), channel_id=1, source_target_pairs={{16,0},{24,8},{0,16},{8,24},{17,1},{25,9},{1,17},{9,25},{18,2},{26... | collective-permute-start | bytes 2359304 | tf_op jit(solution)/shard_map/ppermute | solution.py:19
  180.9 12.8 %collective-permute-start = (bf16[7,2,128,128]{3,2,1,0:T(8,128)(2,1)}, bf16[7,2,128,128]{3,2,1,0:T(8,128)(2,1)S(1)}, u32[]{:S(2)}, u32[]{:S(2)}) collective-permute-start(bf16[7,2,128,128]{3,2,1,0:T(8,128)(2,1)} %get-tuple-element.43), channel_id=1, source_target_pairs={{7,0},{0,1},{1,2},{2,3},{3,4},{4,5},{5,6},{6,7},{15,8},{8,9},{9,10... | collective-permute-start | bytes 1376264 | tf_op jit(solution)/shard_map/ppermute | solution.py:19
  183.7 17.4 %collective-permute-start.1 = (bf16[7,2,128,128]{3,2,1,0:T(8,128)(2,1)}, bf16[7,2,128,128]{3,2,1,0:T(8,128)(2,1)S(1)}, u32[]{:S(2)}, u32[]{:S(2)}) collective-permute-start(bf16[7,2,128,128]{3,2,1,0:T(8,128)(2,1)} %get-tuple-element.44), channel_id=1, source_target_pairs={{6,0},{7,1},{0,2},{1,3},{2,4},{3,5},{4,6},{5,7},{14,8},{15,9},{8,1... | collective-permute-start | bytes 1376264 | tf_op jit(solution)/shard_map/ppermute | solution.py:19
  193.8 21.5 %collective-permute-start.36 = (f32[3,8,128]{2,1,0:T(8,128)S(1)}, f32[3,8,128]{2,1,0:T(8,128)S(1)}, u32[]{:S(2)}, u32[]{:S(2)}) collective-permute-start(f32[3,8,128]{2,1,0:T(8,128)S(1)} %get-tuple-element.76), channel_id=1, source_target_pairs={{24,0},{0,8},{8,16},{16,24},{25,1},{1,9},{9,17},{17,25},{26,2},{2,... | collective-permute-start | bytes 36872 | tf_op jit(solution)/shard_map/ppermute | solution.py:19
  201.1 31.2 %collective-permute-start.35 = (f32[3,8,128]{2,1,0:T(8,128)S(1)}, f32[3,8,128]{2,1,0:T(8,128)S(1)}, u32[]{:S(2)}, u32[]{:S(2)}) collective-permute-start(f32[3,8,128]{2,1,0:T(8,128)S(1)} %get-tuple-element.75), channel_id=1, source_target_pairs={{8,0},{16,8},{24,16},{0,24},{9,1},{17,9},{25,17},{1,25},{10,2},{18... | collective-permute-start | bytes 36872 | tf_op jit(solution)/shard_map/ppermute | solution.py:19
  215.2 21.0 %collective-permute-start.34 = (f32[3,8,128]{2,1,0:T(8,128)S(1)}, f32[3,8,128]{2,1,0:T(8,128)S(1)}, u32[]{:S(2)}, u32[]{:S(2)}) collective-permute-start(f32[3,8,128]{2,1,0:T(8,128)S(1)} %get-tuple-element.74), channel_id=1, source_target_pairs={{16,0},{24,8},{0,16},{8,24},{17,1},{25,9},{1,17},{9,25},{18,2},{26... | collective-permute-start | bytes 36872 | tf_op jit(solution)/shard_map/ppermute | solution.py:19
  232.3 32.0 %collective-permute-start.2 = (bf16[7,2,128,128]{3,2,1,0:T(8,128)(2,1)}, bf16[7,2,128,128]{3,2,1,0:T(8,128)(2,1)S(1)}, u32[]{:S(2)}, u32[]{:S(2)}) collective-permute-start(bf16[7,2,128,128]{3,2,1,0:T(8,128)(2,1)} %get-tuple-element.45), channel_id=1, source_target_pairs={{5,0},{6,1},{7,2},{0,3},{1,4},{2,5},{3,6},{4,7},{13,8},{14,9},{15,... | collective-permute-start | bytes 1376264 | tf_op jit(solution)/shard_map/ppermute | solution.py:19
  236.3 38.7 %collective-permute-start.3 = (bf16[7,2,128,128]{3,2,1,0:T(8,128)(2,1)}, bf16[7,2,128,128]{3,2,1,0:T(8,128)(2,1)S(1)}, u32[]{:S(2)}, u32[]{:S(2)}) collective-permute-start(bf16[7,2,128,128]{3,2,1,0:T(8,128)(2,1)} %get-tuple-element.46), channel_id=1, source_target_pairs={{4,0},{5,1},{6,2},{7,3},{0,4},{1,5},{2,6},{3,7},{12,8},{13,9},{14,... | collective-permute-start | bytes 1376264 | tf_op jit(solution)/shard_map/ppermute | solution.py:19
  236.7 40.5 %collective-permute-start.4 = (bf16[7,2,128,128]{3,2,1,0:T(8,128)(2,1)}, bf16[7,2,128,128]{3,2,1,0:T(8,128)(2,1)S(1)}, u32[]{:S(2)}, u32[]{:S(2)}) collective-permute-start(bf16[7,2,128,128]{3,2,1,0:T(8,128)(2,1)} %get-tuple-element.47), channel_id=1, source_target_pairs={{3,0},{4,1},{5,2},{6,3},{7,4},{0,5},{1,6},{2,7},{11,8},{12,9},{13,... | collective-permute-start | bytes 1376264 | tf_op jit(solution)/shard_map/ppermute | solution.py:19
  239.4 37.8 %collective-permute-start.5 = (bf16[7,2,128,128]{3,2,1,0:T(8,128)(2,1)}, bf16[7,2,128,128]{3,2,1,0:T(8,128)(2,1)S(1)}, u32[]{:S(2)}, u32[]{:S(2)}) collective-permute-start(bf16[7,2,128,128]{3,2,1,0:T(8,128)(2,1)} %get-tuple-element.48), channel_id=1, source_target_pairs={{2,0},{3,1},{4,2},{5,3},{6,4},{7,5},{0,6},{1,7},{10,8},{11,9},{12,... | collective-permute-start | bytes 1376264 | tf_op jit(solution)/shard_map/ppermute | solution.py:19
  239.9 37.3 %collective-permute-start.6 = (bf16[7,2,128,128]{3,2,1,0:T(8,128)(2,1)}, bf16[7,2,128,128]{3,2,1,0:T(8,128)(2,1)S(1)}, u32[]{:S(2)}, u32[]{:S(2)}) collective-permute-start(bf16[7,2,128,128]{3,2,1,0:T(8,128)(2,1)} %get-tuple-element.49), channel_id=1, source_target_pairs={{1,0},{2,1},{3,2},{4,3},{5,4},{6,5},{7,6},{0,7},{9,8},{10,9},{11,1... | collective-permute-start | bytes 1376264 | tf_op jit(solution)/shard_map/ppermute | solution.py:19
  239.9 37.3 %copy-start.2 = (s32[32,128]{1,0:T(8,128)S(1)}, s32[32,128]{1,0:T(8,128)}, u32[]{:S(2)}) copy-start(s32[32,128]{1,0:T(8,128)} %get-tuple-element.42.sends) | copy-start | bytes 49156
  239.9 37.3 %copy-start.11 = (s32[2]{0:T(128)S(1)}, s32[2]{0:T(128)}, u32[]{:S(2)}) copy-start(s32[2]{0:T(128)} %pad_add_fusion.home) | copy-start | bytes 28
  (6 other events, 4.7 us)

commit v2 on v1

--- a/solution.py
+++ b/solution.py
@@ -121,8 +121,10 @@
 
 def attend_body(per_grp, heads, others, ctx_count, cap, home, places, sends, q, keys, values, *rest):
     arrived, rest = rest[: ctx_count - 1], rest[ctx_count - 1 :]
+    parts, sizes = rest[:others], rest[others : 2 * others]
+    rest = rest[2 * others :]
     if others:
-        parts, sizes, out, kbuf, vbuf, sem = rest
+        out, kbuf, vbuf, sem = rest
     else:
         out, size_out, kbuf, vbuf, sem = rest
     tile = pl.program_id(0)
@@ -164,8 +166,7 @@
     )
     pair = 2
     if others:
-        size_rows = [sizes[g] for g in range(others)]
-        size_cols = [jnp.transpose(rows) for rows in size_rows]
+        size_cols = [jnp.transpose(sizes[g][...]) for g in range(others)]
     for first in range(0, heads, pair):
         rows = jnp.concatenate([q[:, (first + i) * hd : (first + i + 1) * hd] for i in range(pair)], axis=0)
         scores = lax.dot_general(
@@ -194,7 +195,7 @@
                 for g in range(others):
                     share = jnp.exp2(theirs[g] - peak)
                     whole = whole + share
-                    merged = merged + parts[g, :, col].astype(jnp.float32) * share
+                    merged = merged + parts[g][:, col].astype(jnp.float32) * share
                 out[:, col] = (merged / whole).astype(out.dtype)
             else:
                 out[:, col] = mine.astype(out.dtype)
@@ -203,12 +204,12 @@
                 )
 
 
-def attend(home, places, sends, q, keys, values, arrived, per_grp, cap, heads, parts=None, sizes=None):
+def attend(home, places, sends, q, keys, values, arrived, per_grp, cap, heads, parts=(), sizes=()):
     tokens, width = q.shape
     block, hd = keys.shape[1:]
     tiles = tokens // block
     ctx_count = len(arrived) + 1
-    others = 0 if parts is None else parts.shape[0]
+    others = len(parts)
     q_spec = pl.BlockSpec((block, width), lambda t, *_: (t, 0))
     size_shape = (heads, block)
     in_specs = [q_spec] + [pl.BlockSpec(memory_space=pl.ANY)] * (ctx_count + 1)
@@ -216,11 +217,9 @@
     out_shape = [jax.ShapeDtypeStruct((tokens, width), q.dtype)]
     out_specs = [q_spec]
     if others:
-        in_specs += [
-            pl.BlockSpec((others, block, width), lambda t, *_: (0, t, 0)),
-            pl.BlockSpec((others, None) + size_shape, lambda t, *_: (0, t, 0, 0)),
-        ]
-        operands += [parts, sizes]
+        in_specs += [q_spec] * others
+        in_specs += [pl.BlockSpec((None,) + size_shape, lambda t, *_: (t, 0, 0))] * others
+        operands += [*parts, *sizes]
     else:
         out_shape.append(jax.ShapeDtypeStruct((tiles,) + size_shape, jnp.float32))
         out_specs.append(pl.BlockSpec((1,) + size_shape, lambda t, *_: (t, 0, 0)))
@@ -279,7 +278,7 @@
             part, size = attend(*local, per_grp, cap, heads)
             parts.append(shifted(part, "grp", -s))
             sizes.append(shifted(size, "grp", -s))
-    return attend(*local, per_grp, cap, heads, jnp.stack(parts), jnp.stack(sizes))[0]
+    return attend(*local, per_grp, cap, heads, parts, sizes)[0]
 
 
 def visit_order(groups):

time: 291 us -> 310 us (1.065)
  the two profiles are of different devices: /device:TPU:3 before, /device:TPU:0 now
where the time goes in v2:
time: 310 us; the launch traced here: 308 us
  waiting for transfers between devices  134 us (43%)
  starting transfers between devices  94.1 us (30%)
  Pallas kernels  59.6 us (19%)
  local copies, waits for them, and re-layouts  16.1 us (5%)
  other arithmetic  3.87 us (1%)
    ppermute x37, waiting for transfers between devices, shifted(): return lax.ppermute(block, axis, route)  128 us
    ppermute x37, starting transfers between devices, shifted(): return lax.ppermute(block, axis, route)  86.7 us
    pallas_call x4, Pallas kernels, attend(): pl.pallas_call(functools.partial(attend_body, per_grp, heads, others, ctx...  41.4 us
    pallas_call x4, Pallas kernels, collect(): pl.pallas_call(functools.partial(collect_body, ctx_count, cap), out_shape...  16.1 us
    unnamed x80, local copies, waits for them, and re-layouts  14.2 us
    all_to_all x1, starting transfers between devices, on_device(): lax.all_to_all(everywhere, ('grp', 'ctx'), split_axis=0, concat_axis=0, t...  7.33 us
  transfers between devices with their start and end apart: 38, of which 20 were waited for; matrix products, arithmetic and copies ran while one was open for 1% of the time, Pallas kernels for 13%

profile of v2, /device:TPU:0, one launch (start us, length us, event | category | flops | bytes accessed | tf_op | source)
XLA Modules:
  0.0 308.2 jit_solution(14790125923127487719)
XLA Ops:
  0.8 1.1 gather_fusion
  2.6 7.3 %all-to-all-start = ((s32[32,1,128]{2,1,0:T(1,128)}), s32[32,1,128]{2,1,0:T(1,128)S(1)}, u32[]{:S(2)}, u32[]{:S(2)}) async-start(s32[32,1,128]{2,1,0:T(1,128)} %broadcast_in_dim.9), calls=%async_computation | async-start | bytes 32768 | tf_op jit(solution)/shard_map/all_to_all | solution.py:260
  11.2 5.8 %all-to-all-done = s32[32,1,128]{2,1,0:T(1,128)S(1)} async-done(((s32[32,1,128]{2,1,0:T(1,128)}), s32[32,1,128]{2,1,0:T(1,128)S(1)}, u32[]{:S(2)}, u32[]{:S(2)}) %all-to-all-start) | async-done | bytes 16416 | tf_op jit(solution)/shard_map/all_to_all | solution.py:260
  17.6 2.1 plan.1
  19.7 4.0 %collect.7 = (bf16[7,2,128,128]{3,2,1,0:T(8,128)(2,1)}, bf16[7,2,128,128]{3,2,1,0:T(8,128)(2,1)}, bf16[7,2,128,128]{3,2,1,0:T(8,128)(2,1)}, bf16[7,2,128,128]{3,...) custom-call(s32[2]{0:T(128)} %pad_add_fusion.4.home, ...), custom_call_target="tpu_custom_call" | custom-call | tf_op jit(solution)/shard_map/collect/pallas_call | solution.py:108
  23.8 1.1 collective-permute-start.27
  25.8 1.4 collective-permute-start.29
  27.2 9.9 %collective-permute-done.26.rest_0_ = bf16[7,2,128,128]{3,2,1,0:T(8,128)(2,1)S(1)} collective-permute-done((bf16[7,2,128,128]{3,2,1,0:T(8,128)(2,1)}, bf16[7,2,128,128]{3,2,1,0:T(8,128)(2,1)S(1)}, u32[]{:S(2)}, u32[]{:S(2)}) %collective-permute-start.26) | collective-permute-done | bytes 458784 | tf_op jit(solution)/shard_map/ppermute | solution.py:19
  37.2 1.3 collective-permute-done.27.rest_1_
  38.4 7.9 %collective-permute-start.32 = (bf16[7,2,128,128]{3,2,1,0:T(8,128)(2,1)}, bf16[7,2,128,128]{3,2,1,0:T(8,128)(2,1)S(1)}, u32[]{:S(2)}, u32[]{:S(2)}) collective-permute-start(bf16[7,2,128,128]{3,2,1,0:T(8,128)(2,1)} %get-tuple-element.72), channel_id=1, source_target_pairs={{1,0},{2,1},{3,2},{4,3},{5,4},{6,5},{7,6},{0,7},{9,8},{10,9},{11,1... | collective-permute-start | bytes 1376264 | tf_op jit(solution)/shard_map/ppermute | solution.py:19
  47.0 4.0 %collect.6 = (bf16[7,2,128,128]{3,2,1,0:T(8,128)(2,1)}, bf16[7,2,128,128]{3,2,1,0:T(8,128)(2,1)}, bf16[7,2,128,128]{3,2,1,0:T(8,128)(2,1)}, bf16[7,2,128,128]{3,...) custom-call(s32[2]{0:T(128)} %pad_add_fusion.3.home, ...), custom_call_target="tpu_custom_call" | custom-call | tf_op jit(solution)/shard_map/collect/pallas_call | solution.py:108
  51.0 6.3 %collective-permute-done.28.rest_2_ = bf16[7,2,128,128]{3,2,1,0:T(8,128)(2,1)S(1)} collective-permute-done((bf16[7,2,128,128]{3,2,1,0:T(8,128)(2,1)}, bf16[7,2,128,128]{3,2,1,0:T(8,128)(2,1)S(1)}, u32[]{:S(2)}, u32[]{:S(2)}) %collective-permute-start.28) | collective-permute-done | bytes 458784 | tf_op jit(solution)/shard_map/ppermute | solution.py:19
  57.5 8.4 %collective-permute-done.30.rest_4_ = bf16[7,2,128,128]{3,2,1,0:T(8,128)(2,1)S(1)} collective-permute-done((bf16[7,2,128,128]{3,2,1,0:T(8,128)(2,1)}, bf16[7,2,128,128]{3,2,1,0:T(8,128)(2,1)S(1)}, u32[]{:S(2)}, u32[]{:S(2)}) %collective-permute-start.30) | collective-permute-done | bytes 458784 | tf_op jit(solution)/shard_map/ppermute | solution.py:19
  65.9 3.2 %collective-permute-start.19 = (bf16[7,2,128,128]{3,2,1,0:T(8,128)(2,1)}, bf16[7,2,128,128]{3,2,1,0:T(8,128)(2,1)}, u32[]{:S(2)}, u32[]{:S(2)}) collective-permute-start(bf16[7,2,128,128]{3,2,1,0:T(8,128)(2,1)} %get-tuple-element.60), channel_id=1, source_target_pairs={{5,0},{6,1},{7,2},{0,3},{1,4},{2,5},{3,6},{4,7},{13,8},{14,9},{15,... | collective-permute-start | bytes 1376264 | tf_op jit(solution)/shard_map/ppermute | solution.py:19
  69.1 1.4 collective-permute-start.20
  70.5 6.0 %collective-permute-done.17.rest_0_ = bf16[7,2,128,128]{3,2,1,0:T(8,128)(2,1)S(1)} collective-permute-done((bf16[7,2,128,128]{3,2,1,0:T(8,128)(2,1)}, bf16[7,2,128,128]{3,2,1,0:T(8,128)(2,1)S(1)}, u32[]{:S(2)}, u32[]{:S(2)}) %collective-permute-start.17) | collective-permute-done | bytes 458784 | tf_op jit(solution)/shard_map/ppermute | solution.py:19
  78.6 7.9 %collective-permute-start.23 = (bf16[7,2,128,128]{3,2,1,0:T(8,128)(2,1)}, bf16[7,2,128,128]{3,2,1,0:T(8,128)(2,1)}, u32[]{:S(2)}, u32[]{:S(2)}) collective-permute-start(bf16[7,2,128,128]{3,2,1,0:T(8,128)(2,1)} %get-tuple-element.64), channel_id=1, source_target_pairs={{1,0},{2,1},{3,2},{4,3},{5,4},{6,5},{7,6},{0,7},{9,8},{10,9},{11,1... | collective-permute-start | bytes 1376264 | tf_op jit(solution)/shard_map/ppermute | solution.py:19
  87.1 4.0 %collect.5 = (bf16[7,2,128,128]{3,2,1,0:T(8,128)(2,1)}, bf16[7,2,128,128]{3,2,1,0:T(8,128)(2,1)}, bf16[7,2,128,128]{3,2,1,0:T(8,128)(2,1)}, bf16[7,2,128,128]{3,...) custom-call(s32[2]{0:T(128)} %pad_add_fusion.2.home, ...), custom_call_target="tpu_custom_call" | custom-call | tf_op jit(solution)/shard_map/collect/pallas_call | solution.py:108
  91.1 5.6 %collective-permute-done.19.rest_2_ = bf16[7,2,128,128]{3,2,1,0:T(8,128)(2,1)} collective-permute-done((bf16[7,2,128,128]{3,2,1,0:T(8,128)(2,1)}, bf16[7,2,128,128]{3,2,1,0:T(8,128)(2,1)}, u32[]{:S(2)}, u32[]{:S(2)}) %collective-permute-start.19) | collective-permute-done | bytes 458784 | tf_op jit(solution)/shard_map/ppermute | solution.py:19
  96.9 8.3 %collective-permute-done.21.rest_4_ = bf16[7,2,128,128]{3,2,1,0:T(8,128)(2,1)} collective-permute-done((bf16[7,2,128,128]{3,2,1,0:T(8,128)(2,1)}, bf16[7,2,128,128]{3,2,1,0:T(8,128)(2,1)}, u32[]{:S(2)}, u32[]{:S(2)}) %collective-permute-start.21) | collective-permute-done | bytes 458784 | tf_op jit(solution)/shard_map/ppermute | solution.py:19
  105.2 5.8 %collective-permute-start.10 = (bf16[7,2,128,128]{3,2,1,0:T(8,128)(2,1)}, bf16[7,2,128,128]{3,2,1,0:T(8,128)(2,1)S(1)}, u32[]{:S(2)}, u32[]{:S(2)}) collective-permute-start(bf16[7,2,128,128]{3,2,1,0:T(8,128)(2,1)} %get-tuple-element.52), channel_id=1, source_target_pairs={{5,0},{6,1},{7,2},{0,3},{1,4},{2,5},{3,6},{4,7},{13,8},{14,9},{15,... | collective-permute-start | bytes 1376264 | tf_op jit(solution)/shard_map/ppermute | solution.py:19
  111.6 4.3 %collective-permute-done.8.rest_0_ = bf16[7,2,128,128]{3,2,1,0:T(8,128)(2,1)S(1)} collective-permute-done((bf16[7,2,128,128]{3,2,1,0:T(8,128)(2,1)}, bf16[7,2,128,128]{3,2,1,0:T(8,128)(2,1)S(1)}, u32[]{:S(2)}, u32[]{:S(2)}) %collective-permute-start.8) | collective-permute-done | bytes 458784 | tf_op jit(solution)/shard_map/ppermute | solution.py:19
  118.6 17.4 %collective-permute-done.10.rest_2_ = bf16[7,2,128,128]{3,2,1,0:T(8,128)(2,1)S(1)} collective-permute-done((bf16[7,2,128,128]{3,2,1,0:T(8,128)(2,1)}, bf16[7,2,128,128]{3,2,1,0:T(8,128)(2,1)S(1)}, u32[]{:S(2)}, u32[]{:S(2)}) %collective-permute-start.10) | collective-permute-done | bytes 458784 | tf_op jit(solution)/shard_map/ppermute | solution.py:19
  138.1 6.0 %collective-permute-done.12.rest_4_ = bf16[7,2,128,128]{3,2,1,0:T(8,128)(2,1)S(1)} collective-permute-done((bf16[7,2,128,128]{3,2,1,0:T(8,128)(2,1)}, bf16[7,2,128,128]{3,2,1,0:T(8,128)(2,1)S(1)}, u32[]{:S(2)}, u32[]{:S(2)}) %collective-permute-start.12) | collective-permute-done | bytes 458784 | tf_op jit(solution)/shard_map/ppermute | solution.py:19
  144.9 4.1 %collective-permute-start.14 = (bf16[7,2,128,128]{3,2,1,0:T(8,128)(2,1)}, bf16[7,2,128,128]{3,2,1,0:T(8,128)(2,1)}, u32[]{:S(2)}, u32[]{:S(2)}) collective-permute-start(bf16[7,2,128,128]{3,2,1,0:T(8,128)(2,1)} %get-tuple-element.56), channel_id=1, source_target_pairs={{1,0},{2,1},{3,2},{4,3},{5,4},{6,5},{7,6},{0,7},{9,8},{10,9},{11,1... | collective-permute-start | bytes 1376264 | tf_op jit(solution)/shard_map/ppermute | solution.py:19
  149.6 4.2 %collect.4 = (bf16[7,2,128,128]{3,2,1,0:T(8,128)(2,1)}, bf16[7,2,128,128]{3,2,1,0:T(8,128)(2,1)}, bf16[7,2,128,128]{3,2,1,0:T(8,128)(2,1)}, bf16[7,2,128,128]{3,...) custom-call(s32[2]{0:T(128)} %pad_add_fusion.home, ...), custom_call_target="tpu_custom_call" | custom-call | tf_op jit(solution)/shard_map/collect/pallas_call | solution.py:108
  153.8 4.4 %collective-permute-start = (bf16[7,2,128,128]{3,2,1,0:T(8,128)(2,1)}, bf16[7,2,128,128]{3,2,1,0:T(8,128)(2,1)S(1)}, u32[]{:S(2)}, u32[]{:S(2)}) collective-permute-start(bf16[7,2,128,128]{3,2,1,0:T(8,128)(2,1)} %get-tuple-element.43), channel_id=1, source_target_pairs={{7,0},{0,1},{1,2},{2,3},{3,4},{4,5},{5,6},{6,7},{15,8},{8,9},{9,10... | collective-permute-start | bytes 1376264 | tf_op jit(solution)/shard_map/ppermute | solution.py:19
  158.2 1.5 collective-permute-start.1
  159.7 1.8 collective-permute-start.2
  161.5 6.9 %collective-permute-done.7.q = bf16[384,1024]{1,0:T(8,128)(2,1)S(1)} collective-permute-done((bf16[384,1024]{1,0:T(8,128)(2,1)S(1)}, bf16[384,1024]{1,0:T(8,128)(2,1)S(1)}, u32[]{:S(2)}, u32[]{:S(2)}) %collective-permute-start.7) | collective-permute-done | bytes 786464 | tf_op jit(solution)/shard_map/ppermute | solution.py:19
  168.4 1.8 collective-permute-start.3
  170.2 1.8 collective-permute-done.25.q
  173.0 1.0 copy-done.6
  174.0 1.0 copy-done.8
  176.1 1.0 copy-done.12
  179.1 9.8 %attend.5 = (bf16[384,1024]{1,0:T(8,128)(2,1)S(1)}, f32[3,8,128]{2,1,0:T(8,128)S(1)}) custom-call(s32[2]{0:T(128)S(1)} %copy-done.33, s32[4,128]{1,0:T(4,128)S(1)} %copy-done.31, s32[32,128]{1,0:T(8,128)S(1)} %copy-done.1, bf16[384,1024]{1,0:T(8,128)(2,1)S(1)} %collective-permute-done.25.q, bf16[128,128,128]{2,1,0:T(8,128)(2,1)} %keys.15, ...), custom_call_target="tpu_custom_call" | custom-call | tf_op jit(solution)/shard_map/attend/pallas_call | solution.py:226
  189.0 9.5 %attend.4 = (bf16[384,1024]{1,0:T(8,128)(2,1)S(1)}, f32[3,8,128]{2,1,0:T(8,128)S(1)}) custom-call(s32[2]{0:T(128)S(1)} %copy-done.34, s32[4,128]{1,0:T(4,128)S(1)} %copy-done.31, s32[32,128]{1,0:T(8,128)S(1)} %copy-done.1, bf16[384,1024]{1,0:T(8,128)(2,1)S(1)} %collective-permute-done.16.q, bf16[128,128,128]{2,1,0:T(8,128)(2,1)} %keys.15, ...), custom_call_target="tpu_custom_call" | custom-call | tf_op jit(solution)/shard_map/attend/pallas_call | solution.py:226
  198.6 10.0 %attend.3 = (bf16[384,1024]{1,0:T(8,128)(2,1)S(1)}, f32[3,8,128]{2,1,0:T(8,128)S(1)}) custom-call(s32[2]{0:T(128)S(1)} %copy-done.35, s32[4,128]{1,0:T(4,128)S(1)} %copy-done.31, s32[32,128]{1,0:T(8,128)S(1)} %copy-done.1, bf16[384,1024]{1,0:T(8,128)(2,1)S(1)} %collective-permute-done.7.q, bf16[128,128,128]{2,1,0:T(8,128)(2,1)} %keys.15, ...), custom_call_target="tpu_custom_call" | custom-call | tf_op jit(solution)/shard_map/attend/pallas_call | solution.py:226
  208.6 15.1 %collective-permute-start.33 = (bf16[384,1024]{1,0:T(8,128)(2,1)S(1)}, bf16[384,1024]{1,0:T(8,128)(2,1)S(1)}, u32[]{:S(2)}, u32[]{:S(2)}) collective-permute-start(bf16[384,1024]{1,0:T(8,128)(2,1)S(1)} %get-tuple-element.73), channel_id=1, source_target_pairs={{24,0},{0,8},{8,16},{16,24},{25,1},{1,9},{9,17},{17,25},{26,2},{2,... | collective-permute-start | bytes 2359304 | tf_op jit(solution)/shard_map/ppermute | solution.py:19
  223.7 1.7 collective-permute-start.15
  225.5 2.0 collective-permute-start.5
  228.2 10.2 %collective-permute-done.5.rest_5_ = bf16[7,2,128,128]{3,2,1,0:T(8,128)(2,1)S(1)} collective-permute-done((bf16[7,2,128,128]{3,2,1,0:T(8,128)(2,1)S(1)}, bf16[7,2,128,128]{3,2,1,0:T(8,128)(2,1)S(1)}, u32[]{:S(2)}, u32[]{:S(2)}) %collective-permute-start.5) | collective-permute-done | bytes 458784 | tf_op jit(solution)/shard_map/ppermute | solution.py:19
  239.1 3.0 collective-permute-done.6.rest_6_
  242.1 2.4 collective-permute-start.35
  244.5 30.3 %collective-permute-done.36.rest_12_ = f32[3,8,128]{2,1,0:T(8,128)S(1)} collective-permute-done((f32[3,8,128]{2,1,0:T(8,128)S(1)}, f32[3,8,128]{2,1,0:T(8,128)S(1)}, u32[]{:S(2)}, u32[]{:S(2)}) %collective-permute-start.36) | collective-permute-done | bytes 12320 | tf_op jit(solution)/shard_map/ppermute | solution.py:19
  274.8 18.6 %collective-permute-start.34 = (f32[3,8,128]{2,1,0:T(8,128)S(1)}, f32[3,8,128]{2,1,0:T(8,128)S(1)}, u32[]{:S(2)}, u32[]{:S(2)}) collective-permute-start(f32[3,8,128]{2,1,0:T(8,128)S(1)} %get-tuple-element.74), channel_id=1, source_target_pairs={{16,0},{24,8},{0,16},{8,24},{17,1},{25,9},{1,17},{9,25},{18,2},{26... | collective-permute-start | bytes 36872 | tf_op jit(solution)/shard_map/ppermute | solution.py:19
  293.4 1.7 collective-permute-done.34.rest_10_
  296.0 12.1 %attend_last.1 = bf16[384,1024]{1,0:T(8,128)(2,1)} custom-call(s32[2]{0:T(128)S(1)} %copy-done.32, s32[4,128]{1,0:T(4,128)S(1)} %copy-done.31, s32[32,128]{1,0:T(8,128)S(1)} %copy-done.1, bf16[384,1024]{1,0:T(8,128)(2,1)S(1)} %copy-done.2, bf16[128,128,128]{2,1,0:T(8,128)(2,1)} %keys.15, bf16[128,128,128]{2,1,0:T(8,128)(2,1)} %values.15, ...), custom_call_target="tpu_custom_call" | custom-call | tf_op jit(solution)/shard_map/attend_last/pallas_call | solution.py:226
  (128 shorter events, 21.4 us)
Async XLA Ops:
  2.6 14.4 %all-to-all-start = ((s32[32,1,128]{2,1,0:T(1,128)}), s32[32,1,128]{2,1,0:T(1,128)S(1)}, u32[]{:S(2)}, u32[]{:S(2)}) async-start(s32[32,1,128]{2,1,0:T(1,128)} %broadcast_in_dim.9), calls=%async_computation | async-start | bytes 32768 | tf_op jit(solution)/shard_map/all_to_all | solution.py:260
  23.7 13.4 %collective-permute-start.26 = (bf16[7,2,128,128]{3,2,1,0:T(8,128)(2,1)}, bf16[7,2,128,128]{3,2,1,0:T(8,128)(2,1)S(1)}, u32[]{:S(2)}, u32[]{:S(2)}) collective-permute-start(bf16[7,2,128,128]{3,2,1,0:T(8,128)(2,1)} %get-tuple-element.66), channel_id=1, source_target_pairs={{7,0},{0,1},{1,2},{2,3},{3,4},{4,5},{5,6},{6,7},{15,8},{8,9},{9,10... | collective-permute-start | bytes 1376264 | tf_op jit(solution)/shard_map/ppermute | solution.py:19
  23.8 14.7 %collective-permute-start.27 = (bf16[7,2,128,128]{3,2,1,0:T(8,128)(2,1)}, bf16[7,2,128,128]{3,2,1,0:T(8,128)(2,1)S(1)}, u32[]{:S(2)}, u32[]{:S(2)}) collective-permute-start(bf16[7,2,128,128]{3,2,1,0:T(8,128)(2,1)} %get-tuple-element.67), channel_id=1, source_target_pairs={{6,0},{7,1},{0,2},{1,3},{2,4},{3,5},{4,6},{5,7},{14,8},{15,9},{8,1... | collective-permute-start | bytes 1376264 | tf_op jit(solution)/shard_map/ppermute | solution.py:19
  24.9 32.4 %collective-permute-start.28 = (bf16[7,2,128,128]{3,2,1,0:T(8,128)(2,1)}, bf16[7,2,128,128]{3,2,1,0:T(8,128)(2,1)S(1)}, u32[]{:S(2)}, u32[]{:S(2)}) collective-permute-start(bf16[7,2,128,128]{3,2,1,0:T(8,128)(2,1)} %get-tuple-element.68), channel_id=1, source_target_pairs={{5,0},{6,1},{7,2},{0,3},{1,4},{2,5},{3,6},{4,7},{13,8},{14,9},{15,... | collective-permute-start | bytes 1376264 | tf_op jit(solution)/shard_map/ppermute | solution.py:19
  25.8 31.6 %collective-permute-start.29 = (bf16[7,2,128,128]{3,2,1,0:T(8,128)(2,1)}, bf16[7,2,128,128]{3,2,1,0:T(8,128)(2,1)S(1)}, u32[]{:S(2)}, u32[]{:S(2)}) collective-permute-start(bf16[7,2,128,128]{3,2,1,0:T(8,128)(2,1)} %get-tuple-element.69), channel_id=1, source_target_pairs={{4,0},{5,1},{6,2},{7,3},{0,4},{1,5},{2,6},{3,7},{12,8},{13,9},{14,... | collective-permute-start | bytes 1376264 | tf_op jit(solution)/shard_map/ppermute | solution.py:19
  27.2 38.6 %collective-permute-start.30 = (bf16[7,2,128,128]{3,2,1,0:T(8,128)(2,1)}, bf16[7,2,128,128]{3,2,1,0:T(8,128)(2,1)S(1)}, u32[]{:S(2)}, u32[]{:S(2)}) collective-permute-start(bf16[7,2,128,128]{3,2,1,0:T(8,128)(2,1)} %get-tuple-element.70), channel_id=1, source_target_pairs={{3,0},{4,1},{5,2},{6,3},{7,4},{0,5},{1,6},{2,7},{11,8},{12,9},{13,... | collective-permute-start | bytes 1376264 | tf_op jit(solution)/shard_map/ppermute | solution.py:19
  37.2 31.9 %collective-permute-start.31 = (bf16[7,2,128,128]{3,2,1,0:T(8,128)(2,1)}, bf16[7,2,128,128]{3,2,1,0:T(8,128)(2,1)S(1)}, u32[]{:S(2)}, u32[]{:S(2)}) collective-permute-start(bf16[7,2,128,128]{3,2,1,0:T(8,128)(2,1)} %get-tuple-element.71), channel_id=1, source_target_pairs={{2,0},{3,1},{4,2},{5,3},{6,4},{7,5},{0,6},{1,7},{10,8},{11,9},{12,... | collective-permute-start | bytes 1376264 | tf_op jit(solution)/shard_map/ppermute | solution.py:19
  38.4 32.1 %collective-permute-start.32 = (bf16[7,2,128,128]{3,2,1,0:T(8,128)(2,1)}, bf16[7,2,128,128]{3,2,1,0:T(8,128)(2,1)S(1)}, u32[]{:S(2)}, u32[]{:S(2)}) collective-permute-start(bf16[7,2,128,128]{3,2,1,0:T(8,128)(2,1)} %get-tuple-element.72), channel_id=1, source_target_pairs={{1,0},{2,1},{3,2},{4,3},{5,4},{6,5},{7,6},{0,7},{9,8},{10,9},{11,1... | collective-permute-start | bytes 1376264 | tf_op jit(solution)/shard_map/ppermute | solution.py:19
  57.3 33.8 %copy-start.7 = (bf16[7,2,128,128]{3,2,1,0:T(8,128)(2,1)}, bf16[7,2,128,128]{3,2,1,0:T(8,128)(2,1)S(1)}, u32[]{:S(2)}) copy-start(bf16[7,2,128,128]{3,2,1,0:T(8,128)(2,1)S(1)} %collective-permute-done.28.rest_2_) | copy-start | bytes 1376260
  57.3 19.3 %collective-permute-start.17 = (bf16[7,2,128,128]{3,2,1,0:T(8,128)(2,1)}, bf16[7,2,128,128]{3,2,1,0:T(8,128)(2,1)S(1)}, u32[]{:S(2)}, u32[]{:S(2)}) collective-permute-start(bf16[7,2,128,128]{3,2,1,0:T(8,128)(2,1)} %get-tuple-element.58), channel_id=1, source_target_pairs={{7,0},{0,1},{1,2},{2,3},{3,4},{4,5},{5,6},{6,7},{15,8},{8,9},{9,10... | collective-permute-start | bytes 1376264 | tf_op jit(solution)/shard_map/ppermute | solution.py:19
  57.5 33.6 %copy-start.9 = (bf16[7,2,128,128]{3,2,1,0:T(8,128)(2,1)}, bf16[7,2,128,128]{3,2,1,0:T(8,128)(2,1)S(1)}, u32[]{:S(2)}) copy-start(bf16[7,2,128,128]{3,2,1,0:T(8,128)(2,1)S(1)} %collective-permute-done.29.rest_3_) | copy-start | bytes 1376260
  57.5 20.3 %collective-permute-start.18 = (bf16[7,2,128,128]{3,2,1,0:T(8,128)(2,1)}, bf16[7,2,128,128]{3,2,1,0:T(8,128)(2,1)S(1)}, u32[]{:S(2)}, u32[]{:S(2)}) collective-permute-start(bf16[7,2,128,128]{3,2,1,0:T(8,128)(2,1)} %get-tuple-element.59), channel_id=1, source_target_pairs={{6,0},{7,1},{0,2},{1,3},{2,4},{3,5},{4,6},{5,7},{14,8},{15,9},{8,1... | collective-permute-start | bytes 1376264 | tf_op jit(solution)/shard_map/ppermute | solution.py:19
  65.9 25.2 %copy-start.11 = (bf16[7,2,128,128]{3,2,1,0:T(8,128)(2,1)}, bf16[7,2,128,128]{3,2,1,0:T(8,128)(2,1)S(1)}, u32[]{:S(2)}) copy-start(bf16[7,2,128,128]{3,2,1,0:T(8,128)(2,1)S(1)} %collective-permute-done.30.rest_4_) | copy-start | bytes 1376260
  65.9 30.9 %collective-permute-start.19 = (bf16[7,2,128,128]{3,2,1,0:T(8,128)(2,1)}, bf16[7,2,128,128]{3,2,1,0:T(8,128)(2,1)}, u32[]{:S(2)}, u32[]{:S(2)}) collective-permute-start(bf16[7,2,128,128]{3,2,1,0:T(8,128)(2,1)} %get-tuple-element.60), channel_id=1, source_target_pairs={{5,0},{6,1},{7,2},{0,3},{1,4},{2,5},{3,6},{4,7},{13,8},{14,9},{15,... | collective-permute-start | bytes 1376264 | tf_op jit(solution)/shard_map/ppermute | solution.py:19
  69.1 27.8 %collective-permute-start.20 = (bf16[7,2,128,128]{3,2,1,0:T(8,128)(2,1)}, bf16[7,2,128,128]{3,2,1,0:T(8,128)(2,1)}, u32[]{:S(2)}, u32[]{:S(2)}) collective-permute-start(bf16[7,2,128,128]{3,2,1,0:T(8,128)(2,1)} %get-tuple-element.61), channel_id=1, source_target_pairs={{4,0},{5,1},{6,2},{7,3},{0,4},{1,5},{2,6},{3,7},{12,8},{13,9},{14,... | collective-permute-start | bytes 1376264 | tf_op jit(solution)/shard_map/ppermute | solution.py:19
  70.5 34.7 %collective-permute-start.21 = (bf16[7,2,128,128]{3,2,1,0:T(8,128)(2,1)}, bf16[7,2,128,128]{3,2,1,0:T(8,128)(2,1)}, u32[]{:S(2)}, u32[]{:S(2)}) collective-permute-start(bf16[7,2,128,128]{3,2,1,0:T(8,128)(2,1)} %get-tuple-element.62), channel_id=1, source_target_pairs={{3,0},{4,1},{5,2},{6,3},{7,4},{0,5},{1,6},{2,7},{11,8},{12,9},{13,... | collective-permute-start | bytes 1376264 | tf_op jit(solution)/shard_map/ppermute | solution.py:19
  77.3 33.7 %collective-permute-start.22 = (bf16[7,2,128,128]{3,2,1,0:T(8,128)(2,1)}, bf16[7,2,128,128]{3,2,1,0:T(8,128)(2,1)}, u32[]{:S(2)}, u32[]{:S(2)}) collective-permute-start(bf16[7,2,128,128]{3,2,1,0:T(8,128)(2,1)} %get-tuple-element.63), channel_id=1, source_target_pairs={{2,0},{3,1},{4,2},{5,3},{6,4},{7,5},{0,6},{1,7},{10,8},{11,9},{12,... | collective-permute-start | bytes 1376264 | tf_op jit(solution)/shard_map/ppermute | solution.py:19
  78.6 33.1 %collective-permute-start.23 = (bf16[7,2,128,128]{3,2,1,0:T(8,128)(2,1)}, bf16[7,2,128,128]{3,2,1,0:T(8,128)(2,1)}, u32[]{:S(2)}, u32[]{:S(2)}) collective-permute-start(bf16[7,2,128,128]{3,2,1,0:T(8,128)(2,1)} %get-tuple-element.64), channel_id=1, source_target_pairs={{1,0},{2,1},{3,2},{4,3},{5,4},{6,5},{7,6},{0,7},{9,8},{10,9},{11,1... | collective-permute-start | bytes 1376264 | tf_op jit(solution)/shard_map/ppermute | solution.py:19
  87.1 29.6 %copy-start.2 = (bf16[384,1024]{1,0:T(8,128)(2,1)S(1)}, bf16[384,1024]{1,0:T(8,128)(2,1)}, u32[]{:S(2)}) copy-start(bf16[384,1024]{1,0:T(8,128)(2,1)} %q.1) | copy-start | bytes 2359300
  96.7 19.2 %collective-permute-start.8 = (bf16[7,2,128,128]{3,2,1,0:T(8,128)(2,1)}, bf16[7,2,128,128]{3,2,1,0:T(8,128)(2,1)S(1)}, u32[]{:S(2)}, u32[]{:S(2)}) collective-permute-start(bf16[7,2,128,128]{3,2,1,0:T(8,128)(2,1)} %get-tuple-element.50), channel_id=1, source_target_pairs={{7,0},{0,1},{1,2},{2,3},{3,4},{4,5},{5,6},{6,7},{15,8},{8,9},{9,10... | collective-permute-start | bytes 1376264 | tf_op jit(solution)/shard_map/ppermute | solution.py:19
  96.9 20.4 %collective-permute-start.9 = (bf16[7,2,128,128]{3,2,1,0:T(8,128)(2,1)}, bf16[7,2,128,128]{3,2,1,0:T(8,128)(2,1)S(1)}, u32[]{:S(2)}, u32[]{:S(2)}) collective-permute-start(bf16[7,2,128,128]{3,2,1,0:T(8,128)(2,1)} %get-tuple-element.51), channel_id=1, source_target_pairs={{6,0},{7,1},{0,2},{1,3},{2,4},{3,5},{4,6},{5,7},{14,8},{15,9},{8,1... | collective-permute-start | bytes 1376264 | tf_op jit(solution)/shard_map/ppermute | solution.py:19
  105.2 30.8 %collective-permute-start.10 = (bf16[7,2,128,128]{3,2,1,0:T(8,128)(2,1)}, bf16[7,2,128,128]{3,2,1,0:T(8,128)(2,1)S(1)}, u32[]{:S(2)}, u32[]{:S(2)}) collective-permute-start(bf16[7,2,128,128]{3,2,1,0:T(8,128)(2,1)} %get-tuple-element.52), channel_id=1, source_target_pairs={{5,0},{6,1},{7,2},{0,3},{1,4},{2,5},{3,6},{4,7},{13,8},{14,9},{15,... | collective-permute-start | bytes 1376264 | tf_op jit(solution)/shard_map/ppermute | solution.py:19
  111.0 26.3 %collective-permute-start.11 = (bf16[7,2,128,128]{3,2,1,0:T(8,128)(2,1)}, bf16[7,2,128,128]{3,2,1,0:T(8,128)(2,1)S(1)}, u32[]{:S(2)}, u32[]{:S(2)}) collective-permute-start(bf16[7,2,128,128]{3,2,1,0:T(8,128)(2,1)} %get-tuple-element.53), channel_id=1, source_target_pairs={{4,0},{5,1},{6,2},{7,3},{0,4},{1,5},{2,6},{3,7},{12,8},{13,9},{14,... | collective-permute-start | bytes 1376264 | tf_op jit(solution)/shard_map/ppermute | solution.py:19
  111.6 32.5 %collective-permute-start.12 = (bf16[7,2,128,128]{3,2,1,0:T(8,128)(2,1)}, bf16[7,2,128,128]{3,2,1,0:T(8,128)(2,1)S(1)}, u32[]{:S(2)}, u32[]{:S(2)}) collective-permute-start(bf16[7,2,128,128]{3,2,1,0:T(8,128)(2,1)} %get-tuple-element.54), channel_id=1, source_target_pairs={{3,0},{4,1},{5,2},{6,3},{7,4},{0,5},{1,6},{2,7},{11,8},{12,9},{13,... | collective-permute-start | bytes 1376264 | tf_op jit(solution)/shard_map/ppermute | solution.py:19
  116.7 43.0 %collective-permute-start.16 = (bf16[384,1024]{1,0:T(8,128)(2,1)S(1)}, bf16[384,1024]{1,0:T(8,128)(2,1)S(1)}, u32[]{:S(2)}, u32[]{:S(2)}) collective-permute-start(bf16[384,1024]{1,0:T(8,128)(2,1)S(1)} %copy-done.2), channel_id=1, source_target_pairs={{24,0},{0,8},{8,16},{16,24},{25,1},{1,9},{9,17},{17,25},{26,2},{2,... | collective-permute-start | bytes 2359304 | tf_op jit(solution)/shard_map/ppermute | solution.py:19
  118.1 50.3 %collective-permute-start.7 = (bf16[384,1024]{1,0:T(8,128)(2,1)S(1)}, bf16[384,1024]{1,0:T(8,128)(2,1)S(1)}, u32[]{:S(2)}, u32[]{:S(2)}) collective-permute-start(bf16[384,1024]{1,0:T(8,128)(2,1)S(1)} %copy-done.2), channel_id=1, source_target_pairs={{16,0},{24,8},{0,16},{8,24},{17,1},{25,9},{1,17},{9,25},{18,2},{26... | collective-permute-start | bytes 2359304 | tf_op jit(solution)/shard_map/ppermute | solution.py:19
  136.8 35.2 %collective-permute-start.25 = (bf16[384,1024]{1,0:T(8,128)(2,1)S(1)}, bf16[384,1024]{1,0:T(8,128)(2,1)S(1)}, u32[]{:S(2)}, u32[]{:S(2)}) collective-permute-start(bf16[384,1024]{1,0:T(8,128)(2,1)S(1)} %copy-done.2), channel_id=1, source_target_pairs={{8,0},{16,8},{24,16},{0,24},{9,1},{17,9},{25,17},{1,25},{10,2},{18... | collective-permute-start | bytes 2359304 | tf_op jit(solution)/shard_map/ppermute | solution.py:19
  138.1 15.7 %collective-permute-start.13 = (bf16[7,2,128,128]{3,2,1,0:T(8,128)(2,1)}, bf16[7,2,128,128]{3,2,1,0:T(8,128)(2,1)}, u32[]{:S(2)}, u32[]{:S(2)}) collective-permute-start(bf16[7,2,128,128]{3,2,1,0:T(8,128)(2,1)} %get-tuple-element.55), channel_id=1, source_target_pairs={{2,0},{3,1},{4,2},{5,3},{6,4},{7,5},{0,6},{1,7},{10,8},{11,9},{12,... | collective-permute-start | bytes 1376264 | tf_op jit(solution)/shard_map/ppermute | solution.py:19
  144.9 13.3 %collective-permute-start.14 = (bf16[7,2,128,128]{3,2,1,0:T(8,128)(2,1)}, bf16[7,2,128,128]{3,2,1,0:T(8,128)(2,1)}, u32[]{:S(2)}, u32[]{:S(2)}) collective-permute-start(bf16[7,2,128,128]{3,2,1,0:T(8,128)(2,1)} %get-tuple-element.56), channel_id=1, source_target_pairs={{1,0},{2,1},{3,2},{4,3},{5,4},{6,5},{7,6},{0,7},{9,8},{10,9},{11,1... | collective-permute-start | bytes 1376264 | tf_op jit(solution)/shard_map/ppermute | solution.py:19
  149.6 22.3 %copy-start.1 = (s32[32,128]{1,0:T(8,128)S(1)}, s32[32,128]{1,0:T(8,128)}, u32[]{:S(2)}) copy-start(s32[32,128]{1,0:T(8,128)} %get-tuple-element.42.sends) | copy-start | bytes 49156
  149.6 22.3 %copy-start.31 = (s32[4,128]{1,0:T(4,128)S(1)}, s32[4,128]{1,0:T(4,128)}, u32[]{:S(2)}) copy-start(s32[4,128]{1,0:T(4,128)} %get-tuple-element.41.places) | copy-start | bytes 6148
  149.6 22.3 %copy-start.33 = (s32[2]{0:T(128)S(1)}, s32[2]{0:T(128)}, u32[]{:S(2)}) copy-start(s32[2]{0:T(128)} %pad_add_fusion.4.home) | copy-start | bytes 28
  153.8 54.8 %collective-permute-start = (bf16[7,2,128,128]{3,2,1,0:T(8,128)(2,1)}, bf16[7,2,128,128]{3,2,1,0:T(8,128)(2,1)S(1)}, u32[]{:S(2)}, u32[]{:S(2)}) collective-permute-start(bf16[7,2,128,128]{3,2,1,0:T(8,128)(2,1)} %get-tuple-element.43), channel_id=1, source_target_pairs={{7,0},{0,1},{1,2},{2,3},{3,4},{4,5},{5,6},{6,7},{15,8},{8,9},{9,10... | collective-permute-start | bytes 1376264 | tf_op jit(solution)/shard_map/ppermute | solution.py:19
  158.2 65.5 %collective-permute-start.1 = (bf16[7,2,128,128]{3,2,1,0:T(8,128)(2,1)}, bf16[7,2,128,128]{3,2,1,0:T(8,128)(2,1)S(1)}, u32[]{:S(2)}, u32[]{:S(2)}) collective-permute-start(bf16[7,2,128,128]{3,2,1,0:T(8,128)(2,1)} %get-tuple-element.44), channel_id=1, source_target_pairs={{6,0},{7,1},{0,2},{1,3},{2,4},{3,5},{4,6},{5,7},{14,8},{15,9},{8,1... | collective-permute-start | bytes 1376264 | tf_op jit(solution)/shard_map/ppermute | solution.py:19
  159.7 64.1 %collective-permute-start.2 = (bf16[7,2,128,128]{3,2,1,0:T(8,128)(2,1)}, bf16[7,2,128,128]{3,2,1,0:T(8,128)(2,1)S(1)}, u32[]{:S(2)}, u32[]{:S(2)}) collective-permute-start(bf16[7,2,128,128]{3,2,1,0:T(8,128)(2,1)} %get-tuple-element.45), channel_id=1, source_target_pairs={{5,0},{6,1},{7,2},{0,3},{1,4},{2,5},{3,6},{4,7},{13,8},{14,9},{15,... | collective-permute-start | bytes 1376264 | tf_op jit(solution)/shard_map/ppermute | solution.py:19
  168.4 57.1 %collective-permute-start.3 = (bf16[7,2,128,128]{3,2,1,0:T(8,128)(2,1)}, bf16[7,2,128,128]{3,2,1,0:T(8,128)(2,1)S(1)}, u32[]{:S(2)}, u32[]{:S(2)}) collective-permute-start(bf16[7,2,128,128]{3,2,1,0:T(8,128)(2,1)} %get-tuple-element.46), channel_id=1, source_target_pairs={{4,0},{5,1},{6,2},{7,3},{0,4},{1,5},{2,6},{3,7},{12,8},{13,9},{14,... | collective-permute-start | bytes 1376264 | tf_op jit(solution)/shard_map/ppermute | solution.py:19
  172.0 55.5 %collective-permute-start.4 = (bf16[7,2,128,128]{3,2,1,0:T(8,128)(2,1)}, bf16[7,2,128,128]{3,2,1,0:T(8,128)(2,1)S(1)}, u32[]{:S(2)}, u32[]{:S(2)}) collective-permute-start(bf16[7,2,128,128]{3,2,1,0:T(8,128)(2,1)} %get-tuple-element.47), channel_id=1, source_target_pairs={{3,0},{4,1},{5,2},{6,3},{7,4},{0,5},{1,6},{2,7},{11,8},{12,9},{13,... | collective-permute-start | bytes 1376264 | tf_op jit(solution)/shard_map/ppermute | solution.py:19
  198.6 26.9 %copy-start.39 = (bf16[7,2,128,128]{3,2,1,0:T(8,128)(2,1)S(1)}, bf16[7,2,128,128]{3,2,1,0:T(8,128)(2,1)}, u32[]{:S(2)}) copy-start(bf16[7,2,128,128]{3,2,1,0:T(8,128)(2,1)} %get-tuple-element.48) | copy-start | bytes 1376260
  198.6 28.9 %copy-start.38 = (bf16[7,2,128,128]{3,2,1,0:T(8,128)(2,1)S(1)}, bf16[7,2,128,128]{3,2,1,0:T(8,128)(2,1)}, u32[]{:S(2)}) copy-start(bf16[7,2,128,128]{3,2,1,0:T(8,128)(2,1)} %get-tuple-element.49) | copy-start | bytes 1376260
  198.6 97.4 %copy-start.32 = (s32[2]{0:T(128)S(1)}, s32[2]{0:T(128)}, u32[]{:S(2)}) copy-start(s32[2]{0:T(128)} %pad_add_fusion.home) | copy-start | bytes 28
  208.6 86.4 %collective-permute-start.33 = (bf16[384,1024]{1,0:T(8,128)(2,1)S(1)}, bf16[384,1024]{1,0:T(8,128)(2,1)S(1)}, u32[]{:S(2)}, u32[]{:S(2)}) collective-permute-start(bf16[384,1024]{1,0:T(8,128)(2,1)S(1)} %get-tuple-element.73), channel_id=1, source_target_pairs={{24,0},{0,8},{8,16},{16,24},{25,1},{1,9},{9,17},{17,25},{26,2},{2,... | collective-permute-start | bytes 2359304 | tf_op jit(solution)/shard_map/ppermute | solution.py:19
  223.7 71.3 %collective-permute-start.24 = (bf16[384,1024]{1,0:T(8,128)(2,1)S(1)}, bf16[384,1024]{1,0:T(8,128)(2,1)S(1)}, u32[]{:S(2)}, u32[]{:S(2)}) collective-permute-start(bf16[384,1024]{1,0:T(8,128)(2,1)S(1)} %get-tuple-element.65), channel_id=1, source_target_pairs={{8,0},{16,8},{24,16},{0,24},{9,1},{17,9},{25,17},{1,25},{10,2},{18... | collective-permute-start | bytes 2359304 | tf_op jit(solution)/shard_map/ppermute | solution.py:19
  223.7 71.3 %collective-permute-start.15 = (bf16[384,1024]{1,0:T(8,128)(2,1)S(1)}, bf16[384,1024]{1,0:T(8,128)(2,1)S(1)}, u32[]{:S(2)}, u32[]{:S(2)}) collective-permute-start(bf16[384,1024]{1,0:T(8,128)(2,1)S(1)} %get-tuple-element.57), channel_id=1, source_target_pairs={{16,0},{24,8},{0,16},{8,24},{17,1},{25,9},{1,17},{9,25},{18,2},{26... | collective-permute-start | bytes 2359304 | tf_op jit(solution)/shard_map/ppermute | solution.py:19
  225.5 12.9 %collective-permute-start.5 = (bf16[7,2,128,128]{3,2,1,0:T(8,128)(2,1)S(1)}, bf16[7,2,128,128]{3,2,1,0:T(8,128)(2,1)S(1)}, u32[]{:S(2)}, u32[]{:S(2)}) collective-permute-start(bf16[7,2,128,128]{3,2,1,0:T(8,128)(2,1)S(1)} %copy-done.39), channel_id=1, source_target_pairs={{2,0},{3,1},{4,2},{5,3},{6,4},{7,5},{0,6},{1,7},{10,8},{11,9},{12,... | collective-permute-start | bytes 1376264 | tf_op jit(solution)/shard_map/ppermute | solution.py:19
  227.5 14.6 %collective-permute-start.6 = (bf16[7,2,128,128]{3,2,1,0:T(8,128)(2,1)S(1)}, bf16[7,2,128,128]{3,2,1,0:T(8,128)(2,1)S(1)}, u32[]{:S(2)}, u32[]{:S(2)}) collective-permute-start(bf16[7,2,128,128]{3,2,1,0:T(8,128)(2,1)S(1)} %copy-done.38), channel_id=1, source_target_pairs={{1,0},{2,1},{3,2},{4,3},{5,4},{6,5},{7,6},{0,7},{9,8},{10,9},{11,1... | collective-permute-start | bytes 1376264 | tf_op jit(solution)/shard_map/ppermute | solution.py:19
  238.4 36.5 %collective-permute-start.36 = (f32[3,8,128]{2,1,0:T(8,128)S(1)}, f32[3,8,128]{2,1,0:T(8,128)S(1)}, u32[]{:S(2)}, u32[]{:S(2)}) collective-permute-start(f32[3,8,128]{2,1,0:T(8,128)S(1)} %get-tuple-element.76), channel_id=1, source_target_pairs={{24,0},{0,8},{8,16},{16,24},{25,1},{1,9},{9,17},{17,25},{26,2},{2,... | collective-permute-start | bytes 36872 | tf_op jit(solution)/shard_map/ppermute | solution.py:19
  242.1 51.3 %collective-permute-start.35 = (f32[3,8,128]{2,1,0:T(8,128)S(1)}, f32[3,8,128]{2,1,0:T(8,128)S(1)}, u32[]{:S(2)}, u32[]{:S(2)}) collective-permute-start(f32[3,8,128]{2,1,0:T(8,128)S(1)} %get-tuple-element.75), channel_id=1, source_target_pairs={{8,0},{16,8},{24,16},{0,24},{9,1},{17,9},{25,17},{1,25},{10,2},{18... | collective-permute-start | bytes 36872 | tf_op jit(solution)/shard_map/ppermute | solution.py:19
  274.8 20.2 %collective-permute-start.34 = (f32[3,8,128]{2,1,0:T(8,128)S(1)}, f32[3,8,128]{2,1,0:T(8,128)S(1)}, u32[]{:S(2)}, u32[]{:S(2)}) collective-permute-start(f32[3,8,128]{2,1,0:T(8,128)S(1)} %get-tuple-element.74), channel_id=1, source_target_pairs={{16,0},{24,8},{0,16},{8,24},{17,1},{25,9},{1,17},{9,25},{18,2},{26... | collective-permute-start | bytes 36872 | tf_op jit(solution)/shard_map/ppermute | solution.py:19
  (30 other events, 170.8 us)

commit v3 on v2

v3 whole, which is shorter than its diff:
```python
import functools
import math

import jax
import jax.numpy as jnp
from jax import lax
from jax.experimental import pallas as pl
from jax.experimental.pallas import tpu as pltpu
from jax.sharding import PartitionSpec as P


LANES = 128
LOG2E = math.log2(math.e)


def shifted(block, axis, distance):
    devices = range(lax.axis_size(axis))
    route = [((i - distance) % len(devices), i) for i in devices]
    return lax.ppermute(block, axis, route)


def plan_body(groups, ctx_count, cap, shift, place, lists, sends, places):
    group, here = place[0], place[1]
    rows = groups * ctx_count
    lane = lax.broadcasted_iota(jnp.int32, (rows, LANES), 1)
    earlier = (
        lax.broadcasted_iota(jnp.int32, (LANES, LANES), 0)
        < lax.broadcasted_iota(jnp.int32, (LANES, LANES), 1)
    ).astype(jnp.float32).astype(jnp.bfloat16)

    def rank_of(mask):
        ones = jnp.where(mask, 1.0, 0.0).astype(jnp.bfloat16)
        return jnp.dot(ones, earlier, preferred_element_type=jnp.float32).astype(jnp.int32)

    pages = lists[...]
    mine = (pages >> shift) == group * ctx_count + here
    rank = rank_of(mine)
    within = pages & ((1 << shift) - 1)
    found = jnp.full((rows, LANES), -1, jnp.int32)
    for k in range(cap):
        chosen = jnp.max(jnp.where(mine & (rank == k), within, -1), axis=1, keepdims=True)
        found = jnp.where(lane == k, chosen, found)
    sends[...] = found

    offset = lax.broadcasted_iota(jnp.int32, (ctx_count, LANES), 0)
    owner = here - offset
    owner = jnp.where(owner < 0, owner + ctx_count, owner)
    order = lax.broadcasted_iota(jnp.int32, (LANES, LANES), 0)
    for home in range(groups):
        listed = jnp.broadcast_to(lists[pl.ds(home * ctx_count + here, 1), :], (ctx_count, LANES))
        member = (listed >> shift) == group * ctx_count + owner
        slot = jnp.where(member, offset * cap + rank_of(member) + 1, 0)
        slot = jnp.broadcast_to(jnp.sum(slot, axis=0, keepdims=True) - 1, (LANES, LANES))
        inside = jnp.broadcast_to(slot[0:1] >= 0, (8, LANES))
        ordinal = (rank_of(inside) + 1).astype(jnp.float32).astype(jnp.bfloat16)
        onehot = jnp.where(slot == order, 1.0, 0.0).astype(jnp.bfloat16)
        position = lax.dot_general(
            ordinal, onehot, (((1,), (1,)), ((), ())), preferred_element_type=jnp.float32
        )
        places[home : home + 1, :] = position[0:1].astype(jnp.int32) - 1


def make_plan(place, lists, groups, ctx_count, cap, pages_here):
    rows = groups * ctx_count
    shift = pages_here.bit_length() - 1
    return pl.pallas_call(
        functools.partial(plan_body, groups, ctx_count, cap, shift),
        out_shape=(
            jax.ShapeDtypeStruct((rows, LANES), jnp.int32),
            jax.ShapeDtypeStruct((groups, LANES), jnp.int32),
        ),
        in_specs=[
            pl.BlockSpec(memory_space=pltpu.SMEM),
            pl.BlockSpec(memory_space=pltpu.VMEM),
        ],
        name="plan",
    )(place, lists)


def collect_body(ctx_count, cap, split, home, sends, keys, values, *rest):
    outs, (stage, sem_in, sem_out) = rest[:-3], rest[-3:]
    here = home[1]
    peers = ctx_count - 1

    def each(k, act):
        row = home[0] * ctx_count + lax.rem(here + k, ctx_count)

        def step(j, carry):
            page = sends[row, j]

            @pl.when(page >= 0)
            def _():
                act(page, j, (k - 1) * cap + j)

            return carry

        lax.fori_loop(0, cap, step, 0)

    def incoming(page, place):
        return (
            pltpu.make_async_copy(keys.at[page], stage.at[place, 0], sem_in.at[place]),
            pltpu.make_async_copy(values.at[page], stage.at[place, 1], sem_in.at[place]),
        )

    def outgoing(k, j, place):
        if split:
            return (
                pltpu.make_async_copy(stage.at[place, 0], outs[k - 1].at[j], sem_out),
                pltpu.make_async_copy(stage.at[place, 1], outs[peers + k - 1].at[j], sem_out),
            )
        return (pltpu.make_async_copy(stage.at[place], outs[k - 1].at[j], sem_out),)

    def fetch(page, j, place):
        for copy in incoming(page, place):
            copy.start()

    for k in range(1, ctx_count):
        each(k, fetch)
    for k in range(1, ctx_count):

        def forward(page, j, place, k=k):
            for copy in incoming(page, place):
                copy.wait()
            for copy in outgoing(k, j, place):
                copy.start()

        each(k, forward)
    for k in range(1, ctx_count):

        def finish(page, j, place, k=k):
            for copy in outgoing(k, j, place):
                copy.wait()

        each(k, finish)


def collect(home, sends, keys, values, ctx_count, cap, split):
    _, block, hd = keys.shape
    peers = ctx_count - 1
    if split:
        shapes = (jax.ShapeDtypeStruct((cap, block, hd), keys.dtype),) * (2 * peers)
    else:
        shapes = (jax.ShapeDtypeStruct((cap, 2, block, hd), keys.dtype),) * peers
    return pl.pallas_call(
        functools.partial(collect_body, ctx_count, cap, split),
        out_shape=shapes,
        grid_spec=pltpu.PrefetchScalarGridSpec(
            num_scalar_prefetch=2,
            grid=(),
            in_specs=[pl.BlockSpec(memory_space=pl.ANY)] * 2,
            out_specs=(pl.BlockSpec(memory_space=pl.ANY),) * len(shapes),
            scratch_shapes=[
                pltpu.VMEM((peers * cap, 2, block, hd), keys.dtype),
                pltpu.SemaphoreType.DMA((peers * cap,)),
                pltpu.SemaphoreType.DMA(()),
            ],
        ),
        name="collect",
    )(home, sends, keys, values)


def load_pages(per_grp, ctx_count, cap, home, places, sends, sources, buffers, sem):
    block, hd = sources[0][0].shape[1:]
    own_row = home[0] * ctx_count + home[1]

    def load(k, j):
        position = places[home[0], k * cap + j]

        @pl.when(position >= 0)
        def _():
            which = position // per_grp
            span = pl.ds(pl.multiple_of(position * block, block), block)
            for source, buffer in zip(sources, buffers):
                origin = source[0].at[sends[own_row, j]] if k == 0 else source[k](j)
                pltpu.make_async_copy(origin, buffer.at[span, pl.ds(0, hd)], sem.at[which]).start()

    for k in range(ctx_count):
        lax.fori_loop(0, cap, lambda j, carry, k=k: (load(k, j), carry)[1], 0)


def wait_pages(per_grp, sources, buffers, tile, sem):
    block, hd = sources[0][0].shape[1:]
    for _ in range(per_grp):
        for source, buffer in zip(sources, buffers):
            pltpu.make_async_copy(
                source[0].at[0], buffer.at[pl.ds(0, block), pl.ds(0, hd)], sem.at[tile]
            ).wait()


def head_rows(q, first, pair, hd):
    return jnp.concatenate([q[:, (first + i) * hd : (first + i + 1) * hd] for i in range(pair)], axis=0)


def weigh(rows, keys_now, factor):
    scores = lax.dot_general(
        rows, keys_now, (((1,), (1,)), ((), ())), preferred_element_type=jnp.float32
    )
    top = jnp.max(scores, axis=1, keepdims=True)
    return jnp.exp2((scores - top) * factor).astype(jnp.bfloat16), top * factor


def as_row(column, diagonal):
    return jnp.sum(jnp.where(diagonal, column, 0.0), axis=0, keepdims=True)


def diagonal_of(block):
    rows = lax.broadcasted_iota(jnp.int32, (block, block), 0)
    return rows == lax.broadcasted_iota(jnp.int32, (block, block), 1)


PAIR = 2


def attend_body(per_grp, heads, ctx_count, cap, home, places, sends, q, keys, values, *rest):
    arrived, (out, size_out, kbuf, vbuf, sem) = rest[: ctx_count - 1], rest[ctx_count - 1 :]
    tile = pl.program_id(0)
    block = q.shape[0]
    hd = q.shape[1] // heads
    sources = [
        [cache] + [lambda j, one=one, part=part: one.at[j, part] for one in arrived]
        for part, cache in enumerate((keys, values))
    ]
    buffers = (kbuf, vbuf)

    @pl.when(tile == 0)
    def _():
        load_pages(per_grp, ctx_count, cap, home, places, sends, sources, buffers, sem)
        vbuf[:, hd:] = jnp.ones((vbuf.shape[0], hd), vbuf.dtype)

    here = pl.ds(pl.multiple_of(tile * per_grp * block, block), per_grp * block)
    wait_pages(per_grp, sources, buffers, tile, sem)
    factor = hd ** (-0.5) * LOG2E
    diagonal = diagonal_of(block)
    for first in range(0, heads, PAIR):
        weights, top = weigh(head_rows(q, first, PAIR, hd), kbuf[here, :], factor)
        summed = jnp.dot(weights, vbuf[here, :], preferred_element_type=jnp.float32)
        for i in range(PAIR):
            span = slice(i * block, (i + 1) * block)
            total = summed[span, hd:]
            out[:, (first + i) * hd : (first + i + 1) * hd] = (summed[span, :hd] / total).astype(out.dtype)
            size_out[0, first + i : first + i + 1, :] = as_row(top[span] + jnp.log2(total), diagonal)


def score_body(per_grp, heads, ctx_count, cap, home, places, sends, q, keys, *rest):
    arrived, (out, top_out, kbuf, sem) = rest[: ctx_count - 1], rest[ctx_count - 1 :]
    tile = pl.program_id(0)
    block = q.shape[0]
    hd = q.shape[1] // heads
    sources = [[keys] + [lambda j, one=one: one.at[j] for one in arrived]]

    @pl.when(tile == 0)
    def _():
        load_pages(per_grp, ctx_count, cap, home, places, sends, sources, (kbuf,), sem)

    here = pl.ds(pl.multiple_of(tile * per_grp * block, block), per_grp * block)
    wait_pages(per_grp, sources, (kbuf,), tile, sem)
    diagonal = diagonal_of(block)
    for first in range(0, heads, PAIR):
        rows = head_rows(q, first, PAIR, hd)
        weights, top = weigh(rows, kbuf[here, :], hd ** (-0.5) * LOG2E)
        out[0, first * block : (first + PAIR) * block, :] = weights
        for i in range(PAIR):
            top_out[0, first + i : first + i + 1, :] = as_row(top[i * block : (i + 1) * block], diagonal)


def finish_body(per_grp, heads, ctx_count, cap, others, home, places, sends, weights, top, values, *rest):
    arrived, rest = rest[: ctx_count - 1], rest[ctx_count - 1 :]
    parts, sizes, (out, vbuf, sem) = rest[:others], rest[others : 2 * others], rest[2 * others :]
    tile = pl.program_id(0)
    block = out.shape[0]
    hd = out.shape[1] // heads
    sources = [[values] + [lambda j, one=one: one.at[j] for one in arrived]]

    @pl.when(tile == 0)
    def _():
        load_pages(per_grp, ctx_count, cap, home, places, sends, sources, (vbuf,), sem)
        vbuf[:, hd:] = jnp.ones((vbuf.shape[0], hd), vbuf.dtype)

    here = pl.ds(pl.multiple_of(tile * per_grp * block, block), per_grp * block)
    wait_pages(per_grp, sources, (vbuf,), tile, sem)
    columns = [jnp.transpose(one[...]) for one in (top,) + tuple(sizes)]
    for first in range(0, heads, PAIR):
        summed = jnp.dot(
            weights[first * block : (first + PAIR) * block, :],
            vbuf[here, :],
            preferred_element_type=jnp.float32,
        )
        for i in range(PAIR):
            span = slice(i * block, (i + 1) * block)
            col = slice((first + i) * hd, (first + i + 1) * hd)
            spread = [jnp.broadcast_to(one[:, first + i : first + i + 1], (block, hd)) for one in columns]
            peak = spread[0]
            for one in spread[1:]:
                peak = jnp.maximum(peak, one)
            share = jnp.exp2(spread[0] - peak)
            whole = summed[span, hd:] * share
            merged = summed[span, :hd] * share
            for part, one in zip(parts, spread[1:]):
                share = jnp.exp2(one - peak)
                whole = whole + share
                merged = merged + part[:, col].astype(jnp.float32) * share
            out[:, col] = (merged / whole).astype(out.dtype)


class Sizes:
    def __init__(self, tokens, block, hd, heads, per_grp, ctx_count, cap, dtype):
        self.block, self.hd, self.heads = block, hd, heads
        self.per_grp, self.ctx_count, self.cap = per_grp, ctx_count, cap
        self.tiles, self.dtype = tokens // block, dtype
        self.keys = per_grp * block
        self.row_spec = pl.BlockSpec((block, heads * hd), lambda t, *_: (t, 0))
        self.rows = jax.ShapeDtypeStruct((tokens, heads * hd), dtype)
        self.stat_spec = pl.BlockSpec((1, heads, block), lambda t, *_: (t, 0, 0))
        self.stat_in = pl.BlockSpec((None, heads, block), lambda t, *_: (t, 0, 0))
        self.stat = jax.ShapeDtypeStruct((self.tiles, heads, block), jnp.float32)

    def call(self, body, in_specs, out_shape, out_specs, buffers, operands, *extra):
        lead = (self.per_grp, self.heads, self.ctx_count, self.cap) + extra
        return pl.pallas_call(
            functools.partial(body, *lead),
            out_shape=out_shape,
            grid_spec=pltpu.PrefetchScalarGridSpec(
                num_scalar_prefetch=3,
                grid=(self.tiles,),
                in_specs=in_specs,
                out_specs=out_specs,
                scratch_shapes=[
                    pltpu.VMEM((self.tiles * self.keys, width), self.dtype) for width in buffers
                ]
                + [pltpu.SemaphoreType.DMA((self.tiles,))],
            ),
            compiler_params=pltpu.CompilerParams(vmem_limit_bytes=48 * 1024 * 1024),
        )(*operands)

    def attend(self, home, places, sends, q, keys, values, arrived):
        return self.call(
            attend_body,
            [self.row_spec] + [pl.BlockSpec(memory_space=pl.ANY)] * (self.ctx_count + 1),
            (self.rows, self.stat),
            (self.row_spec, self.stat_spec),
            (self.hd, 2 * self.hd),
            (home, places, sends, q, keys, values, *arrived),
        )

    def score(self, home, places, sends, q, keys, arrived):
        shape = (self.tiles, self.heads * self.block, self.keys)
        return self.call(
            score_body,
            [self.row_spec] + [pl.BlockSpec(memory_space=pl.ANY)] * self.ctx_count,
            (jax.ShapeDtypeStruct(shape, self.dtype), self.stat),
            (pl.BlockSpec((1,) + shape[1:], lambda t, *_: (t, 0, 0)), self.stat_spec),
            (self.hd,),
            (home, places, sends, q, keys, *arrived),
        )

    def finish(self, home, places, sends, weights, top, values, arrived, parts, sizes):
        return self.call(
            finish_body,
            [pl.BlockSpec((None,) + weights.shape[1:], lambda t, *_: (t, 0, 0)), self.stat_in]
            + [pl.BlockSpec(memory_space=pl.ANY)] * self.ctx_count
            + [self.row_spec] * len(parts)
            + [self.stat_in] * len(sizes),
            self.rows,
            self.row_spec,
            (2 * self.hd,),
            (home, places, sends, weights, top, values, *arrived, *parts, *sizes),
            len(parts),
        )


def on_device(queries, keys_cache, values_cache, block_list, page_table):
    groups = lax.axis_size("grp")
    ctx_count = lax.axis_size("ctx")
    tile_count, listed = block_list.shape
    pages_here, block, hd = keys_cache.shape
    heads = queries.shape[1] // hd
    per_grp = listed // groups
    cap = max(3, (2 * tile_count * per_grp + ctx_count - 1) // ctx_count)
    group_here = lax.axis_index("grp")
    ctx_here = lax.axis_index("ctx")
    place = jnp.stack([group_here, ctx_here]).astype(jnp.int32)
    kernels = Sizes(queries.shape[0], block, hd, heads, per_grp, ctx_count, cap, queries.dtype)

    page_ids = page_table[block_list].reshape(1, tile_count * listed)
    page_ids = jnp.pad(page_ids, ((0, 0), (0, LANES - tile_count * listed)), constant_values=-1)
    everywhere = jnp.broadcast_to(page_ids, (groups * ctx_count, LANES))
    lists = lax.all_to_all(everywhere, ("grp", "ctx"), split_axis=0, concat_axis=0, tiled=True)
    sends, places = make_plan(place, lists, groups, ctx_count, cap, pages_here)

    shifts = visit_order(groups)
    homes = [jnp.stack([(group_here - s) % groups, ctx_here]).astype(jnp.int32) for s in shifts]
    visiting = []
    for s in shifts[:-1]:
        visiting.append(shifted(queries, "grp", s))

    def gather(r, split):
        return collect(homes[r], sends, keys_cache, values_cache, ctx_count, cap, split)

    def swap(gathered):
        arrived = []
        for k in range(1, ctx_count):
            arrived.append(shifted(gathered[k - 1], "ctx", k))
        return arrived

    parts, sizes = [], []
    for r, s in enumerate(shifts[:-1]):
        arrived = swap(gather(r, False))
        part, size = kernels.attend(
            homes[r], places, sends, visiting[r], keys_cache, values_cache, arrived
        )
        parts.append(shifted(part, "grp", -s))
        sizes.append(shifted(size, "grp", -s))
    last = groups - 1
    gathered = gather(last, True)
    arrived_keys = swap(gathered[: ctx_count - 1])
    arrived_values = swap(gathered[ctx_count - 1 :])
    weights, top = kernels.score(homes[last], places, sends, queries, keys_cache, arrived_keys)
    return kernels.finish(
        homes[last], places, sends, weights, top, values_cache, arrived_values, parts, sizes
    )


def visit_order(groups):
    middle = groups // 2
    return [middle] + [s for s in range(1, groups) if s != middle] + [0]


def solution(mesh):
    in_specs = (
        P(("grp", "ctx"), None),
        P(("grp", "ctx"), None, None),
        P(("grp", "ctx"), None, None),
        P(("grp", "ctx"), None),
        P(),
    )
    out_specs = P(("grp", "ctx"), None)

    return jax.shard_map(on_device, mesh=mesh, in_specs=in_specs, out_specs=out_specs, check_vma=False)
```

time: 310 us -> 327 us (1.055)
  starting transfers between devices: 94.1 us -> 121 us
  local copies, waits for them, and re-layouts: 16.1 us -> 7.28 us
  Pallas kernels: 59.6 us -> 63.6 us
  waiting for transfers between devices: 134 us -> 130 us
    ppermute x37 -> x44, starting transfers between devices: 86.7 us -> 113 us  [shifted(): return lax.ppermute(block, axis, route)]
    unnamed x80 -> x52, local copies, waits for them, and re-layouts: 14.2 us -> 5.43 us
    ppermute x37 -> x44, waiting for transfers between devices: 128 us -> 124 us  [shifted(): return lax.ppermute(block, axis, route)]
    pallas_call x8 -> x9, Pallas kernels: 57.5 us -> 61.4 us  [the longest x5 46.9 us: call(): pl.pallas_call(functools.partial(body, *lead), out_shape=out_shape, grid_...]
  transfers between devices with their start and end apart: 38 -> 45, of which waited for: 20 -> 20; matrix products, arithmetic and copies ran while one was open for 1% -> 1% of each run, Pallas kernels for 13% -> 15%
where the time goes in v3:
time: 327 us; the launch traced here: 326 us
  waiting for transfers between devices  130 us (40%)
  starting transfers between devices  121 us (37%)
  Pallas kernels  63.6 us (19%)
  local copies, waits for them, and re-layouts  7.28 us (2%)
  other arithmetic  3.61 us (1%)
    ppermute x44, waiting for transfers between devices, shifted(): return lax.ppermute(block, axis, route)  124 us
    ppermute x44, starting transfers between devices, shifted(): return lax.ppermute(block, axis, route)  113 us
    pallas_call x5, Pallas kernels, call(): pl.pallas_call(functools.partial(body, *lead), out_shape=out_shape, grid_...  46.9 us
    pallas_call x4, Pallas kernels, collect(): pl.pallas_call(functools.partial(collect_body, ctx_count, cap, split), ou...  14.5 us
    all_to_all x1, starting transfers between devices, on_device(): lax.all_to_all(everywhere, ('grp', 'ctx'), split_axis=0, concat_axis=0, t...  7.33 us
  transfers between devices with their start and end apart: 45, of which 20 were waited for; matrix products, arithmetic and copies ran while one was open for 1% of the time, Pallas kernels for 15%

profile of v3, /device:TPU:0, one launch (start us, length us, event | category | flops | bytes accessed | tf_op | source)
XLA Modules:
  0.0 325.6 jit_solution(8967553284137721296)
XLA Ops:
  2.6 7.3 %all-to-all-start = ((s32[32,1,128]{2,1,0:T(1,128)}), s32[32,1,128]{2,1,0:T(1,128)S(1)}, u32[]{:S(2)}, u32[]{:S(2)}) async-start(s32[32,1,128]{2,1,0:T(1,128)} %broadcast_in_dim.9), calls=%async_computation | async-start | bytes 32768 | tf_op jit(solution)/shard_map/all_to_all | solution.py:387
  11.1 5.9 %all-to-all-done = s32[32,1,128]{2,1,0:T(1,128)S(1)} async-done(((s32[32,1,128]{2,1,0:T(1,128)}), s32[32,1,128]{2,1,0:T(1,128)S(1)}, u32[]{:S(2)}, u32[]{:S(2)}) %all-to-all-start) | async-done | bytes 16416 | tf_op jit(solution)/shard_map/all_to_all | solution.py:387
  17.6 2.1 plan.1
  19.7 3.3 %collect.7 = (bf16[7,2,128,128]{3,2,1,0:T(8,128)(2,1)}, bf16[7,2,128,128]{3,2,1,0:T(8,128)(2,1)}, bf16[7,2,128,128]{3,2,1,0:T(8,128)(2,1)}, bf16[7,2,128,128]{3,...) custom-call(s32[2]{0:T(128)} %pad_add_fusion.4.home, ...), custom_call_target="tpu_custom_call" | custom-call | tf_op jit(solution)/shard_map/collect/pallas_call | solution.py:144
  23.4 1.7 collective-permute-start.34
  25.7 4.0 %collect.4 = (bf16[7,128,128]{2,1,0:T(8,128)(2,1)}, bf16[7,128,128]{2,1,0:T(8,128)(2,1)}, bf16[7,128,128]{2,1,0:T(8,128)(2,1)}, bf16[7,128,128]{2,1,0:T(8,128)(2...) custom-call(s32[2]{0:T(128)} %pad_add_fusion.home, ...), custom_call_target="tpu_custom_call" | custom-call | tf_op jit(solution)/shard_map/collect/pallas_call | solution.py:144
  29.7 1.4 collective-permute-start.1
  31.9 17.5 %collective-permute-done.rest_0_ = bf16[7,128,128]{2,1,0:T(8,128)(2,1)S(1)} collective-permute-done((bf16[7,128,128]{2,1,0:T(8,128)(2,1)}, bf16[7,128,128]{2,1,0:T(8,128)(2,1)S(1)}, u32[]{:S(2)}, u32[]{:S(2)}) %collective-permute-start) | collective-permute-done | bytes 229408 | tf_op jit(solution)/shard_map/ppermute | solution.py:19
  50.8 10.8 %collective-permute-done.2.rest_2_ = bf16[7,128,128]{2,1,0:T(8,128)(2,1)S(1)} collective-permute-done((bf16[7,128,128]{2,1,0:T(8,128)(2,1)}, bf16[7,128,128]{2,1,0:T(8,128)(2,1)S(1)}, u32[]{:S(2)}, u32[]{:S(2)}) %collective-permute-start.2) | collective-permute-done | bytes 229408 | tf_op jit(solution)/shard_map/ppermute | solution.py:19
  62.3 1.8 collective-permute-start.39
  64.7 3.8 %collect.6 = (bf16[7,2,128,128]{3,2,1,0:T(8,128)(2,1)}, bf16[7,2,128,128]{3,2,1,0:T(8,128)(2,1)}, bf16[7,2,128,128]{3,2,1,0:T(8,128)(2,1)}, bf16[7,2,128,128]{3,...) custom-call(s32[2]{0:T(128)} %pad_add_fusion.3.home, ...), custom_call_target="tpu_custom_call" | custom-call | tf_op jit(solution)/shard_map/collect/pallas_call | solution.py:144
  68.5 2.9 collective-permute-done.35.rest_2_
  71.4 3.3 %collective-permute-done.37.rest_4_ = bf16[7,2,128,128]{3,2,1,0:T(8,128)(2,1)S(1)} collective-permute-done((bf16[7,2,128,128]{3,2,1,0:T(8,128)(2,1)}, bf16[7,2,128,128]{3,2,1,0:T(8,128)(2,1)S(1)}, u32[]{:S(2)}, u32[]{:S(2)}) %collective-permute-start.37) | collective-permute-done | bytes 458784 | tf_op jit(solution)/shard_map/ppermute | solution.py:19
  74.7 16.5 %collective-permute-start.26 = (bf16[7,2,128,128]{3,2,1,0:T(8,128)(2,1)}, bf16[7,2,128,128]{3,2,1,0:T(8,128)(2,1)}, u32[]{:S(2)}, u32[]{:S(2)}) collective-permute-start(bf16[7,2,128,128]{3,2,1,0:T(8,128)(2,1)} %get-tuple-element.78), channel_id=1, source_target_pairs={{5,0},{6,1},{7,2},{0,3},{1,4},{2,5},{3,6},{4,7},{13,8},{14,9},{15,... | collective-permute-start | bytes 1376264 | tf_op jit(solution)/shard_map/ppermute | solution.py:19
  92.7 1.8 collective-permute-done.24.rest_0_
  96.4 8.0 %collective-permute-start.30 = (bf16[7,2,128,128]{3,2,1,0:T(8,128)(2,1)}, bf16[7,2,128,128]{3,2,1,0:T(8,128)(2,1)}, u32[]{:S(2)}, u32[]{:S(2)}) collective-permute-start(bf16[7,2,128,128]{3,2,1,0:T(8,128)(2,1)} %get-tuple-element.82), channel_id=1, source_target_pairs={{1,0},{2,1},{3,2},{4,3},{5,4},{6,5},{7,6},{0,7},{9,8},{10,9},{11,1... | collective-permute-start | bytes 1376264 | tf_op jit(solution)/shard_map/ppermute | solution.py:19
  105.0 3.4 %collect.5 = (bf16[7,2,128,128]{3,2,1,0:T(8,128)(2,1)}, bf16[7,2,128,128]{3,2,1,0:T(8,128)(2,1)}, bf16[7,2,128,128]{3,2,1,0:T(8,128)(2,1)}, bf16[7,2,128,128]{3,...) custom-call(s32[2]{0:T(128)} %pad_add_fusion.2.home, ...), custom_call_target="tpu_custom_call" | custom-call | tf_op jit(solution)/shard_map/collect/pallas_call | solution.py:144
  108.4 6.3 %collective-permute-done.26.rest_2_ = bf16[7,2,128,128]{3,2,1,0:T(8,128)(2,1)} collective-permute-done((bf16[7,2,128,128]{3,2,1,0:T(8,128)(2,1)}, bf16[7,2,128,128]{3,2,1,0:T(8,128)(2,1)}, u32[]{:S(2)}, u32[]{:S(2)}) %collective-permute-start.26) | collective-permute-done | bytes 458784 | tf_op jit(solution)/shard_map/ppermute | solution.py:19
  114.9 10.9 %collective-permute-start.16 = (bf16[7,2,128,128]{3,2,1,0:T(8,128)(2,1)}, bf16[7,2,128,128]{3,2,1,0:T(8,128)(2,1)S(1)}, u32[]{:S(2)}, u32[]{:S(2)}) collective-permute-start(bf16[7,2,128,128]{3,2,1,0:T(8,128)(2,1)} %get-tuple-element.69), channel_id=1, source_target_pairs={{6,0},{7,1},{0,2},{1,3},{2,4},{3,5},{4,6},{5,7},{14,8},{15,9},{8,1... | collective-permute-start | bytes 1376264 | tf_op jit(solution)/shard_map/ppermute | solution.py:19
  125.7 6.6 %collective-permute-start.17 = (bf16[7,2,128,128]{3,2,1,0:T(8,128)(2,1)}, bf16[7,2,128,128]{3,2,1,0:T(8,128)(2,1)S(1)}, u32[]{:S(2)}, u32[]{:S(2)}) collective-permute-start(bf16[7,2,128,128]{3,2,1,0:T(8,128)(2,1)} %get-tuple-element.70), channel_id=1, source_target_pairs={{5,0},{6,1},{7,2},{0,3},{1,4},{2,5},{3,6},{4,7},{13,8},{14,9},{15,... | collective-permute-start | bytes 1376264 | tf_op jit(solution)/shard_map/ppermute | solution.py:19
  132.4 1.4 collective-permute-start.18
  133.8 2.2 collective-permute-start.14
  136.0 1.3 collective-permute-done.16.rest_1_
  138.2 15.7 %collective-permute-done.17.rest_2_ = bf16[7,2,128,128]{3,2,1,0:T(8,128)(2,1)S(1)} collective-permute-done((bf16[7,2,128,128]{3,2,1,0:T(8,128)(2,1)}, bf16[7,2,128,128]{3,2,1,0:T(8,128)(2,1)S(1)}, u32[]{:S(2)}, u32[]{:S(2)}) %collective-permute-start.17) | collective-permute-done | bytes 458784 | tf_op jit(solution)/shard_map/ppermute | solution.py:19
  154.5 8.4 %collective-permute-done.19.rest_4_ = bf16[7,2,128,128]{3,2,1,0:T(8,128)(2,1)S(1)} collective-permute-done((bf16[7,2,128,128]{3,2,1,0:T(8,128)(2,1)}, bf16[7,2,128,128]{3,2,1,0:T(8,128)(2,1)S(1)}, u32[]{:S(2)}, u32[]{:S(2)}) %collective-permute-start.19) | collective-permute-done | bytes 458784 | tf_op jit(solution)/shard_map/ppermute | solution.py:19
  162.9 3.2 collective-permute-start.21
  166.7 7.8 %collective-permute-done.21.rest_6_ = bf16[7,2,128,128]{3,2,1,0:T(8,128)(2,1)S(1)} collective-permute-done((bf16[7,2,128,128]{3,2,1,0:T(8,128)(2,1)}, bf16[7,2,128,128]{3,2,1,0:T(8,128)(2,1)S(1)}, u32[]{:S(2)}, u32[]{:S(2)}) %collective-permute-start.21) | collective-permute-done | bytes 458784 | tf_op jit(solution)/shard_map/ppermute | solution.py:19
  174.5 3.2 collective-permute-start.4
  177.7 1.2 collective-permute-start.5
  178.9 9.4 %collective-permute-done.32.q = bf16[384,1024]{1,0:T(8,128)(2,1)S(1)} collective-permute-done((bf16[384,1024]{1,0:T(8,128)(2,1)S(1)}, bf16[384,1024]{1,0:T(8,128)(2,1)S(1)}, u32[]{:S(2)}, u32[]{:S(2)}) %collective-permute-start.32) | collective-permute-done | bytes 786464 | tf_op jit(solution)/shard_map/ppermute | solution.py:19
  188.3 2.7 collective-permute-start.6
  192.1 10.2 %shard_map.58 = (bf16[384,1024]{1,0:T(8,128)(2,1)S(1)}, f32[3,8,128]{2,1,0:T(8,128)S(1)}) custom-call(s32[2]{0:T(128)S(1)} %copy-done.15, s32[4,128]{1,0:T(4,128)S(1)} %copy-done.13, s32[32,128]{1,0:T(8,128)S(1)} %copy-done.1, bf16[384,1024]{1,0:T(8,128)(2,1)S(1)} %collective-permute-done.32.q, bf16[128,128,128]{2,1,0:T(8,128)(2,1)} %keys.15, ...), custom_call_target="tpu_custom_call" | custom-call | tf_op jit(solution)/shard_map/pallas_call | solution.py:319
  202.3 9.5 %shard_map.57 = (bf16[384,1024]{1,0:T(8,128)(2,1)S(1)}, f32[3,8,128]{2,1,0:T(8,128)S(1)}) custom-call(s32[2]{0:T(128)S(1)} %copy-done.16, s32[4,128]{1,0:T(4,128)S(1)} %copy-done.13, s32[32,128]{1,0:T(8,128)S(1)} %copy-done.1, bf16[384,1024]{1,0:T(8,128)(2,1)S(1)} %collective-permute-done.23.q, bf16[128,128,128]{2,1,0:T(8,128)(2,1)} %keys.15, ...), custom_call_target="tpu_custom_call" | custom-call | tf_op jit(solution)/shard_map/pallas_call | solution.py:319
  212.0 10.0 %shard_map.56 = (bf16[384,1024]{1,0:T(8,128)(2,1)S(1)}, f32[3,8,128]{2,1,0:T(8,128)S(1)}) custom-call(s32[2]{0:T(128)S(1)} %copy-done.17, s32[4,128]{1,0:T(4,128)S(1)} %copy-done.13, s32[32,128]{1,0:T(8,128)S(1)} %copy-done.1, bf16[384,1024]{1,0:T(8,128)(2,1)S(1)} %collective-permute-done.14.q, bf16[128,128,128]{2,1,0:T(8,128)(2,1)} %keys.15, ...), custom_call_target="tpu_custom_call" | custom-call | tf_op jit(solution)/shard_map/pallas_call | solution.py:319
  222.0 16.2 %collective-permute-start.40 = (bf16[384,1024]{1,0:T(8,128)(2,1)S(1)}, bf16[384,1024]{1,0:T(8,128)(2,1)S(1)}, u32[]{:S(2)}, u32[]{:S(2)}) collective-permute-start(bf16[384,1024]{1,0:T(8,128)(2,1)S(1)} %get-tuple-element.91), channel_id=1, source_target_pairs={{24,0},{0,8},{8,16},{16,24},{25,1},{1,9},{9,17},{17,25},{26,2},{2,... | collective-permute-start | bytes 2359304 | tf_op jit(solution)/shard_map/ppermute | solution.py:19
  238.2 1.5 collective-permute-start.22
  240.8 6.4 %collective-permute-done.8.rest_1_ = bf16[7,128,128]{2,1,0:T(8,128)(2,1)S(1)} collective-permute-done((bf16[7,128,128]{2,1,0:T(8,128)(2,1)S(1)}, bf16[7,128,128]{2,1,0:T(8,128)(2,1)S(1)}, u32[]{:S(2)}, u32[]{:S(2)}) %collective-permute-start.8) | collective-permute-done | bytes 229408 | tf_op jit(solution)/shard_map/ppermute | solution.py:19
  247.2 1.3 collective-permute-start.10
  248.5 4.7 %collective-permute-done.9.rest_2_ = bf16[7,128,128]{2,1,0:T(8,128)(2,1)S(1)} collective-permute-done((bf16[7,128,128]{2,1,0:T(8,128)(2,1)S(1)}, bf16[7,128,128]{2,1,0:T(8,128)(2,1)S(1)}, u32[]{:S(2)}, u32[]{:S(2)}) %collective-permute-start.9) | collective-permute-done | bytes 229408 | tf_op jit(solution)/shard_map/ppermute | solution.py:19
  253.2 2.4 collective-permute-done.10.rest_3_
  255.7 3.2 collective-permute-start.12
  258.9 2.2 collective-permute-start.13
  261.0 3.4 %collective-permute-done.12.rest_5_ = bf16[7,128,128]{2,1,0:T(8,128)(2,1)S(1)} collective-permute-done((bf16[7,128,128]{2,1,0:T(8,128)(2,1)S(1)}, bf16[7,128,128]{2,1,0:T(8,128)(2,1)S(1)}, u32[]{:S(2)}, u32[]{:S(2)}) %collective-permute-start.12) | collective-permute-done | bytes 229408 | tf_op jit(solution)/shard_map/ppermute | solution.py:19
  265.6 2.6 collective-permute-start.42
  268.2 20.6 %collective-permute-done.43.rest_12_ = f32[3,8,128]{2,1,0:T(8,128)S(1)} collective-permute-done((f32[3,8,128]{2,1,0:T(8,128)S(1)}, f32[3,8,128]{2,1,0:T(8,128)S(1)}, u32[]{:S(2)}, u32[]{:S(2)}) %collective-permute-start.43) | collective-permute-done | bytes 12320 | tf_op jit(solution)/shard_map/ppermute | solution.py:19
  288.8 19.3 %collective-permute-start.41 = (f32[3,8,128]{2,1,0:T(8,128)S(1)}, f32[3,8,128]{2,1,0:T(8,128)S(1)}, u32[]{:S(2)}, u32[]{:S(2)}) collective-permute-start(f32[3,8,128]{2,1,0:T(8,128)S(1)} %get-tuple-element.92), channel_id=1, source_target_pairs={{16,0},{24,8},{0,16},{8,24},{17,1},{25,9},{1,17},{9,25},{18,2},{26... | collective-permute-start | bytes 36872 | tf_op jit(solution)/shard_map/ppermute | solution.py:19
  308.1 8.7 %shard_map.55 = (bf16[3,1024,1152]{2,1,0:T(8,128)(2,1)}, f32[3,8,128]{2,1,0:T(8,128)S(1)}) custom-call(s32[2]{0:T(128)S(1)} %copy-done.14, s32[4,128]{1,0:T(4,128)S(1)} %copy-done.13, s32[32,128]{1,0:T(8,128)S(1)} %copy-done.1, bf16[384,1024]{1,0:T(8,128)(2,1)S(1)} %copy-done.2, bf16[128,128,128]{2,1,0:T(8,128)(2,1)} %keys.15, ...), custom_call_target="tpu_custom_call" | custom-call | tf_op jit(solution)/shard_map/pallas_call | solution.py:319
  316.9 8.5 %shard_map.59 = bf16[384,1024]{1,0:T(8,128)(2,1)} custom-call(s32[2]{0:T(128)S(1)} %copy-done.14, s32[4,128]{1,0:T(4,128)S(1)} %copy-done.13, s32[32,128]{1,0:T(8,128)S(1)} %copy-done.1, bf16[3,1024,1152]{2,1,0:T(8,128)(2,1)} %get-tuple-element.59.weights, f32[3,8,128]{2,1,0:T(8,128)S(1)} %get-tuple-element.60.top, bf16[128,128,128]{2,1,0:T(8,128)(2,1)} %values.15, ...), custom_call_target="tpu_custom_call" | custom-call | tf_op jit(solution)/shard_map/pallas_call | solution.py:319
  (115 shorter events, 18.3 us)
Async XLA Ops:
  2.6 14.4 %all-to-all-start = ((s32[32,1,128]{2,1,0:T(1,128)}), s32[32,1,128]{2,1,0:T(1,128)S(1)}, u32[]{:S(2)}, u32[]{:S(2)}) async-start(s32[32,1,128]{2,1,0:T(1,128)} %broadcast_in_dim.9), calls=%async_computation | async-start | bytes 32768 | tf_op jit(solution)/shard_map/all_to_all | solution.py:387
  23.1 39.2 %collective-permute-start.33 = (bf16[7,2,128,128]{3,2,1,0:T(8,128)(2,1)}, bf16[7,2,128,128]{3,2,1,0:T(8,128)(2,1)S(1)}, u32[]{:S(2)}, u32[]{:S(2)}) collective-permute-start(bf16[7,2,128,128]{3,2,1,0:T(8,128)(2,1)} %get-tuple-element.84), channel_id=1, source_target_pairs={{7,0},{0,1},{1,2},{2,3},{3,4},{4,5},{5,6},{6,7},{15,8},{8,9},{9,10... | collective-permute-start | bytes 1376264 | tf_op jit(solution)/shard_map/ppermute | solution.py:19
  23.4 38.9 %collective-permute-start.34 = (bf16[7,2,128,128]{3,2,1,0:T(8,128)(2,1)}, bf16[7,2,128,128]{3,2,1,0:T(8,128)(2,1)S(1)}, u32[]{:S(2)}, u32[]{:S(2)}) collective-permute-start(bf16[7,2,128,128]{3,2,1,0:T(8,128)(2,1)} %get-tuple-element.85), channel_id=1, source_target_pairs={{6,0},{7,1},{0,2},{1,3},{2,4},{3,5},{4,6},{5,7},{14,8},{15,9},{8,1... | collective-permute-start | bytes 1376264 | tf_op jit(solution)/shard_map/ppermute | solution.py:19
  29.7 19.8 %collective-permute-start = (bf16[7,128,128]{2,1,0:T(8,128)(2,1)}, bf16[7,128,128]{2,1,0:T(8,128)(2,1)S(1)}, u32[]{:S(2)}, u32[]{:S(2)}) collective-permute-start(bf16[7,128,128]{2,1,0:T(8,128)(2,1)} %get-tuple-element.52), channel_id=1, source_target_pairs={{7,0},{0,1},{1,2},{2,3},{3,4},{4,5},{5,6},{6,7},{15,8},{8,9},{9,10... | collective-permute-start | bytes 688136 | tf_op jit(solution)/shard_map/ppermute | solution.py:19
  29.7 19.7 %collective-permute-start.1 = (bf16[7,128,128]{2,1,0:T(8,128)(2,1)}, bf16[7,128,128]{2,1,0:T(8,128)(2,1)S(1)}, u32[]{:S(2)}, u32[]{:S(2)}) collective-permute-start(bf16[7,128,128]{2,1,0:T(8,128)(2,1)} %get-tuple-element.53), channel_id=1, source_target_pairs={{6,0},{7,1},{0,2},{1,3},{2,4},{3,5},{4,6},{5,7},{14,8},{15,9},{8,1... | collective-permute-start | bytes 688136 | tf_op jit(solution)/shard_map/ppermute | solution.py:19
  31.1 30.4 %collective-permute-start.2 = (bf16[7,128,128]{2,1,0:T(8,128)(2,1)}, bf16[7,128,128]{2,1,0:T(8,128)(2,1)S(1)}, u32[]{:S(2)}, u32[]{:S(2)}) collective-permute-start(bf16[7,128,128]{2,1,0:T(8,128)(2,1)} %get-tuple-element.54), channel_id=1, source_target_pairs={{5,0},{6,1},{7,2},{0,3},{1,4},{2,5},{3,6},{4,7},{13,8},{14,9},{15,... | collective-permute-start | bytes 688136 | tf_op jit(solution)/shard_map/ppermute | solution.py:19
  49.5 21.9 %collective-permute-start.35 = (bf16[7,2,128,128]{3,2,1,0:T(8,128)(2,1)}, bf16[7,2,128,128]{3,2,1,0:T(8,128)(2,1)S(1)}, u32[]{:S(2)}, u32[]{:S(2)}) collective-permute-start(bf16[7,2,128,128]{3,2,1,0:T(8,128)(2,1)} %get-tuple-element.86), channel_id=1, source_target_pairs={{5,0},{6,1},{7,2},{0,3},{1,4},{2,5},{3,6},{4,7},{13,8},{14,9},{15,... | collective-permute-start | bytes 1376264 | tf_op jit(solution)/shard_map/ppermute | solution.py:19
  50.2 21.2 %collective-permute-start.36 = (bf16[7,2,128,128]{3,2,1,0:T(8,128)(2,1)}, bf16[7,2,128,128]{3,2,1,0:T(8,128)(2,1)S(1)}, u32[]{:S(2)}, u32[]{:S(2)}) collective-permute-start(bf16[7,2,128,128]{3,2,1,0:T(8,128)(2,1)} %get-tuple-element.87), channel_id=1, source_target_pairs={{4,0},{5,1},{6,2},{7,3},{0,4},{1,5},{2,6},{3,7},{12,8},{13,9},{14,... | collective-permute-start | bytes 1376264 | tf_op jit(solution)/shard_map/ppermute | solution.py:19
  62.3 12.5 %collective-permute-start.37 = (bf16[7,2,128,128]{3,2,1,0:T(8,128)(2,1)}, bf16[7,2,128,128]{3,2,1,0:T(8,128)(2,1)S(1)}, u32[]{:S(2)}, u32[]{:S(2)}) collective-permute-start(bf16[7,2,128,128]{3,2,1,0:T(8,128)(2,1)} %get-tuple-element.88), channel_id=1, source_target_pairs={{3,0},{4,1},{5,2},{6,3},{7,4},{0,5},{1,6},{2,7},{11,8},{12,9},{13,... | collective-permute-start | bytes 1376264 | tf_op jit(solution)/shard_map/ppermute | solution.py:19
  62.3 29.0 %collective-permute-start.38 = (bf16[7,2,128,128]{3,2,1,0:T(8,128)(2,1)}, bf16[7,2,128,128]{3,2,1,0:T(8,128)(2,1)S(1)}, u32[]{:S(2)}, u32[]{:S(2)}) collective-permute-start(bf16[7,2,128,128]{3,2,1,0:T(8,128)(2,1)} %get-tuple-element.89), channel_id=1, source_target_pairs={{2,0},{3,1},{4,2},{5,3},{6,4},{7,5},{0,6},{1,7},{10,8},{11,9},{12,... | collective-permute-start | bytes 1376264 | tf_op jit(solution)/shard_map/ppermute | solution.py:19
  62.3 30.4 %collective-permute-start.39 = (bf16[7,2,128,128]{3,2,1,0:T(8,128)(2,1)S(1)}, bf16[7,2,128,128]{3,2,1,0:T(8,128)(2,1)}, u32[]{:S(2)}, u32[]{:S(2)}) collective-permute-start(bf16[7,2,128,128]{3,2,1,0:T(8,128)(2,1)S(1)} %copy-done.19), channel_id=1, source_target_pairs={{1,0},{2,1},{3,2},{4,3},{5,4},{6,5},{7,6},{0,7},{9,8},{10,9},{11,1... | collective-permute-start | bytes 1376264 | tf_op jit(solution)/shard_map/ppermute | solution.py:19
  71.4 23.1 %collective-permute-start.24 = (bf16[7,2,128,128]{3,2,1,0:T(8,128)(2,1)}, bf16[7,2,128,128]{3,2,1,0:T(8,128)(2,1)S(1)}, u32[]{:S(2)}, u32[]{:S(2)}) collective-permute-start(bf16[7,2,128,128]{3,2,1,0:T(8,128)(2,1)} %get-tuple-element.76), channel_id=1, source_target_pairs={{7,0},{0,1},{1,2},{2,3},{3,4},{4,5},{5,6},{6,7},{15,8},{8,9},{9,10... | collective-permute-start | bytes 1376264 | tf_op jit(solution)/shard_map/ppermute | solution.py:19
  71.4 24.3 %collective-permute-start.25 = (bf16[7,2,128,128]{3,2,1,0:T(8,128)(2,1)}, bf16[7,2,128,128]{3,2,1,0:T(8,128)(2,1)S(1)}, u32[]{:S(2)}, u32[]{:S(2)}) collective-permute-start(bf16[7,2,128,128]{3,2,1,0:T(8,128)(2,1)} %get-tuple-element.77), channel_id=1, source_target_pairs={{6,0},{7,1},{0,2},{1,3},{2,4},{3,5},{4,6},{5,7},{14,8},{15,9},{8,1... | collective-permute-start | bytes 1376264 | tf_op jit(solution)/shard_map/ppermute | solution.py:19
  74.7 39.9 %collective-permute-start.26 = (bf16[7,2,128,128]{3,2,1,0:T(8,128)(2,1)}, bf16[7,2,128,128]{3,2,1,0:T(8,128)(2,1)}, u32[]{:S(2)}, u32[]{:S(2)}) collective-permute-start(bf16[7,2,128,128]{3,2,1,0:T(8,128)(2,1)} %get-tuple-element.78), channel_id=1, source_target_pairs={{5,0},{6,1},{7,2},{0,3},{1,4},{2,5},{3,6},{4,7},{13,8},{14,9},{15,... | collective-permute-start | bytes 1376264 | tf_op jit(solution)/shard_map/ppermute | solution.py:19
  92.0 22.8 %collective-permute-start.27 = (bf16[7,2,128,128]{3,2,1,0:T(8,128)(2,1)}, bf16[7,2,128,128]{3,2,1,0:T(8,128)(2,1)}, u32[]{:S(2)}, u32[]{:S(2)}) collective-permute-start(bf16[7,2,128,128]{3,2,1,0:T(8,128)(2,1)} %get-tuple-element.79), channel_id=1, source_target_pairs={{4,0},{5,1},{6,2},{7,3},{0,4},{1,5},{2,6},{3,7},{12,8},{13,9},{14,... | collective-permute-start | bytes 1376264 | tf_op jit(solution)/shard_map/ppermute | solution.py:19
  92.7 33.1 %collective-permute-start.28 = (bf16[7,2,128,128]{3,2,1,0:T(8,128)(2,1)}, bf16[7,2,128,128]{3,2,1,0:T(8,128)(2,1)}, u32[]{:S(2)}, u32[]{:S(2)}) collective-permute-start(bf16[7,2,128,128]{3,2,1,0:T(8,128)(2,1)} %get-tuple-element.80), channel_id=1, source_target_pairs={{3,0},{4,1},{5,2},{6,3},{7,4},{0,5},{1,6},{2,7},{11,8},{12,9},{13,... | collective-permute-start | bytes 1376264 | tf_op jit(solution)/shard_map/ppermute | solution.py:19
  95.3 37.1 %collective-permute-start.29 = (bf16[7,2,128,128]{3,2,1,0:T(8,128)(2,1)}, bf16[7,2,128,128]{3,2,1,0:T(8,128)(2,1)}, u32[]{:S(2)}, u32[]{:S(2)}) collective-permute-start(bf16[7,2,128,128]{3,2,1,0:T(8,128)(2,1)} %get-tuple-element.81), channel_id=1, source_target_pairs={{2,0},{3,1},{4,2},{5,3},{6,4},{7,5},{0,6},{1,7},{10,8},{11,9},{12,... | collective-permute-start | bytes 1376264 | tf_op jit(solution)/shard_map/ppermute | solution.py:19
  96.4 37.3 %collective-permute-start.30 = (bf16[7,2,128,128]{3,2,1,0:T(8,128)(2,1)}, bf16[7,2,128,128]{3,2,1,0:T(8,128)(2,1)}, u32[]{:S(2)}, u32[]{:S(2)}) collective-permute-start(bf16[7,2,128,128]{3,2,1,0:T(8,128)(2,1)} %get-tuple-element.82), channel_id=1, source_target_pairs={{1,0},{2,1},{3,2},{4,3},{5,4},{6,5},{7,6},{0,7},{9,8},{10,9},{11,1... | collective-permute-start | bytes 1376264 | tf_op jit(solution)/shard_map/ppermute | solution.py:19
  114.7 19.1 %collective-permute-start.15 = (bf16[7,2,128,128]{3,2,1,0:T(8,128)(2,1)}, bf16[7,2,128,128]{3,2,1,0:T(8,128)(2,1)S(1)}, u32[]{:S(2)}, u32[]{:S(2)}) collective-permute-start(bf16[7,2,128,128]{3,2,1,0:T(8,128)(2,1)} %get-tuple-element.68), channel_id=1, source_target_pairs={{7,0},{0,1},{1,2},{2,3},{3,4},{4,5},{5,6},{6,7},{15,8},{8,9},{9,10... | collective-permute-start | bytes 1376264 | tf_op jit(solution)/shard_map/ppermute | solution.py:19
  114.9 22.5 %collective-permute-start.16 = (bf16[7,2,128,128]{3,2,1,0:T(8,128)(2,1)}, bf16[7,2,128,128]{3,2,1,0:T(8,128)(2,1)S(1)}, u32[]{:S(2)}, u32[]{:S(2)}) collective-permute-start(bf16[7,2,128,128]{3,2,1,0:T(8,128)(2,1)} %get-tuple-element.69), channel_id=1, source_target_pairs={{6,0},{7,1},{0,2},{1,3},{2,4},{3,5},{4,6},{5,7},{14,8},{15,9},{8,1... | collective-permute-start | bytes 1376264 | tf_op jit(solution)/shard_map/ppermute | solution.py:19
  125.7 28.2 %collective-permute-start.17 = (bf16[7,2,128,128]{3,2,1,0:T(8,128)(2,1)}, bf16[7,2,128,128]{3,2,1,0:T(8,128)(2,1)S(1)}, u32[]{:S(2)}, u32[]{:S(2)}) collective-permute-start(bf16[7,2,128,128]{3,2,1,0:T(8,128)(2,1)} %get-tuple-element.70), channel_id=1, source_target_pairs={{5,0},{6,1},{7,2},{0,3},{1,4},{2,5},{3,6},{4,7},{13,8},{14,9},{15,... | collective-permute-start | bytes 1376264 | tf_op jit(solution)/shard_map/ppermute | solution.py:19
  132.4 22.1 %collective-permute-start.18 = (bf16[7,2,128,128]{3,2,1,0:T(8,128)(2,1)}, bf16[7,2,128,128]{3,2,1,0:T(8,128)(2,1)S(1)}, u32[]{:S(2)}, u32[]{:S(2)}) collective-permute-start(bf16[7,2,128,128]{3,2,1,0:T(8,128)(2,1)} %get-tuple-element.71), channel_id=1, source_target_pairs={{4,0},{5,1},{6,2},{7,3},{0,4},{1,5},{2,6},{3,7},{12,8},{13,9},{14,... | collective-permute-start | bytes 1376264 | tf_op jit(solution)/shard_map/ppermute | solution.py:19
  133.8 29.1 %collective-permute-start.19 = (bf16[7,2,128,128]{3,2,1,0:T(8,128)(2,1)}, bf16[7,2,128,128]{3,2,1,0:T(8,128)(2,1)S(1)}, u32[]{:S(2)}, u32[]{:S(2)}) collective-permute-start(bf16[7,2,128,128]{3,2,1,0:T(8,128)(2,1)} %get-tuple-element.72), channel_id=1, source_target_pairs={{3,0},{4,1},{5,2},{6,3},{7,4},{0,5},{1,6},{2,7},{11,8},{12,9},{13,... | collective-permute-start | bytes 1376264 | tf_op jit(solution)/shard_map/ppermute | solution.py:19
  133.8 43.8 %collective-permute-start.14 = (bf16[384,1024]{1,0:T(8,128)(2,1)S(1)}, bf16[384,1024]{1,0:T(8,128)(2,1)S(1)}, u32[]{:S(2)}, u32[]{:S(2)}) collective-permute-start(bf16[384,1024]{1,0:T(8,128)(2,1)S(1)} %copy-done.2), channel_id=1, source_target_pairs={{16,0},{24,8},{0,16},{8,24},{17,1},{25,9},{1,17},{9,25},{18,2},{26... | collective-permute-start | bytes 2359304 | tf_op jit(solution)/shard_map/ppermute | solution.py:19
  137.3 51.0 %collective-permute-start.32 = (bf16[384,1024]{1,0:T(8,128)(2,1)S(1)}, bf16[384,1024]{1,0:T(8,128)(2,1)S(1)}, u32[]{:S(2)}, u32[]{:S(2)}) collective-permute-start(bf16[384,1024]{1,0:T(8,128)(2,1)S(1)} %copy-done.2), channel_id=1, source_target_pairs={{8,0},{16,8},{24,16},{0,24},{9,1},{17,9},{25,17},{1,25},{10,2},{18... | collective-permute-start | bytes 2359304 | tf_op jit(solution)/shard_map/ppermute | solution.py:19
  153.9 37.1 %collective-permute-start.23 = (bf16[384,1024]{1,0:T(8,128)(2,1)S(1)}, bf16[384,1024]{1,0:T(8,128)(2,1)S(1)}, u32[]{:S(2)}, u32[]{:S(2)}) collective-permute-start(bf16[384,1024]{1,0:T(8,128)(2,1)S(1)} %copy-done.2), channel_id=1, source_target_pairs={{24,0},{0,8},{8,16},{16,24},{25,1},{1,9},{9,17},{17,25},{26,2},{2,... | collective-permute-start | bytes 2359304 | tf_op jit(solution)/shard_map/ppermute | solution.py:19
  154.5 11.6 %collective-permute-start.20 = (bf16[7,2,128,128]{3,2,1,0:T(8,128)(2,1)}, bf16[7,2,128,128]{3,2,1,0:T(8,128)(2,1)S(1)}, u32[]{:S(2)}, u32[]{:S(2)}) collective-permute-start(bf16[7,2,128,128]{3,2,1,0:T(8,128)(2,1)} %get-tuple-element.73), channel_id=1, source_target_pairs={{2,0},{3,1},{4,2},{5,3},{6,4},{7,5},{0,6},{1,7},{10,8},{11,9},{12,... | collective-permute-start | bytes 1376264 | tf_op jit(solution)/shard_map/ppermute | solution.py:19
  162.9 11.6 %collective-permute-start.21 = (bf16[7,2,128,128]{3,2,1,0:T(8,128)(2,1)}, bf16[7,2,128,128]{3,2,1,0:T(8,128)(2,1)S(1)}, u32[]{:S(2)}, u32[]{:S(2)}) collective-permute-start(bf16[7,2,128,128]{3,2,1,0:T(8,128)(2,1)} %get-tuple-element.74), channel_id=1, source_target_pairs={{1,0},{2,1},{3,2},{4,3},{5,4},{6,5},{7,6},{0,7},{9,8},{10,9},{11,1... | collective-permute-start | bytes 1376264 | tf_op jit(solution)/shard_map/ppermute | solution.py:19
  166.1 55.9 %collective-permute-start.3 = (bf16[7,128,128]{2,1,0:T(8,128)(2,1)}, bf16[7,128,128]{2,1,0:T(8,128)(2,1)S(1)}, u32[]{:S(2)}, u32[]{:S(2)}) collective-permute-start(bf16[7,128,128]{2,1,0:T(8,128)(2,1)} %get-tuple-element.55), channel_id=1, source_target_pairs={{4,0},{5,1},{6,2},{7,3},{0,4},{1,5},{2,6},{3,7},{12,8},{13,9},{14,... | collective-permute-start | bytes 688136 | tf_op jit(solution)/shard_map/ppermute | solution.py:19
  174.5 63.7 %collective-permute-start.4 = (bf16[7,128,128]{2,1,0:T(8,128)(2,1)}, bf16[7,128,128]{2,1,0:T(8,128)(2,1)S(1)}, u32[]{:S(2)}, u32[]{:S(2)}) collective-permute-start(bf16[7,128,128]{2,1,0:T(8,128)(2,1)} %get-tuple-element.56), channel_id=1, source_target_pairs={{3,0},{4,1},{5,2},{6,3},{7,4},{0,5},{1,6},{2,7},{11,8},{12,9},{13,... | collective-permute-start | bytes 688136 | tf_op jit(solution)/shard_map/ppermute | solution.py:19
  177.7 60.6 %collective-permute-start.5 = (bf16[7,128,128]{2,1,0:T(8,128)(2,1)}, bf16[7,128,128]{2,1,0:T(8,128)(2,1)S(1)}, u32[]{:S(2)}, u32[]{:S(2)}) collective-permute-start(bf16[7,128,128]{2,1,0:T(8,128)(2,1)} %get-tuple-element.57), channel_id=1, source_target_pairs={{2,0},{3,1},{4,2},{5,3},{6,4},{7,5},{0,6},{1,7},{10,8},{11,9},{12,... | collective-permute-start | bytes 688136 | tf_op jit(solution)/shard_map/ppermute | solution.py:19
  188.3 51.5 %collective-permute-start.6 = (bf16[7,128,128]{2,1,0:T(8,128)(2,1)}, bf16[7,128,128]{2,1,0:T(8,128)(2,1)S(1)}, u32[]{:S(2)}, u32[]{:S(2)}) collective-permute-start(bf16[7,128,128]{2,1,0:T(8,128)(2,1)} %get-tuple-element.58), channel_id=1, source_target_pairs={{1,0},{2,1},{3,2},{4,3},{5,4},{6,5},{7,6},{0,7},{9,8},{10,9},{11,1... | collective-permute-start | bytes 688136 | tf_op jit(solution)/shard_map/ppermute | solution.py:19
  191.0 48.8 %collective-permute-start.7 = (bf16[7,128,128]{2,1,0:T(8,128)(2,1)}, bf16[7,128,128]{2,1,0:T(8,128)(2,1)S(1)}, u32[]{:S(2)}, u32[]{:S(2)}) collective-permute-start(bf16[7,128,128]{2,1,0:T(8,128)(2,1)} %get-tuple-element.61), channel_id=1, source_target_pairs={{7,0},{0,1},{1,2},{2,3},{3,4},{4,5},{5,6},{6,7},{15,8},{8,9},{9,10... | collective-permute-start | bytes 688136 | tf_op jit(solution)/shard_map/ppermute | solution.py:19
  211.9 96.2 %copy-start.10 = (bf16[7,128,128]{2,1,0:T(8,128)(2,1)S(1)}, bf16[7,128,128]{2,1,0:T(8,128)(2,1)}, u32[]{:S(2)}) copy-start(bf16[7,128,128]{2,1,0:T(8,128)(2,1)} %copy-done.9) | copy-start | bytes 688132
  211.9 96.2 %copy-start.12 = (bf16[7,128,128]{2,1,0:T(8,128)(2,1)S(1)}, bf16[7,128,128]{2,1,0:T(8,128)(2,1)}, u32[]{:S(2)}) copy-start(bf16[7,128,128]{2,1,0:T(8,128)(2,1)} %copy-done.11) | copy-start | bytes 688132
  211.9 96.2 %copy-start.14 = (s32[2]{0:T(128)S(1)}, s32[2]{0:T(128)}, u32[]{:S(2)}) copy-start(s32[2]{0:T(128)} %pad_add_fusion.home) | copy-start | bytes 28
  222.0 94.9 %collective-permute-start.40 = (bf16[384,1024]{1,0:T(8,128)(2,1)S(1)}, bf16[384,1024]{1,0:T(8,128)(2,1)S(1)}, u32[]{:S(2)}, u32[]{:S(2)}) collective-permute-start(bf16[384,1024]{1,0:T(8,128)(2,1)S(1)} %get-tuple-element.91), channel_id=1, source_target_pairs={{24,0},{0,8},{8,16},{16,24},{25,1},{1,9},{9,17},{17,25},{26,2},{2,... | collective-permute-start | bytes 2359304 | tf_op jit(solution)/shard_map/ppermute | solution.py:19
  238.2 78.7 %collective-permute-start.31 = (bf16[384,1024]{1,0:T(8,128)(2,1)S(1)}, bf16[384,1024]{1,0:T(8,128)(2,1)S(1)}, u32[]{:S(2)}, u32[]{:S(2)}) collective-permute-start(bf16[384,1024]{1,0:T(8,128)(2,1)S(1)} %get-tuple-element.83), channel_id=1, source_target_pairs={{8,0},{16,8},{24,16},{0,24},{9,1},{17,9},{25,17},{1,25},{10,2},{18... | collective-permute-start | bytes 2359304 | tf_op jit(solution)/shard_map/ppermute | solution.py:19
  238.2 78.7 %collective-permute-start.22 = (bf16[384,1024]{1,0:T(8,128)(2,1)S(1)}, bf16[384,1024]{1,0:T(8,128)(2,1)S(1)}, u32[]{:S(2)}, u32[]{:S(2)}) collective-permute-start(bf16[384,1024]{1,0:T(8,128)(2,1)S(1)} %get-tuple-element.75), channel_id=1, source_target_pairs={{16,0},{24,8},{0,16},{8,24},{17,1},{25,9},{1,17},{9,25},{18,2},{26... | collective-permute-start | bytes 2359304 | tf_op jit(solution)/shard_map/ppermute | solution.py:19
  239.7 7.4 %collective-permute-start.8 = (bf16[7,128,128]{2,1,0:T(8,128)(2,1)S(1)}, bf16[7,128,128]{2,1,0:T(8,128)(2,1)S(1)}, u32[]{:S(2)}, u32[]{:S(2)}) collective-permute-start(bf16[7,128,128]{2,1,0:T(8,128)(2,1)S(1)} %copy-done.25), channel_id=1, source_target_pairs={{6,0},{7,1},{0,2},{1,3},{2,4},{3,5},{4,6},{5,7},{14,8},{15,9},{8,1... | collective-permute-start | bytes 688136 | tf_op jit(solution)/shard_map/ppermute | solution.py:19
  239.8 13.5 %collective-permute-start.9 = (bf16[7,128,128]{2,1,0:T(8,128)(2,1)S(1)}, bf16[7,128,128]{2,1,0:T(8,128)(2,1)S(1)}, u32[]{:S(2)}, u32[]{:S(2)}) collective-permute-start(bf16[7,128,128]{2,1,0:T(8,128)(2,1)S(1)} %copy-done.24), channel_id=1, source_target_pairs={{5,0},{6,1},{7,2},{0,3},{1,4},{2,5},{3,6},{4,7},{13,8},{14,9},{15,... | collective-permute-start | bytes 688136 | tf_op jit(solution)/shard_map/ppermute | solution.py:19
  247.2 8.5 %collective-permute-start.10 = (bf16[7,128,128]{2,1,0:T(8,128)(2,1)S(1)}, bf16[7,128,128]{2,1,0:T(8,128)(2,1)S(1)}, u32[]{:S(2)}, u32[]{:S(2)}) collective-permute-start(bf16[7,128,128]{2,1,0:T(8,128)(2,1)S(1)} %copy-done.23), channel_id=1, source_target_pairs={{4,0},{5,1},{6,2},{7,3},{0,4},{1,5},{2,6},{3,7},{12,8},{13,9},{14,... | collective-permute-start | bytes 688136 | tf_op jit(solution)/shard_map/ppermute | solution.py:19
  253.2 5.6 %collective-permute-start.11 = (bf16[7,128,128]{2,1,0:T(8,128)(2,1)S(1)}, bf16[7,128,128]{2,1,0:T(8,128)(2,1)S(1)}, u32[]{:S(2)}, u32[]{:S(2)}) collective-permute-start(bf16[7,128,128]{2,1,0:T(8,128)(2,1)S(1)} %copy-done.22), channel_id=1, source_target_pairs={{3,0},{4,1},{5,2},{6,3},{7,4},{0,5},{1,6},{2,7},{11,8},{12,9},{13,... | collective-permute-start | bytes 688136 | tf_op jit(solution)/shard_map/ppermute | solution.py:19
  255.7 8.7 %collective-permute-start.12 = (bf16[7,128,128]{2,1,0:T(8,128)(2,1)S(1)}, bf16[7,128,128]{2,1,0:T(8,128)(2,1)S(1)}, u32[]{:S(2)}, u32[]{:S(2)}) collective-permute-start(bf16[7,128,128]{2,1,0:T(8,128)(2,1)S(1)} %copy-done.21), channel_id=1, source_target_pairs={{2,0},{3,1},{4,2},{5,3},{6,4},{7,5},{0,6},{1,7},{10,8},{11,9},{12,... | collective-permute-start | bytes 688136 | tf_op jit(solution)/shard_map/ppermute | solution.py:19
  258.9 6.7 %collective-permute-start.13 = (bf16[7,128,128]{2,1,0:T(8,128)(2,1)S(1)}, bf16[7,128,128]{2,1,0:T(8,128)(2,1)S(1)}, u32[]{:S(2)}, u32[]{:S(2)}) collective-permute-start(bf16[7,128,128]{2,1,0:T(8,128)(2,1)S(1)} %copy-done.20), channel_id=1, source_target_pairs={{1,0},{2,1},{3,2},{4,3},{5,4},{6,5},{7,6},{0,7},{9,8},{10,9},{11,1... | collective-permute-start | bytes 688136 | tf_op jit(solution)/shard_map/ppermute | solution.py:19
  264.4 24.4 %collective-permute-start.43 = (f32[3,8,128]{2,1,0:T(8,128)S(1)}, f32[3,8,128]{2,1,0:T(8,128)S(1)}, u32[]{:S(2)}, u32[]{:S(2)}) collective-permute-start(f32[3,8,128]{2,1,0:T(8,128)S(1)} %get-tuple-element.94), channel_id=1, source_target_pairs={{24,0},{0,8},{8,16},{16,24},{25,1},{1,9},{9,17},{17,25},{26,2},{2,... | collective-permute-start | bytes 36872 | tf_op jit(solution)/shard_map/ppermute | solution.py:19
  265.6 51.2 %collective-permute-start.42 = (f32[3,8,128]{2,1,0:T(8,128)S(1)}, f32[3,8,128]{2,1,0:T(8,128)S(1)}, u32[]{:S(2)}, u32[]{:S(2)}) collective-permute-start(f32[3,8,128]{2,1,0:T(8,128)S(1)} %get-tuple-element.93), channel_id=1, source_target_pairs={{8,0},{16,8},{24,16},{0,24},{9,1},{17,9},{25,17},{1,25},{10,2},{18... | collective-permute-start | bytes 36872 | tf_op jit(solution)/shard_map/ppermute | solution.py:19
  288.8 28.0 %collective-permute-start.41 = (f32[3,8,128]{2,1,0:T(8,128)S(1)}, f32[3,8,128]{2,1,0:T(8,128)S(1)}, u32[]{:S(2)}, u32[]{:S(2)}) collective-permute-start(f32[3,8,128]{2,1,0:T(8,128)S(1)} %get-tuple-element.92), channel_id=1, source_target_pairs={{16,0},{24,8},{0,16},{8,24},{17,1},{25,9},{1,17},{9,25},{18,2},{26... | collective-permute-start | bytes 36872 | tf_op jit(solution)/shard_map/ppermute | solution.py:19
  (23 other events, 593.0 us)
